TPU v7x, 32 devices: a whole 2x2x4 slice. The times are simulated.
32 devices in a mesh: dp: 16 (over z, y, x), mp: 2 (over core).
Axes of the slice: x: 2, y: 2, z: 4, core: 2. Of those that a mesh axis runs over, the one named last changes fastest.
Arguments:
- series: float32 [32, 1024], P('dp'), may hold values from -10 to 10
- observed: int32 [32, 1024], P('dp'), may hold values from 0 to 1
- routes: int32 [32, 1024, 2], P('dp'), may hold values from 0 to 7, all different within a row; in each aligned block of 2048 rows (0 to 2047, 2048 to 4095, ..., all dimensions but the last counted through in order) at most 1024 rows name the same one
- step_count: int32 [1], replicated, may hold values from 2 to 20
- joint_proj: float32 [3, 384, 384], P(None, 'dp', 'mp'), may hold values from -0.3125 to 0.3125
- joint_moment: float32 [3, 384, 384], P(None, 'dp', 'mp'), may hold values from -4.172325e-07 to 4.172325e-07
- joint_square: float32 [3, 384, 384], P(None, 'dp', 'mp'), may hold values from 3.1761813e-15 to 1.2680571e-14
- mixer_proj: float32 [384, 384], P('mp', 'dp'), may hold values from -1.25 to 1.25
- mixer_moment: float32 [384, 384], P('mp', 'dp'), may hold values from -4.172325e-07 to 4.172325e-07
- mixer_square: float32 [384, 384], P('mp', 'dp'), may hold values from 3.1761813e-15 to 1.2680571e-14
- upward_proj: float32 [9, 384, 2, 1536], P(None, 'dp', None, 'mp'), may hold values from -0.3125 to 0.3125
- upward_moment: float32 [9, 384, 2, 1536], P(None, 'dp', None, 'mp'), may hold values from -4.172325e-07 to 4.172325e-07
- upward_square: float32 [9, 384, 2, 1536], P(None, 'dp', None, 'mp'), may hold values from 3.1761813e-15 to 1.2680571e-14
- downward_proj: float32 [9, 1536, 384], P(None, 'mp', 'dp'), may hold values from -0.625 to 0.625
- downward_moment: float32 [9, 1536, 384], P(None, 'mp', 'dp'), may hold values from -4.172325e-07 to 4.172325e-07
- downward_square: float32 [9, 1536, 384], P(None, 'mp', 'dp'), may hold values from 3.1761813e-15 to 1.2680571e-14
- readout: float32 [384, 114], P('dp'), may hold values from -0.3125 to 0.3125
- readout_moment: float32 [384, 114], P('dp'), may hold values from -4.172325e-07 to 4.172325e-07
- readout_square: float32 [384, 114], P('dp'), may hold values from 3.1761813e-15 to 1.2680571e-14
- vectors: float32 [5, 384], P(None, 'dp'), may hold values from -4 to 4, as said below
- vectors_moment: float32 [5, 384], P(None, 'dp'), may hold values from -3.8146973e-06 to 3.8146973e-06
- vectors_square: float32 [5, 384], P(None, 'dp'), may hold values from 3.176181e-13 to 1.2680572e-12
Outputs:
- total_loss: float32 [], replicated
- grad_norm: float32 [], replicated
- joint_updated: float32 [3, 384, 384], P(None, 'dp', 'mp')
- joint_moment_next: float32 [3, 384, 384], P(None, 'dp', 'mp')
- joint_square_next: float32 [3, 384, 384], P(None, 'dp', 'mp')
- mixer_updated: float32 [384, 384], P('mp', 'dp')
- mixer_moment_next: float32 [384, 384], P('mp', 'dp')
- mixer_square_next: float32 [384, 384], P('mp', 'dp')
- upward_updated: float32 [9, 384, 2, 1536], P(None, 'dp', None, 'mp')
- upward_moment_next: float32 [9, 384, 2, 1536], P(None, 'dp', None, 'mp')
- upward_square_next: float32 [9, 384, 2, 1536], P(None, 'dp', None, 'mp')
- downward_updated: float32 [9, 1536, 384], P(None, 'mp', 'dp')
- downward_moment_next: float32 [9, 1536, 384], P(None, 'mp', 'dp')
- downward_square_next: float32 [9, 1536, 384], P(None, 'mp', 'dp')
- readout_updated: float32 [384, 114], P('dp')
- readout_moment_next: float32 [384, 114], P('dp')
- readout_square_next: float32 [384, 114], P('dp')
- vectors_updated: float32 [5, 384], P(None, 'dp')
- vectors_moment_next: float32 [5, 384], P(None, 'dp')
- vectors_square_next: float32 [5, 384], P(None, 'dp')
Inputs may be any that keep to these rules, and one draw needn't show every extreme that they name: `routes`: in the rows of one device no expert is named by more than 1024 pairs, a bound that some block reaches; a point names two different experts. `vectors`: rows 0 to 2 are positive.
All inputs are finite; a program needn't handle non-finite values.
Results may differ from a plain program's by a relative error of at most 0.00065.
The roundings to bfloat16 on the way count: a program that leaves them out, or rounds other values in their place, can miss the bound.
Values may be sent and summed in bfloat16 or wider, within the bound.
A program may use at most 320 MiB of HBM per device.

v0:
```python
import jax
import jax.numpy as jnp
from jax import lax
from jax.sharding import PartitionSpec as P

D = 384
HEAD = 32
ROUTED_EXPERTS = 8


horizons = (1, 8, 32, 64)
quadratic_cutoff = 2.0
aux_factor = 0.02
clip_limit = 0.001
beta_one = 0.9
beta_two = 0.95
adam_eps = 1e-08
decay_rate = 0.1
matrix_rate = 0.05
vector_rate = 0.25
norm_eps = 1e-06
rope_base = 10000.0


def rms_scale(tensor, gain_row):
    return (
        tensor * lax.rsqrt(jnp.mean(tensor * tensor, axis=-1, keepdims=True) + norm_eps) * gain_row
    )


def rope_tables(length, columns):
    halfway = columns // 2
    frequency = rope_base ** (-2.0 * jnp.arange(halfway, dtype=jnp.float32) / columns)
    angles = jnp.arange(length, dtype=jnp.float32)[:, None] * frequency[None, :]
    return (jnp.cos(angles), jnp.sin(angles))


def rotate(tensor, cosine_table, sine_table):
    halfway = tensor.shape[-1] // 2
    front_part = tensor[..., :halfway]
    back_part = tensor[..., halfway:]
    return jnp.concatenate(
        [
            front_part * cosine_table - back_part * sine_table,
            back_part * cosine_table + front_part * sine_table,
        ],
        axis=-1,
    )


def swiglu(tensor):
    halfway = tensor.shape[-1] // 2
    return jax.nn.silu(tensor[..., :halfway]) * tensor[..., halfway:]


def targets_of(series, observed):
    row_count, length = series.shape
    longest = max(horizons)
    padded_values = jnp.concatenate([series, jnp.zeros((row_count, longest), jnp.float32)], axis=1)
    padded_marks = jnp.concatenate(
        [observed.astype(jnp.float32), jnp.zeros((row_count, longest), jnp.float32)], axis=1
    )
    value_window = jnp.stack(
        [padded_values[:, 1 + offset : 1 + offset + length] for offset in range(longest)], axis=-1
    )
    mark_window = jnp.stack(
        [padded_marks[:, 1 + offset : 1 + offset + length] for offset in range(longest)], axis=-1
    )
    observed_future_series = jnp.concatenate(
        [value_window[..., :horizon] for horizon in horizons], axis=-1
    )
    valid_mask = jnp.concatenate([mark_window[..., :horizon] for horizon in horizons], axis=-1)
    return (
        observed_future_series.reshape(row_count * length, -1),
        valid_mask.reshape(row_count * length, -1),
    )


def head_counts(valid_mask):
    beginnings = [sum(horizons[:index]) for index in range(len(horizons))]
    return jnp.stack(
        [
            jnp.sum(valid_mask[:, beginning : beginning + horizon])
            for beginning, horizon in zip(beginnings, horizons)
        ]
    )


def head_weights(head_count):
    return jnp.concatenate(
        [
            jnp.zeros((horizon,), jnp.float32) + 0.25 / head_count[index]
            for index, horizon in enumerate(horizons)
        ]
    )


def dispatch_plan(route_rows, experts, capacity):
    flat_routes = route_rows.reshape(-1)
    entries = flat_routes.shape[0]
    onehot = (flat_routes[:, None] == jnp.arange(experts, dtype=jnp.int32)[None, :]).astype(
        jnp.int32
    )
    position = jnp.sum(jnp.cumsum(onehot, axis=0) * onehot, axis=1) - 1
    slot_index = flat_routes * capacity + position
    source = (
        jnp.full((experts * capacity,), entries, jnp.int32)
        .at[slot_index]
        .set(jnp.arange(entries, dtype=jnp.int32))
    )
    return (slot_index, source)


def adam_update(master, moment, square, gradient, factor, bias_one, bias_two, step_rate):
    clipped = gradient * factor
    new_moment = beta_one * moment + (1.0 - beta_one) * clipped
    new_square = beta_two * square + (1.0 - beta_two) * clipped * clipped
    updated = master - step_rate * (
        new_moment / bias_one / (jnp.sqrt(new_square / bias_two) + adam_eps) + decay_rate * master
    )
    return (updated, new_moment, new_square)


def split_heads(matrix, series_count, length):
    return matrix.reshape(series_count, length, matrix.shape[1] // HEAD, HEAD).transpose(0, 2, 1, 3)


def merge_heads(tensor):
    series_count, heads_here, length, head_size = tensor.shape
    return tensor.transpose(0, 2, 1, 3).reshape(series_count * length, heads_here * head_size)


def block_scores(query_block, key_heads, offset, length):
    block_rows = query_block.shape[1]
    scores = jnp.einsum(
        "hqe,hke->hqk", query_block, key_heads, preferred_element_type=jnp.float32
    ) * HEAD ** (-0.5)
    allowed = (offset + jnp.arange(block_rows))[:, None] >= jnp.arange(length)[None, :]
    return jnp.where(allowed[None], scores, -1e30)


def attend_forward(pieces):
    query_heads, key_heads, value_heads = pieces
    length = query_heads.shape[1]
    block_rows = min(length, 512)
    outputs = []
    totals = []
    for offset in range(0, length, block_rows):
        scores = block_scores(
            query_heads[:, offset : offset + block_rows], key_heads, offset, length
        )
        row_peak = jnp.max(scores, axis=-1, keepdims=True)
        exponent = jnp.exp(scores - row_peak)
        row_mass = jnp.sum(exponent, axis=-1, keepdims=True)
        outputs.append(
            jnp.einsum(
                "hqk,hke->hqe",
                (exponent / row_mass).astype(jnp.bfloat16),
                value_heads,
                preferred_element_type=jnp.float32,
            )
        )
        totals.append(row_peak + jnp.log(row_mass))
    return (jnp.concatenate(outputs, axis=1), jnp.concatenate(totals, axis=1))


def attend_backward(pieces):
    query_heads, key_heads, value_heads, grads_out, totals = pieces
    length = query_heads.shape[1]
    block_rows = min(length, 512)
    key_grad = jnp.zeros(key_heads.shape, jnp.float32)
    value_grad = jnp.zeros(value_heads.shape, jnp.float32)
    query_grads = []
    for offset in range(0, length, block_rows):
        query_block = query_heads[:, offset : offset + block_rows]
        grad_block = grads_out[:, offset : offset + block_rows]
        weights = jnp.exp(
            block_scores(query_block, key_heads, offset, length)
            - totals[:, offset : offset + block_rows]
        )
        grad_weights = jnp.einsum(
            "hqe,hke->hqk", grad_block, value_heads, preferred_element_type=jnp.float32
        )
        score_grad = (
            weights
            * (grad_weights - jnp.sum(weights * grad_weights, axis=-1, keepdims=True))
            * HEAD ** (-0.5)
        ).astype(jnp.bfloat16)
        query_grads.append(
            jnp.einsum("hqk,hke->hqe", score_grad, key_heads, preferred_element_type=jnp.float32)
        )
        key_grad = key_grad + jnp.einsum(
            "hqk,hqe->hke", score_grad, query_block, preferred_element_type=jnp.float32
        )
        value_grad = value_grad + jnp.einsum(
            "hqk,hqe->hke",
            weights.astype(jnp.bfloat16),
            grad_block,
            preferred_element_type=jnp.float32,
        )
    return (jnp.concatenate(query_grads, axis=1), key_grad, value_grad)


def branch_total(partial_sum):
    return lax.psum(partial_sum, "mp")


def input_total(partial_sum):
    return lax.psum(partial_sum, "mp")


def on_device(
    series,
    observed,
    routes,
    step_count,
    joint_proj,
    joint_moment,
    joint_square,
    mixer_proj,
    mixer_moment,
    mixer_square,
    upward_proj,
    upward_moment,
    upward_square,
    downward_proj,
    downward_moment,
    downward_square,
    readout,
    readout_moment,
    readout_square,
    vectors,
    vectors_moment,
    vectors_square,
):
    dp_count = lax.axis_size("dp")
    hidden_local = upward_proj.shape[3]
    joint_full, mixer_full, upward_full, downward_full, readout_complete, vector_full = (
        lax.all_gather(joint_proj.astype(jnp.bfloat16), "dp", axis=1, tiled=True),
        lax.all_gather(mixer_proj.astype(jnp.bfloat16), "dp", axis=1, tiled=True),
        lax.all_gather(upward_proj.astype(jnp.bfloat16), "dp", axis=1, tiled=True),
        lax.all_gather(downward_proj.astype(jnp.bfloat16), "dp", axis=2, tiled=True),
        lax.all_gather(readout.astype(jnp.bfloat16), "dp", axis=0, tiled=True),
        lax.all_gather(vectors.astype(jnp.bfloat16), "dp", axis=1, tiled=True),
    )
    up_local = upward_full.reshape(upward_full.shape[0], D, -1)
    shared_up_weight = up_local[-1]
    shared_down_weight = downward_full[-1]
    expert_up = up_local[:ROUTED_EXPERTS]
    expert_down = downward_full[:ROUTED_EXPERTS]
    gain_rows = vector_full.astype(jnp.float32)
    series_count, length = series.shape
    entries = series_count * length
    route_rows = routes.reshape(entries, 2)
    onehot = route_rows[:, :, None] == jnp.arange(ROUTED_EXPERTS, dtype=jnp.int32)[None, None, :]
    observed_future_series, valid_mask = targets_of(series, observed)
    expert_count, head_count = lax.psum(
        (jnp.sum(onehot.astype(jnp.float32), axis=(0, 1)), head_counts(valid_mask)), "dp"
    )
    total_tokens = entries * dp_count
    inputs = (series * observed.astype(jnp.float32)).reshape(entries, 1)

    def embed(gate_vector, up_vector):
        return jax.nn.silu(inputs * gate_vector) * (inputs * up_vector)

    embedded, embed_back = jax.vjp(embed, gain_rows[3], gain_rows[4])
    normed_one, norm_one_back = jax.vjp(rms_scale, embedded, gain_rows[0])
    first_input = normed_one.astype(jnp.bfloat16)
    projected = jnp.einsum(
        "td,cde->cte", first_input, joint_full, preferred_element_type=jnp.float32
    )
    cosine_table, sine_table = rope_tables(length, HEAD)
    query_heads = rotate(
        split_heads(projected[0], series_count, length), cosine_table, sine_table
    ).astype(jnp.bfloat16)
    key_heads = rotate(
        split_heads(projected[1], series_count, length), cosine_table, sine_table
    ).astype(jnp.bfloat16)
    value_heads = split_heads(projected[2], series_count, length).astype(jnp.bfloat16)
    attended, totals = lax.map(attend_forward, (query_heads, key_heads, value_heads))
    attended_low = merge_heads(attended).astype(jnp.bfloat16)
    after_attn = embedded + branch_total(
        jnp.dot(attended_low, mixer_full, preferred_element_type=jnp.float32)
    )
    normed_two, norm_two_back = jax.vjp(rms_scale, after_attn, gain_rows[1])
    second_input = normed_two.astype(jnp.bfloat16)
    logits = jnp.dot(
        second_input, readout_complete[:, : ROUTED_EXPERTS + 1], preferred_element_type=jnp.float32
    )

    def gating(logit_rows):
        probabilities = jax.nn.softmax(logit_rows[:, :ROUTED_EXPERTS], axis=-1)
        chosen = jnp.sum(jnp.where(onehot, probabilities[:, None, :], 0.0), axis=-1)
        balance = (
            aux_factor
            * ROUTED_EXPERTS
            * jnp.sum(expert_count / total_tokens * jnp.sum(probabilities, axis=0) / total_tokens)
        )
        return (chosen, jax.nn.sigmoid(logit_rows[:, ROUTED_EXPERTS]), balance)

    (gate_values, shared_gate, balance), gating_back = jax.vjp(gating, logits)
    capacity = entries // 2
    slot_index, source = dispatch_plan(route_rows, ROUTED_EXPERTS, capacity)
    token_of = source // 2
    padded_input = jnp.concatenate([second_input, jnp.zeros((1, D), jnp.bfloat16)], axis=0)
    gathered = padded_input[token_of].reshape(ROUTED_EXPERTS, capacity, D)
    gate_up = jnp.einsum("ecd,edf->ecf", gathered, expert_up, preferred_element_type=jnp.float32)
    hidden_f, swiglu_back = jax.vjp(swiglu, gate_up)
    hidden = hidden_f.astype(jnp.bfloat16)
    expert_out = jnp.einsum(
        "ecf,efd->ecd", hidden, expert_down, preferred_element_type=jnp.float32
    ).reshape(ROUTED_EXPERTS * capacity, D)
    picked = expert_out[slot_index].reshape(entries, 2, D)
    shared_up = jnp.dot(second_input, shared_up_weight, preferred_element_type=jnp.float32)
    shared_f, shared_back = jax.vjp(swiglu, shared_up)
    shared_hidden = shared_f.astype(jnp.bfloat16)
    shared_out = jnp.dot(shared_hidden, shared_down_weight, preferred_element_type=jnp.float32)
    mixed_part = (
        jnp.sum(gate_values[:, :, None] * picked, axis=1) + shared_gate[:, None] * shared_out
    )
    after_mixer = after_attn + branch_total(mixed_part)
    normalized_output, norm_out_back = jax.vjp(rms_scale, after_mixer, gain_rows[2])
    output_input = normalized_output.astype(jnp.bfloat16)
    model_estimates = jnp.dot(
        output_input, readout_complete[:, ROUTED_EXPERTS + 1 :], preferred_element_type=jnp.float32
    )
    prediction_misses = model_estimates - observed_future_series
    absolute_miss = jnp.abs(prediction_misses)
    horizon_importance_factors = head_weights(head_count)[None, :] * valid_mask
    robust_penalty_entries = jnp.where(
        absolute_miss <= quadratic_cutoff,
        0.5 * prediction_misses * prediction_misses,
        quadratic_cutoff * (absolute_miss - 0.5 * quadratic_cutoff),
    )
    local_loss = jnp.sum(robust_penalty_entries * horizon_importance_factors) + balance
    mp_count = lax.axis_size("mp")
    loss_total = lax.psum(local_loss, "dp")
    predicted_gradient = (
        jnp.clip(prediction_misses, -quadratic_cutoff, quadratic_cutoff)
        * horizon_importance_factors
    ).astype(jnp.bfloat16)
    head_grad = jnp.einsum(
        "ka,ky->ay", output_input, predicted_gradient, preferred_element_type=jnp.float32
    )
    out_input_grad = jnp.einsum(
        "aw,iw->ai",
        predicted_gradient,
        readout_complete[:, ROUTED_EXPERTS + 1 :],
        preferred_element_type=jnp.float32,
    )
    mixer_grad_in, gain_three_grad = norm_out_back(out_input_grad)
    picked_dots = jnp.sum(picked * mixer_grad_in[:, None, :], axis=-1)
    shared_dots = jnp.sum(shared_out * mixer_grad_in, axis=-1)
    gate_grads, shared_gate_grad = lax.psum((picked_dots, shared_dots), "mp")
    (logit_grad,) = gating_back((gate_grads, shared_gate_grad, jnp.ones((), jnp.float32)))
    logit_low = logit_grad.astype(jnp.bfloat16)
    router_grad = jnp.einsum(
        "ka,ky->ay", second_input, logit_low, preferred_element_type=jnp.float32
    )
    router_input_grad = jnp.einsum(
        "aw,iw->ai",
        logit_low,
        readout_complete[:, : ROUTED_EXPERTS + 1],
        preferred_element_type=jnp.float32,
    )
    gates_padded = jnp.concatenate([gate_values.reshape(-1), jnp.zeros((1,), jnp.float32)], axis=0)
    residual_padded = jnp.concatenate([mixer_grad_in, jnp.zeros((1, D), jnp.float32)], axis=0)
    expert_out_grad = (
        (gates_padded[source][:, None] * residual_padded[token_of])
        .astype(jnp.bfloat16)
        .reshape(ROUTED_EXPERTS, capacity, D)
    )
    hidden_grad = jnp.einsum(
        "ecd,efd->ecf", expert_out_grad, expert_down, preferred_element_type=jnp.float32
    )
    down_grad_experts = jnp.einsum(
        "ecf,ecd->efd", hidden, expert_out_grad, preferred_element_type=jnp.float32
    )
    gate_up_grad = swiglu_back(hidden_grad)[0].astype(jnp.bfloat16)
    up_grad_experts = jnp.einsum(
        "ecd,ecf->edf", gathered, gate_up_grad, preferred_element_type=jnp.float32
    )
    rows_grad = jnp.einsum(
        "ecf,edf->ecd", gate_up_grad, expert_up, preferred_element_type=jnp.float32
    ).reshape(ROUTED_EXPERTS * capacity, D)
    routed_grad = jnp.sum(rows_grad[slot_index].reshape(entries, 2, D), axis=1)
    shared_out_grad = (shared_gate[:, None] * mixer_grad_in).astype(jnp.bfloat16)
    shared_hidden_grad = jnp.einsum(
        "td,fd->tf", shared_out_grad, shared_down_weight, preferred_element_type=jnp.float32
    )
    down_grad_shared = jnp.einsum(
        "tf,td->fd", shared_hidden, shared_out_grad, preferred_element_type=jnp.float32
    )
    shared_up_grad = shared_back(shared_hidden_grad)[0].astype(jnp.bfloat16)
    up_grad_shared = jnp.einsum(
        "td,tf->df", second_input, shared_up_grad, preferred_element_type=jnp.float32
    )
    input_part = routed_grad + jnp.einsum(
        "tf,df->td", shared_up_grad, shared_up_weight, preferred_element_type=jnp.float32
    )
    second_input_grad = input_total(input_part) + router_input_grad
    upward_grad = jnp.concatenate([up_grad_experts, up_grad_shared[None]], axis=0).reshape(
        ROUTED_EXPERTS + 1, D, 2, hidden_local
    )
    downward_grad = jnp.concatenate([down_grad_experts, down_grad_shared[None]], axis=0)
    attn_grad_in, gain_two_grad = norm_two_back(second_input_grad)
    attn_total_grad = mixer_grad_in + attn_grad_in
    attn_low = attn_total_grad.astype(jnp.bfloat16)
    mixer_grad = jnp.einsum("tf,td->fd", attended_low, attn_low, preferred_element_type=jnp.float32)
    attended_grad = jnp.einsum(
        "td,fd->tf", attn_low, mixer_full, preferred_element_type=jnp.float32
    ).astype(jnp.bfloat16)
    query_grad, key_grad, value_grad = lax.map(
        attend_backward,
        (
            query_heads,
            key_heads,
            value_heads,
            split_heads(attended_grad, series_count, length),
            totals,
        ),
    )
    projected_grad = jnp.stack(
        [
            merge_heads(rotate(query_grad, cosine_table, -sine_table)),
            merge_heads(rotate(key_grad, cosine_table, -sine_table)),
            merge_heads(value_grad),
        ],
        axis=0,
    ).astype(jnp.bfloat16)
    joint_grad = jnp.einsum(
        "td,cte->cde", first_input, projected_grad, preferred_element_type=jnp.float32
    )
    first_input_grad = input_total(
        jnp.einsum("cte,cde->td", projected_grad, joint_full, preferred_element_type=jnp.float32)
    )
    embed_grad_in, gain_one_grad = norm_one_back(first_input_grad)
    gate_vector_grad, up_vector_grad = embed_back(attn_total_grad + embed_grad_in)
    vector_grad = jnp.stack(
        [gain_one_grad, gain_two_grad, gain_three_grad, gate_vector_grad, up_vector_grad], axis=0
    )
    readout_grad = jnp.concatenate([router_grad, head_grad], axis=1)
    joint_red, mixer_red, upward_red, downward_red, readout_red, vector_red = (
        lax.psum_scatter(joint_grad, "dp", scatter_dimension=1, tiled=True),
        lax.psum_scatter(mixer_grad, "dp", scatter_dimension=1, tiled=True),
        lax.psum_scatter(upward_grad, "dp", scatter_dimension=1, tiled=True),
        lax.psum_scatter(downward_grad, "dp", scatter_dimension=2, tiled=True),
        lax.psum_scatter(readout_grad, "dp", scatter_dimension=0, tiled=True),
        lax.psum_scatter(vector_grad, "dp", scatter_dimension=1, tiled=True),
    )
    split_squares = (
        jnp.sum(joint_red * joint_red)
        + jnp.sum(mixer_red * mixer_red)
        + jnp.sum(upward_red * upward_red)
        + jnp.sum(downward_red * downward_red)
    )
    shared_squares = jnp.sum(readout_red * readout_red) + jnp.sum(vector_red * vector_red)
    partial_squares = split_squares + shared_squares / mp_count
    norm_squared = lax.psum(partial_squares, ("dp", "mp"))
    grad_norm = jnp.sqrt(norm_squared)
    factor = clip_limit / (grad_norm + 1e-06)
    steps_taken = step_count[0].astype(jnp.float32)
    bias_one = 1.0 - beta_one**steps_taken
    bias_two = 1.0 - beta_two**steps_taken
    joint_new = adam_update(
        joint_proj, joint_moment, joint_square, joint_red, factor, bias_one, bias_two, matrix_rate
    )
    mixer_new = adam_update(
        mixer_proj, mixer_moment, mixer_square, mixer_red, factor, bias_one, bias_two, matrix_rate
    )
    upward_new = adam_update(
        upward_proj,
        upward_moment,
        upward_square,
        upward_red,
        factor,
        bias_one,
        bias_two,
        matrix_rate,
    )
    downward_new = adam_update(
        downward_proj,
        downward_moment,
        downward_square,
        downward_red,
        factor,
        bias_one,
        bias_two,
        matrix_rate,
    )
    readout_new = adam_update(
        readout,
        readout_moment,
        readout_square,
        readout_red,
        factor,
        bias_one,
        bias_two,
        matrix_rate,
    )
    vector_new = adam_update(
        vectors, vectors_moment, vectors_square, vector_red, factor, bias_one, bias_two, vector_rate
    )
    return (
        loss_total,
        grad_norm,
        joint_new[0],
        joint_new[1],
        joint_new[2],
        mixer_new[0],
        mixer_new[1],
        mixer_new[2],
        upward_new[0],
        upward_new[1],
        upward_new[2],
        downward_new[0],
        downward_new[1],
        downward_new[2],
        readout_new[0],
        readout_new[1],
        readout_new[2],
        vector_new[0],
        vector_new[1],
        vector_new[2],
    )


def solution(mesh):
    return jax.shard_map(
        on_device,
        mesh=mesh,
        in_specs=(
            P("dp", None),
            P("dp", None),
            P("dp", None, None),
            P(),
            P(None, "dp", "mp"),
            P(None, "dp", "mp"),
            P(None, "dp", "mp"),
            P("mp", "dp"),
            P("mp", "dp"),
            P("mp", "dp"),
            P(None, "dp", None, "mp"),
            P(None, "dp", None, "mp"),
            P(None, "dp", None, "mp"),
            P(None, "mp", "dp"),
            P(None, "mp", "dp"),
            P(None, "mp", "dp"),
            P("dp", None),
            P("dp", None),
            P("dp", None),
            P(None, "dp"),
            P(None, "dp"),
            P(None, "dp"),
        ),
        out_specs=(
            P(),
            P(),
            P(None, "dp", "mp"),
            P(None, "dp", "mp"),
            P(None, "dp", "mp"),
            P("mp", "dp"),
            P("mp", "dp"),
            P("mp", "dp"),
            P(None, "dp", None, "mp"),
            P(None, "dp", None, "mp"),
            P(None, "dp", None, "mp"),
            P(None, "mp", "dp"),
            P(None, "mp", "dp"),
            P(None, "mp", "dp"),
            P("dp", None),
            P("dp", None),
            P("dp", None),
            P(None, "dp"),
            P(None, "dp"),
            P(None, "dp"),
        ),
        check_vma=False,
    )
```

profile of v0, /device:TPU:0, one launch (start us, length us, event | category | flops | bytes accessed | tf_op | source)
XLA Modules:
  0.0 2251.1 jit_solution(2250609799435873)
XLA Ops:
  10.6 42.6 %all-gather = bf16[16,24,5]{1,2,0:T(8,128)(2,1)S(1)} all-gather(bf16[1,24,5]{1,2,0:T(8,128)(2,1)S(1)} %convert_bitcast_fusion.2), channel_id=1, replica_groups=mesh['dp'=16,'mp'=2] {'dp'}, dimensions={0}, use_global_device_ids=true | all-gather | bytes 4080 | tf_op jit(solution)/shard_map/all_gather | solution.py:244
  56.1 38.7 %all_gather.19 = bf16[3,384,192]{2,1,0:T(8,128)(2,1)S(1)} all-gather(bf16[3,24,192]{2,1,0:T(8,128)(2,1)S(1)} %convert_element_type.118), channel_id=1, replica_groups=mesh['dp'=16,'mp'=2] {'dp'}, dimensions={1}, use_global_device_ids=true | all-gather | bytes 470016 | tf_op jit(solution)/shard_map/all_gather | solution.py:239
  116.1 41.7 %while.28 = (s32[]{:T(128)}, bf16[2,6,1024,32]{2,3,1,0:T(8,128)(2,1)S(1)}, f32[2,6,1024,1]{2,1,3,0:T(8,128)S(1)}, bf16[2,6,1024,32]{2,3,1,0:T(8,128)(2,1)S(1)}, ...) while((s32[]{:T(128)}, bf16[2,6,1024,32]{2,3,1,0:T(8,128)(2,1)S(1)}, ...), condition=%wide.region_6.0_spmd.clone, body=%wide.region_1.6_spmd.sunk.clone | while | flops 882639360 | bytes 83906648 | solution.py:280
  158.9 38.5 %all_gather.20 = bf16[192,384]{0,1:T(8,128)(2,1)S(1)} all-gather(bf16[192,24]{0,1:T(8,128)(2,1)S(1)} %convert_element_type.124), channel_id=1, replica_groups=mesh['dp'=16,'mp'=2] {'dp'}, dimensions={1}, use_global_device_ids=true | all-gather | bytes 156672 | tf_op jit(solution)/shard_map/all_gather | solution.py:240
  209.7 15.5 scatter_custom_fusion
  225.3 37.8 %all_gather.21 = bf16[384,114]{1,0:T(8,128)(2,1)S(1)} all-gather(bf16[24,114]{1,0:T(8,128)(2,1)S(1)} %convert_element_type.126), channel_id=1, replica_groups=mesh['dp'=16,'mp'=2] {'dp'}, dimensions={0}, use_global_device_ids=true | all-gather | bytes 93024 | tf_op jit(solution)/shard_map/all_gather | solution.py:243
  272.6 33.1 %gather_fusion = bf16[8192,384]{1,0:T(8,128)(2,1)} fusion(bf16[2049,384]{1,0:T(8,128)(2,1)S(1)} %concatenate.214, s32[8192]{0:T(1024)S(1)} %get-tuple-element.382), kind=kCustom, calls=%fused_computation | custom fusion | bytes 12615680 | tf_op jit(solution)/shard_map/gather | solution.py:306
  305.7 27.9 %all-gather.4.cloned.1.call-done = bf16[9,384,2,768]{3,2,1,0:T(2,128)(2,1)} async-done(((bf16[9,24,2,768]{3,2,1,0:T(2,128)(2,1)}), bf16[9,384,2,768]{3,2,1,0:T(2,128)(2,1)}) %all-gather.4.cloned.1.call-update) | async-done | bytes 10616848 | tf_op jit(solution)/shard_map/all_gather | solution.py:241
  333.6 9.1 slice.725
  342.7 20.9 slice.546
  363.6 26.3 %fusion.253 = f32[8,1024,1536]{2,1,0:T(8,128)} fusion(bf16[8,1024,384]{2,1,0:T(8,128)(2,1)} %bitcast.917, bf16[8,384,1536]{2,1,0:T(8,128)(2,1)} %slice.546), kind=kOutput, calls=%fused_computation.574 | convolution fusion | flops 9663676416 | bytes 66060288 | tf_op jit(solution)/shard_map/ecd,edf->ecf/dot_general | solution.py:307
  389.9 22.0 multiply_convert_fusion.2
  411.9 7.5 all-gather.6.cloned.1.call-done
  419.4 13.7 fusion.167
  433.0 21.7 gather_fusion.1
  454.7 8.4 reshape.863
  474.3 32.1 %multiply_reduce_fusion.3 = f32[2048,384]{1,0:T(8,128)S(1)} fusion(f32[2048,2,384]{2,1,0:T(2,128)S(1)} %bitcast.915, f32[2048,2]{1,0:T(8,128)S(1)} %copy-done.22), kind=kLoop, calls=%fused_computation.165 | loop fusion | flops 2359296 | bytes 9453568 | tf_op jit(solution)/shard_map/reduce_sum | solution.py:319
  559.7 39.5 %psum.72 = f32[4]{0:T(128)S(1)} all-reduce(f32[4]{0:T(128)S(1)} %pad_maximum_fusion.6), channel_id=1, replica_groups=mesh['dp'=16,'mp'=2] {'dp'}, use_global_device_ids=true, to_apply=%region_83.84 | all-reduce | flops 4 | bytes 32 | tf_op jit(solution)/shard_map/psum | solution.py:257
  606.7 10.1 concatenate.285
  616.8 10.1 concatenate.249
  627.4 45.5 %gather_fusion.2 = f32[8192]{0:T(1024)S(1)} fusion(f32[4097]{0:T(1024)S(1)} %pad_maximum_fusion.5, s32[8192]{0:T(1024)S(1)} %get-tuple-element.381), kind=kCustom, calls=%fused_computation.2 | custom fusion | bytes 98304 | tf_op jit(solution)/shard_map/gather | solution.py:369
  684.1 32.0 %gather_fusion.3 = f32[8192,384]{1,0:T(8,128)} fusion(f32[2049,384]{1,0:T(8,128)S(1)} %concatenate.287, s32[8192]{0:T(1024)S(1)} %get-tuple-element.382), kind=kCustom, calls=%fused_computation.3 | custom fusion | bytes 25198592 | tf_op jit(solution)/shard_map/gather | solution.py:369
  716.2 42.5 %fusion.182 = (f32[8,1024,768]{2,1,0:T(8,128)}, f32[8,1024,768]{2,1,0:T(8,128)}) fusion(f32[8,1024,1536]{2,1,0:T(8,128)} %fusion.253, bf16[9,768,384]{1,2,0:T(8,128)(2,1)} %all-gather.6.cloned.1.call-done, f32[8,1024,384]{2,1,0:T(8,128)} %bitcast.912, f32[8,1024]{1,0:T(8,128)S(1)} %mul.997), kind=kOutput, calls=%fused_computation.209 | convolution fusion | flops 4913627136 | bytes 117997568 | tf_op jit(solution)/shard_map/ecd,efd->ecf/dot_general | solution.py:373
  758.7 25.5 %fusion.172 = f32[8,1024,384]{2,1,0:T(8,128)} fusion(bf16[8,384,1536]{2,1,0:T(8,128)(2,1)} %slice.546, f32[8,1024,768]{2,1,0:T(8,128)} %get-tuple-element.360, f32[8,1024,768]{2,1,0:T(8,128)} %get-tuple-element.359), kind=kOutput, calls=%fused_computation.180 | convolution fusion | flops 9688842240 | bytes 72351744 | tf_op jit(solution)/shard_map/ecf,edf->ecd/dot_general | solution.py:383
  784.2 21.7 gather_fusion.4
  805.9 8.2 reshape.866
  814.1 35.8 %reduce_sum.1049 = f32[2048,384]{1,0:T(8,128)} reduce(f32[2048,2,384]{2,1,0:T(2,128)} %reshape.866, f32[]{:T(128)} %constant.68.clone.1), dimensions={1}, to_apply=%region_91.92 | reduce | flops 786432 | bytes 9437188 | tf_op jit(solution)/shard_map/reduce_sum | solution.py:386
  849.9 7.5 fusion.196
  867.9 34.4 %multiply_reduce_fusion.2 = f32[2048,2]{1,0:T(8,128)} fusion(f32[2048,2,384]{2,1,0:T(2,128)} %reshape.863, f32[2048,384]{1,0:T(8,128)S(1)} %copy-done.10), kind=kLoop, calls=%fused_computation.161 | loop fusion | flops 3141632 | bytes 9453568 | tf_op jit(solution)/shard_map/reduce_sum | solution.py:352
  902.3 6.4 all-reduce.15
  909.3 36.8 %psum.73 = f32[8]{0:T(128)S(1)} all-reduce(f32[8]{0:T(128)S(1)} %get-tuple-element.216), channel_id=1, replica_groups=mesh['dp'=16,'mp'=2] {'dp'}, use_global_device_ids=true, to_apply=%region_86.87 | all-reduce | flops 8 | bytes 64 | tf_op jit(solution)/shard_map/psum | solution.py:257
  966.6 328.3 %while.29 = (s32[]{:T(128)}, f32[2,6,1024,32]{2,3,1,0:T(8,128)}, f32[2,6,1024,32]{2,3,1,0:T(8,128)}, bf16[2,6,1024,32]{2,3,1,0:T(8,128)(2,1)}, bf16[2,6,1024,32]...) while((s32[]{:T(128)}, f32[2,6,1024,32]{2,3,1,0:T(8,128)}, ...), condition=%wide.region_103.104_spmd.clone, body=%wide.region_100.103_spmd.sunk.clone | while | flops 2178499072 | bytes 298109600 | solution.py:413
  967.9 6.4 fusion.397
  982.2 34.9 %fusion.400 = f32[6,1024,32]{1,2,0:T(8,128)} fusion(f32[6,512,1024]{2,1,0:T(8,128)} %fusion.396, f32[6,512,1024]{2,1,0:T(8,128)} %fusion.397, f32[6,512]{1,0:T(8,128)S(1)} %get-tuple-element.675, pred[512,1024]{1,0:T(8,128)(4,1)} %iota_compare_fusion.18, bf16[6,1024,32]{1,2,0:T(8,128)(2,1)S(1)} %get-tuple-element.673), kind=kOutput, calls=%fused_computation.59.clone.1.clone | convolution fusion | flops 235933696 | bytes 52396032 | tf_op jit(solution)/shard_map/while/body/eval_jaxpr/hqk,hqe->hke/dot_general | solution.py:192
  1017.1 6.4 fusion.394
  1023.5 6.4 fusion.393
  1031.1 29.8 %fusion.401 = f32[2,6,1024,32]{2,3,1,0:T(8,128)} fusion(f32[2,6,1024,32]{2,3,1,0:T(8,128)} %get-tuple-element.715, s32[]{:T(128)} %get-tuple-element.713, f32[6,1024,32]{1,2,0:T(8,128)} %fusion.400, f32[6,512,1024]{2,1,0:T(8,128)} %fusion.393, f32[6,512,1024]{2,1,0:T(8,128)} %fusion.394, f32[6,512]{1,0:T(8,128)S(1)} %get-tuple-element.674, ...), kind=kOutput, calls=%fused_computation.91.clone.1.clone | convolution fusion | flops 236130304 | bytes 53182976 | tf_op jit(solution)/shard_map/while/body/eval_jaxpr/hqk,hqe->hke/dot_general | solution.py:192
  1060.9 27.7 %fusion.398 = f32[6,512,32]{1,2,0:T(8,128)S(1)} fusion(f32[6,512,1024]{2,1,0:T(8,128)} %fusion.396, f32[6,512,1024]{2,1,0:T(8,128)} %fusion.397, f32[6,512]{1,0:T(8,128)S(1)} %get-tuple-element.675, pred[512,1024]{1,0:T(8,128)(4,1)} %iota_compare_fusion.18, bf16[2,6,1024,32]{2,3,1,0:T(8,128)(2,1)S(1)} %get-tuple-element.727, ...), kind=kOutput, calls=%fused_computation.60.clone.1.clone | convolution fusion | flops 235933696 | bytes 52199936 | tf_op jit(solution)/shard_map/while/body/eval_jaxpr/hqk,hke->hqe/dot_general | solution.py:190
  1088.6 27.4 %fusion.395 = f32[6,512,32]{1,2,0:T(8,128)S(1)} fusion(f32[6,512,1024]{2,1,0:T(8,128)} %fusion.393, f32[6,512,1024]{2,1,0:T(8,128)} %fusion.394, f32[6,512]{1,0:T(8,128)} %copy-done.53, pred[512,1024]{1,0:T(8,128)(4,1)} %iota_compare_fusion.17, bf16[2,6,1024,32]{2,3,1,0:T(8,128)(2,1)S(1)} %get-tuple-element.727, s32[]{:T(128)} %get-tuple-element.713), kind=kOutput, calls=%fused_computation.63.clone.1.clone | convolution fusion | flops 235933696 | bytes 52199936 | tf_op jit(solution)/shard_map/while/body/eval_jaxpr/hqk,hke->hqe/dot_general | solution.py:190
  1117.0 6.6 fusion.402
  1123.5 7.1 fusion.403
  1146.1 34.9 %fusion.400 = f32[6,1024,32]{1,2,0:T(8,128)} fusion(f32[6,512,1024]{2,1,0:T(8,128)} %fusion.396, f32[6,512,1024]{2,1,0:T(8,128)} %fusion.397, f32[6,512]{1,0:T(8,128)S(1)} %get-tuple-element.675, pred[512,1024]{1,0:T(8,128)(4,1)} %iota_compare_fusion.18, bf16[6,1024,32]{1,2,0:T(8,128)(2,1)S(1)} %get-tuple-element.673), kind=kOutput, calls=%fused_computation.59.clone.1.clone | convolution fusion | flops 235933696 | bytes 52396032 | tf_op jit(solution)/shard_map/while/body/eval_jaxpr/hqk,hqe->hke/dot_general | solution.py:192
  1181.0 6.4 fusion.394
  1187.4 6.4 fusion.393
  1194.9 29.8 %fusion.401 = f32[2,6,1024,32]{2,3,1,0:T(8,128)} fusion(f32[2,6,1024,32]{2,3,1,0:T(8,128)} %get-tuple-element.715, s32[]{:T(128)} %get-tuple-element.713, f32[6,1024,32]{1,2,0:T(8,128)} %fusion.400, f32[6,512,1024]{2,1,0:T(8,128)} %fusion.393, f32[6,512,1024]{2,1,0:T(8,128)} %fusion.394, f32[6,512]{1,0:T(8,128)S(1)} %get-tuple-element.674, ...), kind=kOutput, calls=%fused_computation.91.clone.1.clone | convolution fusion | flops 236130304 | bytes 53182976 | tf_op jit(solution)/shard_map/while/body/eval_jaxpr/hqk,hqe->hke/dot_general | solution.py:192
  1224.7 27.7 %fusion.398 = f32[6,512,32]{1,2,0:T(8,128)S(1)} fusion(f32[6,512,1024]{2,1,0:T(8,128)} %fusion.396, f32[6,512,1024]{2,1,0:T(8,128)} %fusion.397, f32[6,512]{1,0:T(8,128)S(1)} %get-tuple-element.675, pred[512,1024]{1,0:T(8,128)(4,1)} %iota_compare_fusion.18, bf16[2,6,1024,32]{2,3,1,0:T(8,128)(2,1)S(1)} %get-tuple-element.727, ...), kind=kOutput, calls=%fused_computation.60.clone.1.clone | convolution fusion | flops 235933696 | bytes 52199936 | tf_op jit(solution)/shard_map/while/body/eval_jaxpr/hqk,hke->hqe/dot_general | solution.py:190
  1252.5 27.4 %fusion.395 = f32[6,512,32]{1,2,0:T(8,128)S(1)} fusion(f32[6,512,1024]{2,1,0:T(8,128)} %fusion.393, f32[6,512,1024]{2,1,0:T(8,128)} %fusion.394, f32[6,512]{1,0:T(8,128)} %copy-done.53, pred[512,1024]{1,0:T(8,128)(4,1)} %iota_compare_fusion.17, bf16[2,6,1024,32]{2,3,1,0:T(8,128)(2,1)S(1)} %get-tuple-element.727, s32[]{:T(128)} %get-tuple-element.713), kind=kOutput, calls=%fused_computation.63.clone.1.clone | convolution fusion | flops 235933696 | bytes 52199936 | tf_op jit(solution)/shard_map/while/body/eval_jaxpr/hqk,hke->hqe/dot_general | solution.py:190
  1280.8 6.6 fusion.402
  1287.4 7.1 fusion.403
  1322.7 14.3 fusion.183
  1337.0 8.4 pad_maximum_fusion.1
  1345.4 15.0 copy.264
  1360.5 26.5 %fusion.171 = f32[8,384,1536]{2,1,0:T(8,128)} fusion(bf16[8,1024,384]{2,1,0:T(8,128)(2,1)} %bitcast.918, f32[8,1024,768]{2,1,0:T(8,128)} %get-tuple-element.360, f32[8,1024,768]{2,1,0:T(8,128)} %get-tuple-element.359), kind=kOutput, calls=%fused_computation.179 | convolution fusion | flops 9688842240 | bytes 75497472 | tf_op jit(solution)/shard_map/ecd,ecf->edf/dot_general | solution.py:380
  1387.0 22.5 concatenate.290
  1409.5 8.7 fusion.192
  1421.2 14.2 copy_bitcast_fusion
  1435.4 25.5 %reshape.929 = f32[384,13824]{1,0:T(8,128)} reshape(f32[384,9,2,768]{3,2,1,0:T(2,128)} %copy_bitcast_fusion) | data formatting | bytes 42467328
  1465.8 84.5 %all-reduce.30.cloned.1.call-done = (f32[3,384,192]{2,0,1:T(4,128)}, f32[384,114]{0,1:T(8,128)}) async-done(((f32[3,384,192]{2,0,1:T(4,128)}, f32[384,114]{0,1:T(8,128)}), (f32[3,384,192]{2,0,1:T(4,128)}, f32[384,114]{0,1:T(8,128)})) %all-reduce.30.cloned.1.call-update) | async-done | bytes 1059856
  1553.5 21.4 all-reduce.28.cloned.1.call-done
  1584.3 81.5 %all-reduce.13 = (f32[]{:T(128)}, f32[5,384]{1,0:T(8,128)S(1)}) all-reduce(f32[]{:T(128)S(6)} %add.368, f32[5,384]{1,0:T(8,128)S(1)} %stack.351), channel_id=1, replica_groups=mesh['dp'=16,'mp'=2] {'dp'}, use_global_device_ids=true, to_apply=%region_89.90 | all-reduce | flops 1921 | bytes 15368 | tf_op jit(solution)/shard_map/psum | solution.py:337
  1667.7 199.7 %reduce-scatter.10.cloned.1.call-done = f32[9,768,24]{1,0,2:T(8,128)} async-done(((f32[9,768,384]{1,0,2:T(8,128)}), f32[9,768,24]{1,0,2:T(8,128)}) %reduce-scatter.10.cloned.1.call-update) | async-done | bytes 663568 | tf_op jit(solution)/shard_map/reduce_scatter | solution.py:447
  1869.6 315.4 %reduce-scatter.12.cloned.1.call-done = f32[24,13824]{1,0:T(8,128)} async-done(((f32[384,13824]{1,0:T(8,128)}), f32[24,13824]{1,0:T(8,128)}) %reduce-scatter.12.cloned.1.call-update) | async-done | bytes 1327120
  2190.6 39.4 %psum.79 = f32[]{:T(128)} all-reduce(f32[]{:T(128)S(6)} %add.381), channel_id=1, replica_groups=mesh['dp'=16,'mp'=2] {'dp','mp'}, use_global_device_ids=true, to_apply=%region_123.124 | all-reduce | flops 1 | bytes 8 | tf_op jit(solution)/shard_map/psum | solution.py:459
  2231.6 6.9 multiply_subtract_fusion
  (619 shorter events, 246.0 us)
Async XLA Ops:
  8.0 255.1 %all-reduce.22.cloned.1.call-start = ((), (), s32[]{:S(2)}) async-start(), calls=%async_computation.3 | async-start | bytes 6291456 | tf_op jit(solution)/shard_map/psum | solution.py:205
  9.9 87.9 %copy-start.54 = (f32[1,8,2,128]{3,1,2,0:T(8,128)}, f32[1,8,2,128]{3,1,2,0:T(8,128)S(1)}, u32[]{:S(2)}) copy-start(f32[1,8,2,128]{3,1,2,0:T(8,128)S(1)} %copy.444) | copy-start | bytes 24580
  53.8 41.0 %copy-start.69 = (f32[384]{0:T(512)}, f32[384]{0:T(512)S(1)}, u32[]{:S(2)}) copy-start(f32[384]{0:T(512)S(1)} %get-tuple-element.220) | copy-start | bytes 4612
  53.8 41.0 %copy-start.73 = (f32[384]{0:T(512)}, f32[384]{0:T(512)S(1)}, u32[]{:S(2)}) copy-start(f32[384]{0:T(512)S(1)} %get-tuple-element.221) | copy-start | bytes 4612
  53.8 44.0 %copy-start.110 = (f32[384]{0:T(512)}, f32[384]{0:T(512)S(1)}, u32[]{:S(2)}) copy-start(f32[384]{0:T(512)S(1)} %get-tuple-element.219) | copy-start | bytes 4612
  55.2 39.6 %copy-start.97 = (f32[2048]{0:T(1024)}, f32[2048]{0:T(1024)S(1)}, u32[]{:S(2)}) copy-start(f32[2048]{0:T(1024)S(1)} %multiply_reduce_fusion.14) | copy-start | bytes 24580
  55.2 39.6 %copy-start.80 = (f32[2048]{0:T(1024)}, f32[2048]{0:T(1024)S(1)}, u32[]{:S(2)}) copy-start(f32[2048]{0:T(1024)S(1)} %fusion.227) | copy-start | bytes 24580
  157.8 42.7 %copy-start = (bf16[2,6,1024,32]{2,3,1,0:T(8,128)(2,1)}, bf16[2,6,1024,32]{2,3,1,0:T(8,128)(2,1)S(1)}, u32[]{:S(2)}) copy-start(bf16[2,6,1024,32]{2,3,1,0:T(8,128)(2,1)S(1)} %get-tuple-element.744) | copy-start | bytes 2359300
  157.8 42.7 %copy-start.15 = (bf16[2,6,1024,32]{2,3,1,0:T(8,128)(2,1)}, bf16[2,6,1024,32]{2,3,1,0:T(8,128)(2,1)S(1)}, u32[]{:S(2)}) copy-start(bf16[2,6,1024,32]{2,3,1,0:T(8,128)(2,1)S(1)} %get-tuple-element.750) | copy-start | bytes 2359300
  157.8 42.7 %copy-start.17 = (bf16[2,6,1024,32]{2,3,1,0:T(8,128)(2,1)}, bf16[2,6,1024,32]{2,3,1,0:T(8,128)(2,1)S(1)}, u32[]{:S(2)}) copy-start(bf16[2,6,1024,32]{2,3,1,0:T(8,128)(2,1)S(1)} %get-tuple-element.751) | copy-start | bytes 2359300
  157.8 42.7 %copy-start.52 = (f32[2,6,1024,1]{2,1,3,0:T(8,128)}, f32[2,6,1024,1]{2,1,3,0:T(8,128)S(1)}, u32[]{:S(2)}) copy-start(f32[2,6,1024,1]{2,1,3,0:T(8,128)S(1)} %get-tuple-element.710) | copy-start | bytes 147460
  158.9 38.6 %copy-start.23 = (bf16[24,8,2,1024]{3,1,2,0:T(8,128)(2,1)}, bf16[24,8,2,1024]{3,1,2,0:T(8,128)(2,1)S(1)}, u32[]{:S(2)}) copy-start(bf16[24,8,2,1024]{3,1,2,0:T(8,128)(2,1)S(1)} %copy.279) | copy-start | bytes 2359300
  200.6 133.0 %all-gather.4.cloned.1.call-start = ((), (), s32[]{:S(2)}) async-start(), calls=%async_computation.4 | async-start | bytes 11280384 | tf_op jit(solution)/shard_map/all_gather | solution.py:241
  203.3 216.1 %all-gather.6.cloned.1.call-start = ((), (), s32[]{:S(2)}) async-start(), calls=%async_computation.5 | async-start | bytes 5640192 | tf_op jit(solution)/shard_map/all_gather | solution.py:242
  204.1 59.0 %copy-start.55 = (f32[1,8,2,128]{3,1,2,0:T(8,128)S(1)}, f32[1,8,2,128]{3,1,2,0:T(8,128)}, u32[]{:S(2)}) copy-start(f32[1,8,2,128]{3,1,2,0:T(8,128)} %copy-done.54) | copy-start | bytes 24580
  204.2 59.0 %copy-start.70 = (f32[384]{0:T(512)S(1)}, f32[384]{0:T(512)}, u32[]{:S(2)}) copy-start(f32[384]{0:T(512)} %copy-done.69) | copy-start | bytes 4612
  204.2 59.0 %copy-start.74 = (f32[384]{0:T(512)S(1)}, f32[384]{0:T(512)}, u32[]{:S(2)}) copy-start(f32[384]{0:T(512)} %copy-done.73) | copy-start | bytes 4612
  204.2 468.9 %all-reduce.24.cloned.1.call-start = ((), (), s32[]{:S(2)}) async-start(), calls=%async_computation.6 | async-start | bytes 6291456 | tf_op jit(solution)/shard_map/psum | solution.py:205
  207.9 59.7 %copy-start.112 = (f32[384]{0:T(512)S(1)}, f32[384]{0:T(512)}, u32[]{:S(2)}) copy-start(f32[384]{0:T(512)} %get-tuple-element.218) | copy-start | bytes 4612
  263.0 415.3 %copy-start.42 = (bf16[384,114]{1,0:T(8,128)(2,1)}, bf16[384,114]{1,0:T(8,128)(2,1)S(1)}, u32[]{:S(2)}) copy-start(bf16[384,114]{1,0:T(8,128)(2,1)S(1)} %all_gather.21) | copy-start | bytes 262660
  263.1 170.0 %copy-start.63 = (s32[4096]{0:T(1024)}, s32[4096]{0:T(1024)S(1)}, u32[]{:S(2)}) copy-start(s32[4096]{0:T(1024)S(1)} %broadcast_clamp_fusion) | copy-start | bytes 49156
  269.1 195.5 %copy-start.13 = (bf16[2048,384]{1,0:T(8,128)(2,1)}, bf16[2048,384]{1,0:T(8,128)(2,1)S(1)}, u32[]{:S(2)}) copy-start(bf16[2048,384]{1,0:T(8,128)(2,1)S(1)} %multiply_convert_fusion.7) | copy-start | bytes 4718596
  269.7 35.9 %copy-start.37 = (f32[2048,9]{0,1:T(8,128)}, f32[2048,9]{0,1:T(8,128)S(1)}, u32[]{:S(2)}) copy-start(f32[2048,9]{0,1:T(8,128)S(1)} %fusion.207) | copy-start | bytes 221188
  305.7 200.7 %copy-start.88 = (f32[2048,1]{0,1:T(1,128)}, f32[2048,1]{0,1:T(1,128)S(1)}, u32[]{:S(2)}) copy-start(f32[2048,1]{0,1:T(1,128)S(1)} %fusion.226) | copy-start | bytes 24580
  474.3 32.1 %copy-start.21 = (bf16[2048,768]{1,0:T(8,128)(2,1)}, bf16[2048,768]{1,0:T(8,128)(2,1)S(1)}, u32[]{:S(2)}) copy-start(bf16[2048,768]{1,0:T(8,128)(2,1)S(1)} %multiply_convert_fusion.4) | copy-start | bytes 9437188
  512.0 92.5 %copy-start.51 = (f32[2,1024]{1,0:T(2,128)S(1)}, f32[2,1024]{1,0:T(2,128)}, u32[]{:S(2)}) copy-start(f32[2,1024]{1,0:T(2,128)} %param.26) | copy-start | bytes 24580
  512.0 92.7 %copy-start.107 = (f32[1,1,2,1024]{3,2,1,0:T(2,128)S(1)}, f32[1,1,2,1024]{3,2,1,0:T(2,128)}, u32[]{:S(2)}) copy-start(f32[1,1,2,1024]{3,2,1,0:T(2,128)} %get-tuple-element.453) | copy-start | bytes 24580
  512.0 92.7 %copy-start.106 = (f32[1,1,2,1024]{3,2,1,0:T(2,128)S(1)}, f32[1,1,2,1024]{3,2,1,0:T(2,128)}, u32[]{:S(2)}) copy-start(f32[1,1,2,1024]{3,2,1,0:T(2,128)} %get-tuple-element.454) | copy-start | bytes 24580
  512.0 92.7 %copy-start.105 = (f32[1,1,2,1024]{3,2,1,0:T(2,128)S(1)}, f32[1,1,2,1024]{3,2,1,0:T(2,128)}, u32[]{:S(2)}) copy-start(f32[1,1,2,1024]{3,2,1,0:T(2,128)} %get-tuple-element.455) | copy-start | bytes 24580
  512.0 92.7 %copy-start.104 = (f32[1,1,2,1024]{3,2,1,0:T(2,128)S(1)}, f32[1,1,2,1024]{3,2,1,0:T(2,128)}, u32[]{:S(2)}) copy-start(f32[1,1,2,1024]{3,2,1,0:T(2,128)} %get-tuple-element.456) | copy-start | bytes 24580
  512.0 94.6 %copy-start.103 = (f32[1,1,2,1024]{3,2,1,0:T(2,128)S(1)}, f32[1,1,2,1024]{3,2,1,0:T(2,128)}, u32[]{:S(2)}) copy-start(f32[1,1,2,1024]{3,2,1,0:T(2,128)} %get-tuple-element.449) | copy-start | bytes 24580
  512.1 94.6 %copy-start.102 = (f32[1,1,2,1024]{3,2,1,0:T(2,128)S(1)}, f32[1,1,2,1024]{3,2,1,0:T(2,128)}, u32[]{:S(2)}) copy-start(f32[1,1,2,1024]{3,2,1,0:T(2,128)} %get-tuple-element.450) | copy-start | bytes 24580
  512.1 94.6 %copy-start.101 = (f32[1,1,2,1024]{3,2,1,0:T(2,128)S(1)}, f32[1,1,2,1024]{3,2,1,0:T(2,128)}, u32[]{:S(2)}) copy-start(f32[1,1,2,1024]{3,2,1,0:T(2,128)} %get-tuple-element.451) | copy-start | bytes 24580
  512.1 94.6 %copy-start.100 = (f32[1,1,2,1024]{3,2,1,0:T(2,128)S(1)}, f32[1,1,2,1024]{3,2,1,0:T(2,128)}, u32[]{:S(2)}) copy-start(f32[1,1,2,1024]{3,2,1,0:T(2,128)} %get-tuple-element.452) | copy-start | bytes 24580
  512.1 440.3 %all-reduce.26.cloned.1.call-start = ((), (), s32[]{:S(2)}) async-start(), calls=%async_computation.7 | async-start | bytes 6291456 | tf_op jit(solution)/shard_map/psum | solution.py:209
  627.4 45.6 %copy-start.3 = (f32[2048,384]{1,0:T(8,128)S(1)}, f32[2048,384]{1,0:T(8,128)}, u32[]{:S(2)}) copy-start(f32[2048,384]{1,0:T(8,128)} %all-reduce.22.cloned.1.call-done) | copy-start | bytes 9437188
  673.0 43.2 %copy-start.44 = (f32[8,1024]{1,0:T(8,128)}, f32[8,1024]{1,0:T(8,128)S(1)}, u32[]{:S(2)}) copy-start(f32[8,1024]{1,0:T(8,128)S(1)} %mul.997) | copy-start | bytes 98308
  814.1 35.8 %copy-start.10 = (f32[2048,384]{1,0:T(8,128)S(1)}, f32[2048,384]{1,0:T(8,128)}, u32[]{:S(2)}) copy-start(f32[2048,384]{1,0:T(8,128)} %copy-done.9) | copy-start | bytes 9437188
  814.1 35.8 %copy-start.89 = (f32[2048,1]{0,1:T(1,128)S(1)}, f32[2048,1]{0,1:T(1,128)}, u32[]{:S(2)}) copy-start(f32[2048,1]{0,1:T(1,128)} %copy-done.88) | copy-start | bytes 24580
  867.2 597.3 %reduce-scatter.8.cloned.1.call-start = ((), (), s32[]{:S(2)}) async-start(), calls=%async_computation.8 | async-start | bytes 417792 | tf_op jit(solution)/shard_map/reduce_scatter | solution.py:445
  867.8 34.5 %copy-start.94 = (f32[2048]{0:T(1024)S(1)}, f32[2048]{0:T(1024)}, u32[]{:S(2)}) copy-start(f32[2048]{0:T(1024)} %get-tuple-element.343) | copy-start | bytes 24580
  867.9 41.2 %copy-start.60 = (s32[2,1024,2]{1,2,0:T(2,128)S(1)}, s32[2,1024,2]{1,2,0:T(2,128)}, u32[]{:S(2)}) copy-start(s32[2,1024,2]{1,2,0:T(2,128)} %param.28) | copy-start | bytes 49156
  867.9 78.2 %copy-start.120 = (f32[8]{0:T(128)S(1)}, f32[8]{0:T(128)}, u32[]{:S(2)}) copy-start(f32[8]{0:T(128)} %get-tuple-element.345) | copy-start | bytes 100
  867.9 78.8 %copy-start.38 = (f32[2048,9]{0,1:T(8,128)S(1)}, f32[2048,9]{0,1:T(8,128)}, u32[]{:S(2)}) copy-start(f32[2048,9]{0,1:T(8,128)} %copy-done.37) | copy-start | bytes 221188
  867.9 78.8 %copy-start.62 = (f32[2048]{0:T(1024)S(1)}, f32[2048]{0:T(1024)}, u32[]{:S(2)}) copy-start(f32[2048]{0:T(1024)} %copy-done.61) | copy-start | bytes 24580
  902.3 46.8 %copy-start.66 = (f32[2048]{0:T(1024)S(1)}, f32[2048]{0:T(1024)}, u32[]{:S(2)}) copy-start(f32[2048]{0:T(1024)} %copy-done.65) | copy-start | bytes 24580
  909.2 43.2 %copy-start.4 = (f32[2048,384]{1,0:T(8,128)S(1)}, f32[2048,384]{1,0:T(8,128)}, u32[]{:S(2)}) copy-start(f32[2048,384]{1,0:T(8,128)} %all-reduce.22.cloned.1.call-done) | copy-start | bytes 9437188
  909.2 43.2 %copy-start.43 = (bf16[384,114]{1,0:T(8,128)(2,1)S(1)}, bf16[384,114]{1,0:T(8,128)(2,1)}, u32[]{:S(2)}) copy-start(bf16[384,114]{1,0:T(8,128)(2,1)} %copy-done.42) | copy-start | bytes 262660
  909.2 43.2 %copy-start.56 = (f32[1,8,2,128]{3,1,2,0:T(8,128)S(1)}, f32[1,8,2,128]{3,1,2,0:T(8,128)}, u32[]{:S(2)}) copy-start(f32[1,8,2,128]{3,1,2,0:T(8,128)} %copy-done.54) | copy-start | bytes 24580
  909.2 43.2 %copy-start.71 = (f32[384]{0:T(512)S(1)}, f32[384]{0:T(512)}, u32[]{:S(2)}) copy-start(f32[384]{0:T(512)} %copy-done.69) | copy-start | bytes 4612
  909.2 43.2 %copy-start.75 = (f32[384]{0:T(512)S(1)}, f32[384]{0:T(512)}, u32[]{:S(2)}) copy-start(f32[384]{0:T(512)} %copy-done.73) | copy-start | bytes 4612
  909.3 43.2 %copy-start.87 = (f32[2048]{0:T(1024)S(1)}, f32[2048]{0:T(1024)}, u32[]{:S(2)}) copy-start(f32[2048]{0:T(1024)} %copy-done.86) | copy-start | bytes 24580
  981.3 49.8 %copy-start.53 = (f32[6,512]{1,0:T(8,128)}, f32[6,512]{1,0:T(8,128)S(1)}, u32[]{:S(2)}) copy-start(f32[6,512]{1,0:T(8,128)S(1)} %get-tuple-element.674) | copy-start | bytes 36868 | tf_op jit(solution)/shard_map/while
  1145.2 49.8 %copy-start.53 = (f32[6,512]{1,0:T(8,128)}, f32[6,512]{1,0:T(8,128)S(1)}, u32[]{:S(2)}) copy-start(f32[6,512]{1,0:T(8,128)S(1)} %get-tuple-element.674) | copy-start | bytes 36868 | tf_op jit(solution)/shard_map/while
  1303.8 246.5 %all-reduce.30.cloned.1.call-start = ((), (), s32[]{:S(2)}) async-start(), calls=%async_computation.12 | async-start | bytes 3514368
  1310.7 264.2 %all-reduce.28.cloned.1.call-start = ((), (), s32[]{:S(2)}) async-start(), calls=%async_computation.10 | async-start | bytes 6291456 | tf_op jit(solution)/shard_map/psum | solution.py:209
  1316.1 551.4 %reduce-scatter.10.cloned.1.call-start = ((), (), s32[]{:S(2)}) async-start(), calls=%async_computation.9 | async-start | bytes 20054016 | tf_op jit(solution)/shard_map/reduce_scatter | solution.py:447
  1360.5 824.6 %reduce-scatter.12.cloned.1.call-start = ((), (), s32[]{:S(2)}) async-start(), calls=%async_computation.11 | async-start | bytes 22560768
  1460.9 117.1 %copy-start.98 = (f32[2048]{0:T(1024)S(1)}, f32[2048]{0:T(1024)}, u32[]{:S(2)}) copy-start(f32[2048]{0:T(1024)} %copy-done.97) | copy-start | bytes 24580
  1461.0 117.1 %copy-start.6 = (f32[2048,384]{1,0:T(8,128)S(1)}, f32[2048,384]{1,0:T(8,128)}, u32[]{:S(2)}) copy-start(f32[2048,384]{1,0:T(8,128)} %copy-done.5) | copy-start | bytes 9437188
  1582.8 648.0 %copy-start.114 = (f32[5,24]{1,0:T(8,128)S(1)}, f32[5,24]{1,0:T(8,128)}, u32[]{:S(2)}) copy-start(f32[5,24]{1,0:T(8,128)} %param.45) | copy-start | bytes 1444
  1582.8 648.0 %copy-start.118 = (f32[5,24]{1,0:T(8,128)S(1)}, f32[5,24]{1,0:T(8,128)}, u32[]{:S(2)}) copy-start(f32[5,24]{1,0:T(8,128)} %param.47) | copy-start | bytes 1444
  1582.8 648.0 %copy-start.119 = (f32[5,24]{1,0:T(8,128)S(1)}, f32[5,24]{1,0:T(8,128)}, u32[]{:S(2)}) copy-start(f32[5,24]{1,0:T(8,128)} %param.46) | copy-start | bytes 1444
  1582.8 648.7 %copy-start.26 = (f32[9,24,2,768]{3,2,1,0:T(2,128)S(1)}, f32[9,24,2,768]{3,2,1,0:T(2,128)}, u32[]{:S(2)}) copy-start(f32[9,24,2,768]{3,2,1,0:T(2,128)} %param.36) | copy-start | bytes 3981316
  (76 other events, 366.9 us)
Sparse Core Ops, SparseCore 0:
  200.7 19.1 all-reduce.21
  512.2 22.0 all-reduce.23
  867.3 19.2 all-reduce.25
Sparse Core Ops, SparseCore 1:
  204.4 129.2 all-gather.3
  336.8 82.6 all-gather.5
  1303.9 120.8 reduce-scatter.7
  1430.5 119.8 all-reduce.29
  1552.7 22.1 all-reduce.27
  1580.6 286.8 reduce-scatter.9
  1873.3 311.7 reduce-scatter.11
where the time goes:
time: 2260 us; the launch traced here: 2250 us
  waiting for transfers between devices  657 us (29%)
  matrix products  556 us (25%)
  local copies, waits for them, and re-layouts  367 us (16%)
  blocking collectives  361 us (16%)
  other arithmetic  239 us (11%)
  between operations  69.7 us (3%)
    unnamed x12, waiting for transfers between devices  400 us
    reduce_scatter x1, waiting for transfers between devices, on_device(): lax.psum_scatter(downward_grad, 'dp', scatter_dimension=2, tiled=True)  200 us
    dot_general x4, matrix products, attend_backward(): jnp.einsum('hqk,hqe->hke', score_grad, query_block, preferred_element_typ...  129 us
    dot_general x4, matrix products, attend_backward(): jnp.einsum('hqk,hke->hqe', score_grad, key_heads, preferred_element_type=...  110 us
    psum x1, blocking collectives, on_device(): loss_total = lax.psum(local_loss, 'dp')  81.5 us
    psum x2, blocking collectives, on_device(): lax.psum((jnp.sum(onehot.astype(jnp.float32), axis=(0, 1)), head_counts(v...  76.3 us
    unnamed x401, local copies, waits for them, and re-layouts  55.3 us
    gather x1, local copies, waits for them, and re-layouts, on_device(): gates_padded[source][:, None] * residual_padded[token_of]  45.5 us
  transfers between devices with their start and end apart: 10, of which 6 were waited for; matrix products, arithmetic and copies ran while one was open for 19% of the time, Pallas kernels for 0%

commit v1 on v0

v1 whole, which is shorter than its diff:
```python
import functools
import jax
import jax.numpy as jnp
from jax import lax
from jax.experimental import pallas as pl
from jax.experimental.pallas import tpu as pltpu
from jax.sharding import PartitionSpec as P

D = 384
HEAD = 32
ROUTED_EXPERTS = 8
LANES = 128
TILE = 256
SHARD = 24

horizons = (1, 8, 32, 64)
quadratic_cutoff = 2.0
aux_factor = 0.02
clip_limit = 0.001
beta_one = 0.9
beta_two = 0.95
adam_eps = 1e-08
decay_rate = 0.1
matrix_rate = 0.05
vector_rate = 0.25
norm_eps = 1e-06
rope_base = 10000.0

F32 = jnp.float32
BF16 = jnp.bfloat16
MESH = pl.DeviceIdType.MESH
VMEM = pl.BlockSpec(memory_space=pltpu.VMEM)
ANY = pl.BlockSpec(memory_space=pl.ANY)


def dot(a, b, da=1, db=0):
    return lax.dot_general(a, b, (((da,), (db,)), ((), ())), preferred_element_type=F32)


def params(megabytes=60, **more):
    return pltpu.CompilerParams(vmem_limit_bytes=megabytes * 1024 * 1024, **more)


def sigmoid(v):
    return 1.0 / (1.0 + jnp.exp(-v))


def column(row, length):
    return jnp.transpose(jnp.broadcast_to(row, (LANES, length)))


def embed_chunk(xb, gate_row, up_row):
    u = xb * gate_row
    return u * sigmoid(u) * (xb * up_row)


def rotated(t, cos, sin):
    half = HEAD // 2
    front, back = t[:half], t[half:]
    return jnp.concatenate([front * cos - back * sin, back * cos + front * sin], axis=0)


def unrotated(t, cos, sin):
    half = HEAD // 2
    front, back = t[:half], t[half:]
    return jnp.concatenate([front * cos + back * sin, back * cos - front * sin], axis=0)


def score_block(k_rows, q_cols, low, length):
    s = dot(k_rows, q_cols)
    keys = lax.broadcasted_iota(jnp.int32, s.shape, 0)
    queries = lax.broadcasted_iota(jnp.int32, s.shape, 1) + low
    return jnp.where(keys <= queries, s, -1e30)


def attend_forward_kernel(
    x_ref, rows_ref, wj_ref, wo_ref, cos_ref, sin_ref,
    x0_ref, a_ref, qkv_ref, lse_ref, o_ref, part_ref,
):
    length = x_ref.shape[-1]
    heads = wo_ref.shape[0] // HEAD
    width = heads * HEAD
    scale = HEAD ** (-0.5)

    def embed(i, carry):
        r = pl.ds(pl.multiple_of(i * TILE, TILE), TILE)
        xb = column(x_ref[0, :, r], TILE)
        cuts = []
        square = None
        for c in range(D // LANES):
            cols = slice(c * LANES, (c + 1) * LANES)
            v = embed_chunk(xb, rows_ref[1:2, cols], rows_ref[2:3, cols])
            x0_ref[r, cols] = v
            square = v * v if square is None else square + v * v
            cuts.append(v)
        scale_row = lax.rsqrt(jnp.sum(square, axis=1, keepdims=True) / D + norm_eps)
        for c in range(D // LANES):
            cols = slice(c * LANES, (c + 1) * LANES)
            a_ref[r, cols] = (cuts[c] * scale_row * rows_ref[0:1, cols]).astype(BF16)
        return carry

    lax.fori_loop(0, length // TILE, embed, 0)
    a = a_ref[...]
    cos, sin = cos_ref[...], sin_ref[...]

    def project(h, carry):
        for part in range(3):
            rows = pl.ds(pl.multiple_of(part * width + h * HEAD, HEAD), HEAD)
            t = dot(wj_ref[rows, :], a, 1, 1)
            if part < 2:
                t = rotated(t, cos, sin)
            qkv_ref[0, rows, :] = t.astype(BF16)
        return carry

    lax.fori_loop(0, heads, project, 0)

    def head(h, carry):
        q_rows = pl.ds(pl.multiple_of(h * HEAD, HEAD), HEAD)
        k_rows = pl.ds(pl.multiple_of(width + h * HEAD, HEAD), HEAD)
        v_rows = pl.ds(pl.multiple_of(2 * width + h * HEAD, HEAD), HEAD)
        k = jnp.transpose(qkv_ref[0, k_rows, :].astype(F32)).astype(BF16)
        for j in range(length // TILE):
            n = TILE * (j + 1)
            cols = slice(j * TILE, (j + 1) * TILE)
            s = score_block(k[:n], qkv_ref[0, q_rows, cols], j * TILE, n)
            peak = jnp.max(s, axis=0, keepdims=True)
            e = jnp.exp((s - peak) * scale)
            mass = jnp.sum(e, axis=0, keepdims=True)
            weights = (e * (1.0 / mass)).astype(BF16)
            o_ref[0, q_rows, cols] = dot(qkv_ref[0, v_rows, :n], weights).astype(BF16)
            lse_ref[0, pl.ds(h, 1), cols] = peak * scale + jnp.log(mass)
        return carry

    lax.fori_loop(0, heads, head, 0)
    part_ref[...] = dot(o_ref[0], wo_ref[...], 0, 0)


def attend_forward(x, rows, wj, wo, cos, sin):
    series, _, length = x.shape
    tokens = series * length
    width = wo.shape[0]
    full = lambda shape: pl.BlockSpec(shape, lambda i: (0,) * len(shape))
    tok = lambda w: pl.BlockSpec((length, w), lambda i: (i, 0))
    ser = lambda r: pl.BlockSpec((1, r, length), lambda i: (i, 0, 0))
    return pl.pallas_call(
        attend_forward_kernel,
        grid=(series,),
        in_specs=[ser(1), full(rows.shape), full(wj.shape), full(wo.shape), full(cos.shape), full(sin.shape)],
        out_specs=[tok(D), tok(D), ser(3 * width), ser(8), ser(width), tok(D)],
        out_shape=[
            jax.ShapeDtypeStruct((tokens, D), F32),
            jax.ShapeDtypeStruct((tokens, D), BF16),
            jax.ShapeDtypeStruct((series, 3 * width, length), BF16),
            jax.ShapeDtypeStruct((series, 8, length), F32),
            jax.ShapeDtypeStruct((series, width, length), BF16),
            jax.ShapeDtypeStruct((tokens, D), F32),
        ],
        compiler_params=params(),
        name="attend_forward",
    )(x, rows, wj, wo, cos, sin)


def attend_backward_kernel(
    qkv_ref, do_ref, lse_ref, a_ref, wj_ref, cos_ref, sin_ref, dw_ref, part_ref, dqkv_ref, dk_ref, dv_ref
):
    length = qkv_ref.shape[-1]
    width = do_ref.shape[1]
    heads = width // HEAD
    scale = HEAD ** (-0.5)
    cos, sin = cos_ref[...], sin_ref[...]

    def flip(t):
        return jnp.transpose(t.astype(F32)).astype(BF16)

    def head(h, carry):
        q_rows = pl.ds(pl.multiple_of(h * HEAD, HEAD), HEAD)
        k_rows = pl.ds(pl.multiple_of(width + h * HEAD, HEAD), HEAD)
        v_rows = pl.ds(pl.multiple_of(2 * width + h * HEAD, HEAD), HEAD)
        q = flip(qkv_ref[0, q_rows, :])
        k = flip(qkv_ref[0, k_rows, :])
        v = flip(qkv_ref[0, v_rows, :])
        do = flip(do_ref[0, q_rows, :])
        dk_ref[...] = jnp.zeros_like(dk_ref)
        dv_ref[...] = jnp.zeros_like(dv_ref)
        for j in range(length // TILE):
            n = TILE * (j + 1)
            cols = slice(j * TILE, (j + 1) * TILE)
            s = score_block(k[:n], qkv_ref[0, q_rows, cols], j * TILE, n)
            w = jnp.exp(s * scale - lse_ref[0, pl.ds(h, 1), cols])
            dv_ref[:n] += dot(w.astype(BF16), do[cols])
            dw = dot(v[:n], do_ref[0, q_rows, cols])
            mean = jnp.sum(w * dw, axis=0, keepdims=True)
            ds = (w * (dw - mean) * scale).astype(BF16)
            dk_ref[:n] += dot(ds, q[cols])
            dq = dot(qkv_ref[0, k_rows, :n], ds)
            dqkv_ref[q_rows, cols] = unrotated(dq, cos[:, cols], sin[:, cols]).astype(BF16)
        dqkv_ref[k_rows, :] = unrotated(jnp.transpose(dk_ref[...]), cos, sin).astype(BF16)
        dqkv_ref[v_rows, :] = jnp.transpose(dv_ref[...]).astype(BF16)
        return carry

    lax.fori_loop(0, heads, head, 0)

    @pl.when(pl.program_id(0) == 0)
    def _():
        dw_ref[...] = jnp.zeros_like(dw_ref)

    dw_ref[...] += dot(dqkv_ref[...], a_ref[...])
    part_ref[...] = dot(dqkv_ref[...], wj_ref[...], 0, 0)


def attend_backward(qkv, do, lse, a, wj, cos, sin):
    series, rows, length = qkv.shape
    tokens = series * length
    full = lambda shape: pl.BlockSpec(shape, lambda i: (0,) * len(shape))
    tok = lambda w: pl.BlockSpec((length, w), lambda i: (i, 0))
    ser = lambda r: pl.BlockSpec((1, r, length), lambda i: (i, 0, 0))
    return pl.pallas_call(
        attend_backward_kernel,
        grid=(series,),
        in_specs=[ser(rows), ser(do.shape[1]), ser(8), tok(D), full(wj.shape), full(cos.shape), full(sin.shape)],
        out_specs=[full((rows, D)), tok(D)],
        out_shape=[jax.ShapeDtypeStruct((rows, D), F32), jax.ShapeDtypeStruct((tokens, D), F32)],
        scratch_shapes=[
            pltpu.VMEM((rows, length), BF16), pltpu.VMEM((length, HEAD), F32), pltpu.VMEM((length, HEAD), F32),
        ],
        compiler_params=params(),
        name="attend_backward",
    )(qkv, do, lse, a, wj, cos, sin)


GROUP = 16


def spread_rows(dest, value, start, count):
    for c in range(value.shape[1] // LANES):
        dest[pl.ds(start * 8 + c, count, stride=8), :] = value[:, c * LANES:(c + 1) * LANES]


def pick_rows(source, tile, index_ref, base):
    def body(i, carry):
        values = []
        for k in range(GROUP):
            t = index_ref[base + i * GROUP + k]
            values.append(source[pl.ds(pl.multiple_of(t * 8, 8), 8), :])
        for k in range(GROUP):
            tile[pl.ds(pl.multiple_of((i * GROUP + k) * 8, 8), 8), :] = values[k]
        return carry

    lax.fori_loop(0, TILE // GROUP, body, 0)


def add_rows(dest, tile, index_ref, base):
    def body(i, carry):
        places, values = [], []
        for k in range(GROUP):
            t = index_ref[base + i * GROUP + k]
            place = pl.ds(pl.multiple_of(t * 8, 8), 8)
            places.append(place)
            values.append(dest[place, :] + tile[pl.ds(pl.multiple_of((i * GROUP + k) * 8, 8), 8), :])
        for k in range(GROUP):
            dest[places[k], :] = values[k]
        return carry

    lax.fori_loop(0, TILE // GROUP, body, 0)


def gathered_columns(tile, columns):
    return [tile[pl.ds(c, TILE, stride=8), :] for c in range(columns)]


def lane_of(block, lane):
    lanes = lax.broadcasted_iota(jnp.int32, block.shape, 1)
    return jnp.sum(jnp.where(lanes == lane, block, 0.0), axis=1, keepdims=True)


def expert_forward_kernel(
    counts, source, b_ref, pc_ref, w_ref, x_ref, y_ref, ys_ref, mix_ref, rows8, acc8, tile8
):
    e = pl.program_id(0)
    tokens = b_ref.shape[0]
    hidden = w_ref.shape[2] // 3

    @pl.when(e == 0)
    def _():
        def lay(i, carry):
            r = pl.ds(pl.multiple_of(i * TILE, TILE), TILE)
            spread_rows(rows8, b_ref[r, :].astype(F32), i * TILE, TILE)
            rows8[pl.ds(i * TILE * 8 + 3, TILE, stride=8), :] = pc_ref[r, :]
            acc8[pl.ds(pl.multiple_of(i * TILE * 8, 8), TILE * 8), :] = jnp.zeros((TILE * 8, LANES), F32)
            return carry
        lax.fori_loop(0, tokens // TILE, lay, 0)
        rows8[pl.ds(tokens * 8, 8), :] = jnp.zeros((8, LANES), F32)
        acc8[pl.ds(tokens * 8, 8), :] = jnp.zeros((8, LANES), F32)

    def run(x):
        g = dot(x, w_ref[0, :, : 2 * hidden])
        gate, up = g[:, :hidden], g[:, hidden:]
        h = (gate * sigmoid(gate) * up).astype(BF16)
        return dot(h, w_ref[0, :, 2 * hidden:], 1, 1)

    @pl.when(e < ROUTED_EXPERTS)
    def _():
        capacity = y_ref.shape[1]

        def step(i, carry):
            base = e * capacity + i * TILE
            r = pl.ds(pl.multiple_of(i * TILE, TILE), TILE)
            pick_rows(rows8, tile8, source, base)
            c0, c1, c2, pc = gathered_columns(tile8, 4)
            x = jnp.concatenate([c0, c1, c2], axis=1).astype(BF16)
            x_ref[0, r, :] = x
            y = run(x)
            y_ref[0, r, :] = y
            spread_rows(tile8, y * lane_of(pc, e), 0, TILE)
            add_rows(acc8, tile8, source, base)
            return carry

        lax.fori_loop(0, (counts[e] + TILE - 1) // TILE, step, 0)

    @pl.when(e == ROUTED_EXPERTS)
    def _():
        def step(i, carry):
            r = pl.ds(pl.multiple_of(i * TILE, TILE), TILE)
            y = run(b_ref[r, :])
            ys_ref[r, :] = y
            shared = y * lane_of(pc_ref[r, :], ROUTED_EXPERTS)
            for c in range(D // LANES):
                cols = slice(c * LANES, (c + 1) * LANES)
                mix_ref[r, cols] = acc8[pl.ds(i * TILE * 8 + c, TILE, stride=8), :] + shared[:, cols]
            return carry

        lax.fori_loop(0, tokens // TILE, step, 0)


def expert_forward(counts, source, b, pc, weights):
    tokens = b.shape[0]
    capacity = tokens // 2
    last = ROUTED_EXPERTS - 1
    full = lambda shape: pl.BlockSpec(shape, lambda e, *_: (0,) * len(shape))
    exp = lambda w: pl.BlockSpec((1, capacity, w), lambda e, *_: (jnp.minimum(e, last), 0, 0))
    return pl.pallas_call(
        expert_forward_kernel,
        grid_spec=pltpu.PrefetchScalarGridSpec(
            num_scalar_prefetch=2,
            grid=(ROUTED_EXPERTS + 1,),
            in_specs=[full(b.shape), full(pc.shape), pl.BlockSpec((1,) + weights.shape[1:], lambda e, *_: (e, 0, 0))],
            out_specs=[exp(D), exp(D), full((tokens, D)), full((tokens, D))],
            scratch_shapes=[
                pltpu.VMEM(((tokens + 1) * 8, LANES), F32),
                pltpu.VMEM(((tokens + 1) * 8, LANES), F32),
                pltpu.VMEM((TILE * 8, LANES), F32),
            ],
        ),
        out_shape=[
            jax.ShapeDtypeStruct((ROUTED_EXPERTS, capacity, D), BF16),
            jax.ShapeDtypeStruct((ROUTED_EXPERTS, capacity, D), F32),
            jax.ShapeDtypeStruct((tokens, D), F32),
            jax.ShapeDtypeStruct((tokens, D), F32),
        ],
        compiler_params=params(),
        name="expert_forward",
    )(counts, source, b, pc, weights)


def expert_backward_kernel(
    counts, source, b_ref, pc_ref, dx_ref, w_ref, x_ref, y_ref, ys_ref, dw_ref, acc_ref, rows8, acc8, tile8
):
    e = pl.program_id(0)
    tokens = b_ref.shape[0]
    hidden = w_ref.shape[2] // 3

    @pl.when(e == 0)
    def _():
        def lay(i, carry):
            r = pl.ds(pl.multiple_of(i * TILE, TILE), TILE)
            spread_rows(rows8, dx_ref[r, :], i * TILE, TILE)
            rows8[pl.ds(i * TILE * 8 + 3, TILE, stride=8), :] = pc_ref[r, :]
            acc8[pl.ds(pl.multiple_of(i * TILE * 8, 8), TILE * 8), :] = jnp.zeros((TILE * 8, LANES), F32)
            return carry
        lax.fori_loop(0, tokens // TILE, lay, 0)
        rows8[pl.ds(tokens * 8, 8), :] = jnp.zeros((8, LANES), F32)
        acc8[pl.ds(tokens * 8, 8), :] = jnp.zeros((8, LANES), F32)

    dw_ref[...] = jnp.zeros_like(dw_ref)

    def run(x, dy):
        u = w_ref[0, :, : 2 * hidden]
        g = dot(x, u)
        gate, up = g[:, :hidden], g[:, hidden:]
        s = sigmoid(gate)
        silu = gate * s
        h = (silu * up).astype(BF16)
        dh = dot(dy, w_ref[0, :, 2 * hidden:])
        d_up = (dh * silu).astype(BF16)
        d_gate = (dh * up * (s * (1.0 + gate * (1.0 - s)))).astype(BF16)
        dg = jnp.concatenate([d_gate, d_up], axis=1)
        dw_ref[0, :, : 2 * hidden] += dot(x, dg, 0, 0)
        dw_ref[0, :, 2 * hidden:] += dot(dy, h, 0, 0)
        return dot(dg, u, 1, 1)

    @pl.when(e < ROUTED_EXPERTS)
    def _():
        capacity = y_ref.shape[1]

        def step(i, carry):
            base = e * capacity + i * TILE
            r = pl.ds(pl.multiple_of(i * TILE, TILE), TILE)
            pick_rows(rows8, tile8, source, base)
            c0, c1, c2, pc = gathered_columns(tile8, 4)
            dx = jnp.concatenate([c0, c1, c2], axis=1)
            d_gate = jnp.sum(y_ref[0, r, :] * dx, axis=1, keepdims=True)
            dy = (dx * lane_of(pc, e)).astype(BF16)
            back = run(x_ref[0, r, :], dy)
            spread_rows(tile8, back, 0, TILE)
            lanes = lax.broadcasted_iota(jnp.int32, (TILE, LANES), 1)
            tile8[pl.ds(3, TILE, stride=8), :] = jnp.where(lanes == e, d_gate, 0.0)
            add_rows(acc8, tile8, source, base)
            return carry

        lax.fori_loop(0, (counts[e] + TILE - 1) // TILE, step, 0)

    @pl.when(e == ROUTED_EXPERTS)
    def _():
        def step(i, carry):
            r = pl.ds(pl.multiple_of(i * TILE, TILE), TILE)
            dx = dx_ref[r, :]
            d_gate = jnp.sum(ys_ref[r, :] * dx, axis=1, keepdims=True)
            dy = (dx * lane_of(pc_ref[r, :], ROUTED_EXPERTS)).astype(BF16)
            back = run(b_ref[r, :], dy)
            for c in range(D // LANES):
                cols = slice(c * LANES, (c + 1) * LANES)
                acc_ref[r, cols] = acc8[pl.ds(i * TILE * 8 + c, TILE, stride=8), :] + back[:, cols]
            lanes = lax.broadcasted_iota(jnp.int32, (TILE, LANES), 1)
            acc_ref[r, D:] = jnp.where(
                lanes == ROUTED_EXPERTS, d_gate, acc8[pl.ds(i * TILE * 8 + 3, TILE, stride=8), :])
            return carry

        lax.fori_loop(0, tokens // TILE, step, 0)


def expert_backward(counts, source, b, pc, dx, weights, x, y, ys):
    tokens = b.shape[0]
    capacity = tokens // 2
    last = ROUTED_EXPERTS - 1
    once = pl.Buffered(1)
    full = lambda shape: pl.BlockSpec(shape, lambda e, *_: (0,) * len(shape), pipeline_mode=once)
    exp = lambda w: pl.BlockSpec((1, capacity, w), lambda e, *_: (jnp.minimum(e, last), 0, 0))
    wide = pl.BlockSpec((1,) + weights.shape[1:], lambda e, *_: (e, 0, 0))
    return pl.pallas_call(
        expert_backward_kernel,
        grid_spec=pltpu.PrefetchScalarGridSpec(
            num_scalar_prefetch=2,
            grid=(ROUTED_EXPERTS + 1,),
            in_specs=[full(b.shape), full(pc.shape), full(dx.shape), wide, exp(D), exp(D), full(ys.shape)],
            out_specs=[wide, full((tokens, D + LANES))],
            scratch_shapes=[
                pltpu.VMEM(((tokens + 1) * 8, LANES), F32),
                pltpu.VMEM(((tokens + 1) * 8, LANES), F32),
                pltpu.VMEM((TILE * 8, LANES), F32),
            ],
        ),
        out_shape=[
            jax.ShapeDtypeStruct(weights.shape, F32),
            jax.ShapeDtypeStruct((tokens, D + LANES), F32),
        ],
        compiler_params=params(),
        name="expert_backward",
    )(counts, source, b, pc, dx, weights, x, y, ys)


def exchange(part, other, send_sem, recv_sem):
    dp, mp = lax.axis_index("dp"), lax.axis_index("mp")
    barrier = pltpu.get_barrier_semaphore()
    pl.semaphore_signal(barrier, inc=1, device_id=(dp, 1 - mp), device_id_type=MESH)
    pl.semaphore_wait(barrier, 1)

    def copy(i):
        r = pl.ds(pl.multiple_of(i * TILE, TILE), TILE)
        return pltpu.make_async_remote_copy(
            src_ref=part.at[r], dst_ref=other.at[r], send_sem=send_sem.at[i], recv_sem=recv_sem.at[i],
            device_id=(dp, 1 - mp), device_id_type=MESH)

    def begin(i, carry):
        copy(i).start()
        return carry

    lax.fori_loop(0, part.shape[0] // TILE, begin, 0)
    return lambda i: copy(i).wait()


def exchange_scratch(part):
    tiles = part.shape[0] // TILE
    return [pltpu.VMEM(part.shape, F32), pltpu.SemaphoreType.DMA((tiles,)), pltpu.SemaphoreType.DMA((tiles,))]


def mid_forward_kernel(part, x0, gain, router, x1, b, pc, total, other, send_sem, recv_sem):
    wait = exchange(part, other, send_sem, recv_sem)
    total[...] = jnp.zeros_like(total)

    def step(i, carry):
        r = pl.ds(pl.multiple_of(i * TILE, TILE), TILE)
        wait(i)
        x = x0[r, :] + (part[r, :] + other[r, :])
        x1[r, :] = x
        scale = lax.rsqrt(jnp.mean(x * x, axis=1, keepdims=True) + norm_eps)
        low = (x * scale * gain[...]).astype(BF16)
        b[r, :] = low
        logits = dot(low, router[...])
        lanes = lax.broadcasted_iota(jnp.int32, logits.shape, 1)
        routed = lanes < ROUTED_EXPERTS
        peak = jnp.max(jnp.where(routed, logits, -jnp.inf), axis=1, keepdims=True)
        e = jnp.where(routed, jnp.exp(jnp.where(routed, logits - peak, 0.0)), 0.0)
        probability = e / jnp.sum(e, axis=1, keepdims=True)
        pc[r, :] = jnp.where(lanes == ROUTED_EXPERTS, sigmoid(logits), probability)
        total[...] += jnp.sum(probability, axis=0, keepdims=True)
        return carry

    lax.fori_loop(0, part.shape[0] // TILE, step, 0)


def mid_forward(part, x0, gain, router, ident):
    tokens = part.shape[0]
    return pl.pallas_call(
        mid_forward_kernel,
        in_specs=[VMEM] * 4,
        out_specs=[VMEM] * 4,
        out_shape=[
            jax.ShapeDtypeStruct((tokens, D), F32), jax.ShapeDtypeStruct((tokens, D), BF16),
            jax.ShapeDtypeStruct((tokens, LANES), F32), jax.ShapeDtypeStruct((1, LANES), F32),
        ],
        scratch_shapes=exchange_scratch(part),
        compiler_params=params(collective_id=ident, has_side_effects=True),
        name="mid_forward",
    )(part, x0, gain, router)


def hankel(base, shape):
    block = jnp.broadcast_to(base, (LANES, 2 * LANES))
    m = pltpu.roll(block, 0, 1, stride=1, stride_axis=0)[:, :LANES]
    lanes = lax.broadcasted_iota(jnp.int32, (LANES, LANES), 1)
    out = pltpu.roll(m, 41, 1)
    out = jnp.where(lanes < 104, pltpu.roll(m, 40, 1), out)
    out = jnp.where(lanes < 96, pltpu.roll(m, 32, 1), out)
    return jnp.where(lanes < 64, m, out)


def loss_kernel(part, x1, gain, heads, heads_t, values, marks, weight, dx2, d_heads, d_gain, loss,
                other, send_sem, recv_sem):
    wait = exchange(part, other, send_sem, recv_sem)
    d_heads[...] = jnp.zeros_like(d_heads)
    d_gain[...] = jnp.zeros_like(d_gain)
    loss[...] = jnp.zeros_like(loss)

    def step(i, carry):
        r = pl.ds(pl.multiple_of(i * TILE, TILE), TILE)
        wait(i)
        x = x1[r, :] + (part[r, :] + other[r, :])
        scale = lax.rsqrt(jnp.mean(x * x, axis=1, keepdims=True) + norm_eps)
        unit = x * scale
        low = (unit * gain[...]).astype(BF16)
        z = dot(low, heads[...])
        target = jnp.concatenate(
            [hankel(values[pl.ds(2 * i + k, 1), :], None) for k in range(2)], axis=0)
        valid = jnp.concatenate(
            [hankel(marks[pl.ds(2 * i + k, 1), :], None) for k in range(2)], axis=0)
        factor = valid * weight[...]
        miss = z - target
        size = jnp.abs(miss)
        huber = jnp.where(
            size <= quadratic_cutoff, 0.5 * miss * miss, quadratic_cutoff * (size - 0.5 * quadratic_cutoff))
        loss[...] += jnp.sum(huber * factor, axis=0, keepdims=True)
        dz = (jnp.clip(miss, -quadratic_cutoff, quadratic_cutoff) * factor).astype(BF16)
        d_heads[...] += dot(dz, low, 0, 0)
        df = dot(dz, heads_t[...])
        d_gain[...] += jnp.sum(df * unit, axis=0, keepdims=True)
        dn = df * gain[...]
        dx2[r, :] = scale * (dn - unit * jnp.mean(dn * unit, axis=1, keepdims=True))
        return carry

    lax.fori_loop(0, part.shape[0] // TILE, step, 0)


def loss_stage(part, x1, gain, heads, heads_t, values, marks, weight, ident):
    tokens = part.shape[0]
    return pl.pallas_call(
        loss_kernel,
        in_specs=[VMEM] * 8,
        out_specs=[VMEM] * 4,
        out_shape=[
            jax.ShapeDtypeStruct((tokens, D), F32), jax.ShapeDtypeStruct((LANES, D), F32),
            jax.ShapeDtypeStruct((1, D), F32), jax.ShapeDtypeStruct((1, LANES), F32),
        ],
        scratch_shapes=exchange_scratch(part),
        compiler_params=params(collective_id=ident, has_side_effects=True),
        name="loss_stage",
    )(part, x1, gain, heads, heads_t, values, marks, weight)


def mid_backward_kernel(part, dx2, x1, b, pc, gain, router_t, balance, wo, o, dx1, do, d_router, d_wo, d_gain,
                        other, send_sem, recv_sem):
    wait = exchange(part, other, send_sem, recv_sem)
    d_router[...] = jnp.zeros_like(d_router)
    d_wo[...] = jnp.zeros_like(d_wo)
    d_gain[...] = jnp.zeros_like(d_gain)
    per = o.shape[2] // TILE

    def step(i, carry):
        r = pl.ds(pl.multiple_of(i * TILE, TILE), TILE)
        wait(i)
        dp = part[r, D:] + other[r, D:] + balance[...]
        p = pc[r, :]
        lanes = lax.broadcasted_iota(jnp.int32, p.shape, 1)
        routed = lanes < ROUTED_EXPERTS
        weighted = jnp.sum(jnp.where(routed, p * dp, 0.0), axis=1, keepdims=True)
        dl = jnp.where(routed, p * (dp - weighted), jnp.where(lanes == ROUTED_EXPERTS, dp * p * (1.0 - p), 0.0))
        dl = dl.astype(BF16)
        low = b[r, :]
        d_router[...] += dot(dl, low, 0, 0)
        db = part[r, :D] + other[r, :D] + dot(dl, router_t[...])
        x = x1[r, :]
        scale = lax.rsqrt(jnp.mean(x * x, axis=1, keepdims=True) + norm_eps)
        unit = x * scale
        d_gain[...] += jnp.sum(db * unit, axis=0, keepdims=True)
        dn = db * gain[...]
        dx = dx2[r, :] + scale * (dn - unit * jnp.mean(dn * unit, axis=1, keepdims=True))
        dx1[r, :] = dx
        d_low = dx.astype(BF16)
        n, cols = i // per, pl.ds(pl.multiple_of(lax.rem(i, per) * TILE, TILE), TILE)
        do[n, :, cols] = dot(wo[...], d_low, 1, 1).astype(BF16)
        d_wo[...] += dot(o[n, :, cols], d_low)
        return carry

    lax.fori_loop(0, part.shape[0] // TILE, step, 0)


def mid_backward(part, dx2, x1, b, pc, gain, router_t, balance, wo, o, ident):
    tokens = part.shape[0]
    return pl.pallas_call(
        mid_backward_kernel,
        in_specs=[VMEM] * 10,
        out_specs=[VMEM] * 5,
        out_shape=[
            jax.ShapeDtypeStruct((tokens, D), F32), jax.ShapeDtypeStruct(o.shape, BF16),
            jax.ShapeDtypeStruct((LANES, D), F32), jax.ShapeDtypeStruct(wo.shape, F32),
            jax.ShapeDtypeStruct((1, D), F32),
        ],
        scratch_shapes=exchange_scratch(part),
        compiler_params=params(collective_id=ident, has_side_effects=True),
        name="mid_backward",
    )(part, dx2, x1, b, pc, gain, router_t, balance, wo, o)


def embed_backward_kernel(part, dx1, x_ref, rows_ref, sums, other, send_sem, recv_sem):
    wait = exchange(part, other, send_sem, recv_sem)
    sums[...] = jnp.zeros_like(sums)
    per = x_ref.shape[2] // TILE

    def step(i, carry):
        r = pl.ds(pl.multiple_of(i * TILE, TILE), TILE)
        wait(i)
        n, cols = i // per, pl.ds(pl.multiple_of(lax.rem(i, per) * TILE, TILE), TILE)
        xb = column(x_ref[n, :, cols], TILE)
        xb = jnp.concatenate([xb] * (D // LANES), axis=1)
        u = xb * rows_ref[1:2, :]
        up = xb * rows_ref[2:3, :]
        s = sigmoid(u)
        silu = u * s
        x = silu * up
        scale = lax.rsqrt(jnp.mean(x * x, axis=1, keepdims=True) + norm_eps)
        unit = x * scale
        da = part[r, :] + other[r, :]
        sums[0:1, :] += jnp.sum(da * unit, axis=0, keepdims=True)
        dn = da * rows_ref[0:1, :]
        dx = dx1[r, :] + scale * (dn - unit * jnp.mean(dn * unit, axis=1, keepdims=True))
        du = dx * up * (s * (1.0 + u * (1.0 - s)))
        sums[1:2, :] += jnp.sum(du * xb, axis=0, keepdims=True)
        sums[2:3, :] += jnp.sum(dx * silu * xb, axis=0, keepdims=True)
        return carry

    lax.fori_loop(0, part.shape[0] // TILE, step, 0)


def embed_backward(part, dx1, x, rows, ident):
    return pl.pallas_call(
        embed_backward_kernel,
        in_specs=[VMEM] * 4,
        out_specs=VMEM,
        out_shape=jax.ShapeDtypeStruct((8, D), F32),
        scratch_shapes=exchange_scratch(part),
        compiler_params=params(collective_id=ident, has_side_effects=True),
        name="embed_backward",
    )(part, dx1, x, rows)
def place():
    dp = lax.axis_index("dp")
    return dp, lax.axis_index("mp"), lax.rem(dp, 2), lax.rem(dp // 2, 2), dp // 4


def greet(dp, mp, x, y, z):
    barrier = pltpu.get_barrier_semaphore()
    xp, yp = dp + 1 - 2 * x, dp + 2 - 4 * y
    for peer in (xp, yp):
        pl.semaphore_signal(barrier, inc=1, device_id=(peer, mp), device_id_type=MESH)

    @pl.when(z > 0)
    def _():
        pl.semaphore_signal(barrier, inc=1, device_id=(dp - 4, mp), device_id_type=MESH)

    @pl.when(z < 3)
    def _():
        pl.semaphore_signal(barrier, inc=1, device_id=(dp + 4, mp), device_id_type=MESH)

    @pl.when((z > 0) & (z < 3))
    def _():
        pl.semaphore_wait(barrier, 4)

    @pl.when((z == 0) | (z == 3))
    def _():
        pl.semaphore_wait(barrier, 3)
    return xp, yp


def gather_kernel(chunks, own, out, stage, in_sem, own_sem, send_xy, send_up, send_dn, z_sem, p2_sem, p3_sem):
    dp, mp, x, y, z = place()
    count = own.shape[0]
    load = pltpu.make_async_copy(own, stage, in_sem)
    load.start()
    xp, yp = greet(dp, mp, x, y, z)
    load.wait()

    def rows(c, slot):
        return out.at[c, pl.ds(pl.multiple_of(slot * SHARD, 8), SHARD), :]

    store = []

    def put(src, c, slot, send, recv, peer):
        pltpu.make_async_remote_copy(
            src_ref=src, dst_ref=rows(c, slot), send_sem=send, recv_sem=recv,
            device_id=(peer, mp), device_id_type=MESH).start()

    def arrived(c, slot, sem):
        pltpu.make_async_copy(rows(c, slot), rows(c, slot), sem).wait()

    def local(c):
        return pltpu.make_async_copy(stage.at[c], rows(c, dp), own_sem)

    first = (lambda k: (yp, xp) if k == 0 else (xp, yp))

    def each(fn):
        def body(i, carry):
            fn(2 * i, 0)
            fn(2 * i + 1, 1)
            return carry
        lax.fori_loop(0, count // 2, body, 0)
        if count % 2:
            fn(count - 1, 0)

    def zup(c, zs, src):
        put(src, c, zs * 4 + 2 * y + x, send_up, z_sem.at[c, zs], dp + 4)

    def zdn(c, zs, src):
        put(src, c, zs * 4 + 2 * y + x, send_dn, z_sem.at[c, zs], dp - 4)

    def spread(c, k, zs, src):
        a, b = first(k)
        slot = zs * 4 + 2 * y + x
        put(src, c, slot, send_xy, p2_sem.at[c, zs], a)
        put(src, c, slot, send_xy, p3_sem, b)

    def begin(c, k):
        @pl.when(z < 3)
        def _():
            zup(c, z, stage.at[c])

        @pl.when(z > 0)
        def _():
            zdn(c, z, stage.at[c])
        spread(c, k, z, stage.at[c])
        local(c).start()
    each(begin)

    def second(c, k, zs):
        a, b = first(k)
        slot = zs * 4 + (2 * (1 - y) + x if k == 0 else 2 * y + 1 - x)
        arrived(c, slot, p2_sem.at[c, zs])
        put(rows(c, slot), c, slot, send_xy, p3_sem, b)

    for dist in (1, 2, 3):
        def step(c, k, dist=dist):
            @pl.when(z >= dist)
            def _():
                zs = z - dist
                arrived(c, zs * 4 + 2 * y + x, z_sem.at[c, zs])
                src = rows(c, zs * 4 + 2 * y + x)

                @pl.when(z < 3)
                def _():
                    zup(c, zs, src)
                spread(c, k, zs, src)

            @pl.when(z + dist <= 3)
            def _():
                zs = z + dist
                arrived(c, zs * 4 + 2 * y + x, z_sem.at[c, zs])
                src = rows(c, zs * 4 + 2 * y + x)

                @pl.when(z > 0)
                def _():
                    zdn(c, zs, src)
                spread(c, k, zs, src)
            if dist == 1:
                second(c, k, z)
            else:
                @pl.when(z >= dist - 1)
                def _():
                    second(c, k, z - dist + 1)

                @pl.when(z + dist - 1 <= 3)
                def _():
                    second(c, k, z + dist - 1)
        each(step)

    def last(c, k):
        @pl.when(z >= 3)
        def _():
            second(c, k, z - 3)

        @pl.when(z <= 0)
        def _():
            second(c, k, z + 3)
    each(last)

    def total(n, sem):
        view = out.at[:, pl.ds(0, n * SHARD), :]
        pltpu.make_async_copy(view, view, sem).wait()
    total(8, p3_sem)
    total(12, send_xy)
    total(1, own_sem)
    for k in range(4):
        @pl.when(z == k)
        def _():
            if k < 3:
                total(k + 1, send_up)
            if k > 0:
                total(4 - k, send_dn)


def gather_rows(own, ident):
    chunks, shard, columns = own.shape
    return pl.pallas_call(
        functools.partial(gather_kernel, chunks),
        out_shape=jax.ShapeDtypeStruct((chunks, 16 * shard, columns), own.dtype),
        in_specs=[pl.BlockSpec(memory_space=pl.ANY)],
        out_specs=pl.BlockSpec(memory_space=pl.ANY),
        scratch_shapes=[
            pltpu.VMEM(own.shape, own.dtype),
            pltpu.SemaphoreType.DMA, pltpu.SemaphoreType.DMA, pltpu.SemaphoreType.DMA,
            pltpu.SemaphoreType.DMA, pltpu.SemaphoreType.DMA,
            pltpu.SemaphoreType.DMA((chunks, 4)), pltpu.SemaphoreType.DMA((chunks, 4)),
            pltpu.SemaphoreType.DMA,
        ],
        compiler_params=pltpu.CompilerParams(collective_id=ident, has_side_effects=True),
        name="gather_rows",
    )(own)


def reduce_kernel(count, halves, *refs):
    (g, out, first, mine, second, up, dn, send1, send2, send_up, send_dn, load_sem,
     sem1, sem2, up_sem, dn_sem) = refs
    dp, mp, x, y, z = place()
    width = out.shape[-1] // halves
    xp, yp = greet(dp, mp, x, y, z)

    def cut(c, k, which):
        e, h = c // halves, lax.rem(c, halves)
        cols = pl.ds(pl.multiple_of(h * width, 128), width)
        if k == 0:
            return g.at[e, :, :, which, :, cols]
        return g.at[e, :, which, :, :, cols]

    def remote(src, dst, send, recv, peer):
        return pltpu.make_async_remote_copy(
            src_ref=src, dst_ref=dst, send_sem=send, recv_sem=recv,
            device_id=(peer, mp), device_id_type=MESH)

    def arrived(view, sem):
        pltpu.make_async_copy(view, view, sem).wait()

    def each(fn):
        def body(i, carry):
            fn(2 * i, 0)
            fn(2 * i + 1, 1)
            return carry
        lax.fori_loop(0, count // 2, body, 0)
        if count % 2:
            fn(count - 1, 0)

    def keep(k):
        return x if k == 0 else y

    def load(c, k, slot):
        return pltpu.make_async_copy(cut(c, k, keep(k)), mine.at[slot], load_sem.at[slot])

    def begin(c, k):
        peer = xp if k == 0 else yp
        remote(cut(c, k, 1 - keep(k)), first.at[c], send1, sem1.at[c], peer).start()
    each(begin)
    load(0, 0, 0).start()
    if count > 1:
        load(1, 1, 1).start()

    def fold(c, k):
        load(c, k, k).wait()
        arrived(first.at[c], sem1.at[c])

        def add(i, carry):
            a, b = i // 2, lax.rem(i, 2)
            first[c, a, b] = first[c, a, b] + mine[k, a, b]
            return carry
        lax.fori_loop(0, 8, add, 0)

        @pl.when(c + 2 < count)
        def _():
            load(c + 2, k, k).start()
        peer = yp if k == 0 else xp
        other = y if k == 0 else x
        remote(first.at[c, :, 1 - other], second.at[c], send2, sem2.at[c], peer).start()
    each(fold)

    def line(c, k):
        other = y if k == 0 else x
        arrived(second.at[c], sem2.at[c])

        def add(a, carry):
            second[c, a] = second[c, a] + first[c, a, other]
            return carry
        lax.fori_loop(0, 4, add, 0)
        for t in (3, 2, 1):
            @pl.when((z < t) & (z == 0))
            def _():
                remote(second.at[c, t], up.at[c, t - 1], send_up, up_sem.at[c, t - 1], dp + 4).start()

            @pl.when((z < t) & (z > 0))
            def _():
                arrived(up.at[c, t - 1], up_sem.at[c, t - 1])
                second[c, t] = second[c, t] + up[c, t - 1]
                remote(second.at[c, t], up.at[c, t - 1], send_up, up_sem.at[c, t - 1], dp + 4).start()
        for t in (0, 1, 2):
            @pl.when((z > t) & (z == 3))
            def _():
                remote(second.at[c, t], dn.at[c, t], send_dn, dn_sem.at[c, t], dp - 4).start()

            @pl.when((z > t) & (z < 3))
            def _():
                arrived(dn.at[c, t], dn_sem.at[c, t])
                second[c, t] = second[c, t] + dn[c, t]
                remote(second.at[c, t], dn.at[c, t], send_dn, dn_sem.at[c, t], dp - 4).start()
    each(line)

    def finish(c, k):
        e, h = c // halves, lax.rem(c, halves)
        cols = pl.ds(pl.multiple_of(h * width, 128), width)
        out[e, :, cols] = second[c, z]
        for t in range(4):
            @pl.when(z == t)
            def _():
                if t > 0:
                    arrived(up.at[c, t - 1], up_sem.at[c, t - 1])
                    out[e, :, cols] = out[e, :, cols] + up[c, t - 1]
                if t < 3:
                    arrived(dn.at[c, t], dn_sem.at[c, t])
                    out[e, :, cols] = out[e, :, cols] + dn[c, t]
    each(finish)

    def total(ref, sem):
        pltpu.make_async_copy(ref, ref, sem).wait()
    total(first, send1)
    total(second, send2)
    for k in range(4):
        @pl.when(z == k)
        def _():
            if k < 3:
                total(up.at[:, pl.ds(k, 3 - k)], send_up)
            if k > 0:
                total(dn.at[:, pl.ds(0, k)], send_dn)


def reduce_rows(g, halves, ident):
    chunks, rows, columns = g.shape
    shard = rows // 16
    count, width = chunks * halves, columns // halves
    f32 = jnp.float32
    return pl.pallas_call(
        functools.partial(reduce_kernel, count, halves),
        out_shape=jax.ShapeDtypeStruct((chunks, shard, columns), f32),
        in_specs=[pl.BlockSpec(memory_space=pl.ANY)],
        out_specs=pl.BlockSpec(memory_space=pltpu.VMEM),
        scratch_shapes=[
            pltpu.VMEM((count, 4, 2, shard, width), f32),
            pltpu.VMEM((2, 4, 2, shard, width), f32),
            pltpu.VMEM((count, 4, shard, width), f32),
            pltpu.VMEM((count, 3, shard, width), f32),
            pltpu.VMEM((count, 3, shard, width), f32),
            pltpu.SemaphoreType.DMA, pltpu.SemaphoreType.DMA, pltpu.SemaphoreType.DMA, pltpu.SemaphoreType.DMA,
            pltpu.SemaphoreType.DMA((2,)),
            pltpu.SemaphoreType.DMA((count,)), pltpu.SemaphoreType.DMA((count,)),
            pltpu.SemaphoreType.DMA((count, 3)), pltpu.SemaphoreType.DMA((count, 3)),
        ],
        compiler_params=pltpu.CompilerParams(
            collective_id=ident, has_side_effects=True, vmem_limit_bytes=60 * 1024 * 1024),
        name="reduce_rows",
    )(g.reshape(chunks, 4, 2, 2, shard, columns))


def all_kernel(n_dp, value, out, send_sem, recv_sem):
    dp, mp = lax.axis_index("dp"), lax.axis_index("mp")
    me = dp * 2 + mp
    n = 2 * n_dp
    barrier = pltpu.get_barrier_semaphore()
    for k in range(1, n):
        peer = lax.rem(me + k, n)
        pl.semaphore_signal(barrier, inc=1, device_id=(peer // 2, lax.rem(peer, 2)), device_id_type=MESH)
    pl.semaphore_wait(barrier, n - 1)
    for k in range(1, n):
        peer = lax.rem(me + k, n)
        pltpu.make_async_remote_copy(src_ref=value, dst_ref=out.at[me], send_sem=send_sem, recv_sem=recv_sem,
                                     device_id=(peer // 2, lax.rem(peer, 2)), device_id_type=MESH).start()
    out[me] = value[...]
    view = out.at[pl.ds(0, n - 1)]
    pltpu.make_async_copy(view, view, recv_sem).wait()
    pltpu.make_async_copy(view, view, send_sem).wait()


def all_blocks(value, n_dp, ident):
    n = 2 * n_dp
    return pl.pallas_call(
        functools.partial(all_kernel, n_dp),
        out_shape=jax.ShapeDtypeStruct((n,) + value.shape, value.dtype),
        in_specs=[pl.BlockSpec(memory_space=pltpu.VMEM)],
        out_specs=pl.BlockSpec(memory_space=pltpu.VMEM),
        scratch_shapes=[pltpu.SemaphoreType.DMA, pltpu.SemaphoreType.DMA],
        compiler_params=pltpu.CompilerParams(collective_id=ident, has_side_effects=True),
        name="all_blocks",
    )(value)


def rope_tables(length):
    halfway = HEAD // 2
    frequency = rope_base ** (-2.0 * jnp.arange(halfway, dtype=F32) / HEAD)
    angles = frequency[:, None] * jnp.arange(length, dtype=F32)[None, :]
    return jnp.cos(angles), jnp.sin(angles)


def hankel_rows(track):
    series, length = track.shape
    padded = jnp.pad(track, ((0, 0), (63, 2 * LANES)))
    first = padded[:, :length].reshape(-1, LANES)[:, ::-1]
    second = padded[:, LANES:LANES + length].reshape(-1, LANES)[:, ::-1]
    return jnp.concatenate([first, second], axis=1)


def head_columns(matrix):
    parts, end = [], matrix.shape[1]
    for horizon in horizons[::-1]:
        parts.append(matrix[:, end - horizon:end][:, ::-1])
        end -= horizon
    return jnp.pad(jnp.concatenate(parts, axis=1), ((0, 0), (0, LANES - matrix.shape[1])))


def head_columns_back(matrix):
    parts, begin = [], 0
    for horizon in horizons[::-1]:
        parts.append(matrix[:, begin:begin + horizon][:, ::-1])
        begin += horizon
    return jnp.concatenate(parts[::-1], axis=1)


def dispatch(route_rows, capacity):
    tokens = route_rows.shape[0]
    experts = jnp.arange(ROUTED_EXPERTS, dtype=jnp.int32)
    member = jnp.any(route_rows[:, :, None] == experts[None, None, :], axis=1)
    count = jnp.cumsum(member.astype(jnp.int32), axis=0)
    total = count[-1]
    place = jnp.where(member, count - 1, -1)
    high = (place[:, :, None] // LANES == jnp.arange(capacity // LANES)[None, None, :]) & member[:, :, None]
    low = (place[:, :, None] % LANES == jnp.arange(LANES)[None, None, :]).astype(BF16)
    token = jnp.arange(tokens, dtype=jnp.int32)
    left = jnp.concatenate(
        [jnp.where(high, part[:, None, None], 0).astype(BF16) for part in (token // 16, token % 16)], axis=2)
    found = jnp.einsum("teh,tel->ehl", left, low, preferred_element_type=F32)
    half = capacity // LANES
    source = (found[:, :half] * 16.0 + found[:, half:]).reshape(ROUTED_EXPERTS, capacity).astype(jnp.int32)
    slots = jnp.arange(capacity, dtype=jnp.int32)
    source = jnp.where(slots[None, :] < total[:, None], source, tokens)
    return total, source.reshape(-1)


def adam_update(master, moment, square, gradient, factor, bias_one, bias_two, step_rate):
    clipped = gradient * factor
    new_moment = beta_one * moment + (1.0 - beta_one) * clipped
    new_square = beta_two * square + (1.0 - beta_two) * clipped * clipped
    updated = master - step_rate * (
        new_moment / bias_one / (jnp.sqrt(new_square / bias_two) + adam_eps) + decay_rate * master
    )
    return (updated, new_moment, new_square)


def on_device(
    near,
    series, observed, routes, step_count,
    joint_proj, joint_moment, joint_square,
    mixer_proj, mixer_moment, mixer_square,
    upward_proj, upward_moment, upward_square,
    downward_proj, downward_moment, downward_square,
    readout, readout_moment, readout_square,
    vectors, vectors_moment, vectors_square,
):
    dp_count = lax.axis_size("dp")
    mp_count = lax.axis_size("mp")
    shard = joint_proj.shape[1]
    width = joint_proj.shape[2]
    hidden = upward_proj.shape[3]
    experts = upward_proj.shape[0]
    series_count, length = series.shape
    tokens = series_count * length
    capacity = tokens // 2
    columns = readout.shape[1]
    small_width = -(-(4 * width + columns + 5) // LANES) * LANES

    def pack_small(joint, mixer_t, read, vec):
        flat = jnp.concatenate([joint[0], joint[1], joint[2], mixer_t, read, vec], axis=1)
        return jnp.pad(flat, ((0, 0), (0, small_width - flat.shape[1])))

    small_own = pack_small(
        joint_proj.astype(BF16), mixer_proj.T.astype(BF16), readout.astype(BF16), vectors.T.astype(BF16))
    big_own = jnp.concatenate(
        [upward_proj.astype(BF16).reshape(experts, shard, 2 * hidden), downward_proj.transpose(0, 2, 1).astype(BF16)],
        axis=2)
    marks = observed.astype(F32)
    route_rows = routes.reshape(tokens, 2)
    expert_here, source = dispatch(route_rows, capacity)
    point = jnp.arange(length, dtype=F32)
    head_here = jnp.stack(
        [jnp.sum(jnp.sum(marks, axis=0) * jnp.minimum(point, float(horizon))) for horizon in horizons])
    tally = jnp.pad(jnp.concatenate([expert_here.astype(F32), head_here]), (0, LANES - 12))
    if near:
        small = gather_rows(small_own[None], 0)[0]
        big = gather_rows(big_own, 1)
        tally = jnp.sum(all_blocks(jnp.broadcast_to(tally[None], (8, LANES)), dp_count, 2)[:, 0], axis=0) / mp_count
    else:
        small = lax.all_gather(small_own, "dp", axis=0, tiled=True)
        big = lax.all_gather(big_own, "dp", axis=1, tiled=True)
        tally = lax.psum(tally, "dp")
    expert_count, head_count = tally[:ROUTED_EXPERTS], tally[ROUTED_EXPERTS:ROUTED_EXPERTS + 4]
    total_tokens = tokens * dp_count

    wj = small[:, :3 * width].T
    wo = small[:, 3 * width:4 * width].T
    read = small[:, 4 * width:4 * width + columns]
    vec = small[:, 4 * width + columns:4 * width + columns + 5].astype(F32).T
    rows = jnp.concatenate([vec[0:1], vec[3:5], jnp.zeros((5, D), F32)], axis=0)
    router = jnp.pad(read[:, :ROUTED_EXPERTS + 1], ((0, 0), (0, LANES - ROUTED_EXPERTS - 1)))
    heads = head_columns(read[:, ROUTED_EXPERTS + 1:])
    cos, sin = rope_tables(length)
    x = (series * marks).reshape(series_count, 1, length)

    x0, a, qkv, lse, o, part = attend_forward(x, rows, wj, wo, cos, sin)
    x1, b, pc, pr_total = mid_forward(part, x0, vec[1:2], router, 3)
    xs, ys, shared, mixed = expert_forward(expert_here, source, b, pc, big)
    head_weight = jnp.concatenate(
        [jnp.zeros((horizon,), F32) + 0.25 / head_count[3 - index] for index, horizon in enumerate(horizons[::-1])])
    head_weight = jnp.pad(head_weight, (0, LANES - head_weight.shape[0]))[None]
    dx2, d_heads, d_gain3, fit = loss_stage(
        mixed, x1, vec[2:3], heads, heads.T, hankel_rows(series), hankel_rows(marks), head_weight, 4)
    d_big, back = expert_backward(expert_here, source, b, pc, dx2, big, xs, ys, shared)
    balance = aux_factor * ROUTED_EXPERTS * expert_count / total_tokens / total_tokens
    balance = jnp.pad(balance, (0, LANES - ROUTED_EXPERTS))[None]
    local_loss = jnp.sum(fit) + jnp.sum(pr_total * balance)
    dx1, do, d_router, d_wo, d_gain2 = mid_backward(
        back, dx2, x1, b, pc, vec[1:2], router.T, balance, wo, o, 5)
    d_wj, da = attend_backward(qkv, do, lse, a, wj, cos, sin)
    sums = embed_backward(da, dx1, x, rows, 6)

    d_read = jnp.concatenate([d_router[:ROUTED_EXPERTS + 1].T, head_columns_back(d_heads.T)], axis=1)
    d_vec = jnp.concatenate([sums[0:1], d_gain2, d_gain3, sums[1:3]], axis=0).T
    d_wj = d_wj.T
    d_small = pack_small(
        [d_wj[:, k * width:(k + 1) * width] for k in range(3)], d_wo.T, d_read, d_vec)
    if near:
        big_red = reduce_rows(d_big, 2, 7)
        small_red = reduce_rows(d_small[None], 1, 8)[0]
    else:
        big_red = lax.psum_scatter(d_big, "dp", scatter_dimension=1, tiled=True)
        small_red = lax.psum_scatter(d_small, "dp", scatter_dimension=0, tiled=True)
    attn_red = small_red[:, :4 * width]
    rest_red = small_red[:, 4 * width:4 * width + columns + 5]
    squares = (
        jnp.sum(big_red * big_red) + jnp.sum(attn_red * attn_red) + jnp.sum(rest_red * rest_red) / mp_count
    )
    pair = jnp.pad(jnp.stack([squares, local_loss / mp_count]), (0, LANES - 2))
    if near:
        pair = jnp.sum(all_blocks(jnp.broadcast_to(pair[None], (8, LANES)), dp_count, 9)[:, 0], axis=0)
    else:
        pair = lax.psum(pair, ("dp", "mp"))
    grad_norm, loss_total = jnp.sqrt(pair[0]), pair[1]

    factor = clip_limit / (grad_norm + 1e-06)
    steps_taken = step_count[0].astype(F32)
    bias_one = 1.0 - beta_one**steps_taken
    bias_two = 1.0 - beta_two**steps_taken

    def update(master, moment, square, gradient, rate=matrix_rate):
        return adam_update(master, moment, square, gradient, factor, bias_one, bias_two, rate)

    joint_red = jnp.stack([attn_red[:, k * width:(k + 1) * width] for k in range(3)], axis=0)
    mixer_red = attn_red[:, 3 * width:].T
    upward_red = big_red[:, :, :2 * hidden].reshape(upward_proj.shape)
    downward_red = big_red[:, :, 2 * hidden:].transpose(0, 2, 1)
    return (
        loss_total,
        grad_norm,
        *update(joint_proj, joint_moment, joint_square, joint_red),
        *update(mixer_proj, mixer_moment, mixer_square, mixer_red),
        *update(upward_proj, upward_moment, upward_square, upward_red),
        *update(downward_proj, downward_moment, downward_square, downward_red),
        *update(readout, readout_moment, readout_square, rest_red[:, :columns]),
        *update(vectors, vectors_moment, vectors_square, rest_red[:, columns:].T, vector_rate),
    )


def solution(mesh):
    token = [P("dp", None), P("dp", None), P("dp", None, None), P()]
    weights = [
        P(None, "dp", "mp"), P("mp", "dp"), P(None, "dp", None, "mp"), P(None, "mp", "dp"), P("dp", None), P(None, "dp"),
    ]
    triple = tuple(spec for spec in weights for _ in range(3))
    near = mesh.shape["dp"] == 16 and mesh.shape["mp"] == 2
    return jax.shard_map(
        functools.partial(on_device, near),
        mesh=mesh,
        in_specs=tuple(token) + triple,
        out_specs=(P(), P()) + triple,
        check_vma=False,
    )
```

time: 2260 us -> 903 us (0.40)
  Pallas kernels: 0 us -> 828 us
  waiting for transfers between devices: 657 us -> 0 us
  matrix products: 556 us -> 3.7 us
  blocking collectives: 361 us -> 0 us
  local copies, waits for them, and re-layouts: 367 us -> 25.8 us
  other arithmetic: 239 us -> 33.5 us
  between operations: 69.7 us -> 9.92 us
    pallas_call x0 -> x14, Pallas kernels: none -> 828 us  [the longest x2 381 us: reduce_rows(): pl.pallas_call(functools.partial(reduce_kernel, count, halves), out_shape...]
    dot_general x52 -> x1, matrix products: 556 us -> 3.7 us  [dispatch(): found = jnp.einsum('teh,tel->ehl', left, low, preferred_element_type=F32)]
    unnamed x12 -> x0, waiting for transfers between devices: 400 us -> none
    psum x5 -> x0, blocking collectives: 204 us -> none  [the longest x1 81.5 us: on_device(): loss_total = lax.psum(local_loss, 'dp')]
    reduce_scatter x2 -> x0, waiting for transfers between devices: 200 us -> none  [the longest x1 200 us: on_device(): lax.psum_scatter(downward_grad, 'dp', scatter_dimension=2, tiled=True)]
    all_gather x4 -> x0, blocking collectives: 158 us -> none  [the longest x1 42.6 us: on_device(): lax.all_gather(vectors.astype(jnp.bfloat16), 'dp', axis=1, tiled=True)]
    gather x5 -> x0, local copies, waits for them, and re-layouts: 154 us -> none  [the longest x1 45.5 us: on_device(): gates_padded[source][:, None] * residual_padded[token_of]]
    reduce_sum x33 -> x9, other arithmetic: 153 us -> 9.91 us  [the longest x1 2.67 us: on_device(): jnp.sum(big_red * big_red) + jnp.sum(attn_red * attn_red)]
  transfers between devices with their start and end apart: 10 -> 0, of which waited for: 6 -> 0; matrix products, arithmetic and copies ran while one was open for 19% -> 0% of each run, Pallas kernels for 0% -> 0%
where the time goes in v1:
time: 903 us; the launch traced here: 901 us
  Pallas kernels  828 us (92%)
  other arithmetic  33.5 us (4%)
  local copies, waits for them, and re-layouts  25.8 us (3%)
  between operations  9.92 us (1%)
    pallas_call x2, Pallas kernels, reduce_rows(): pl.pallas_call(functools.partial(reduce_kernel, count, halves), out_shape...  381 us
    pallas_call x2, Pallas kernels, gather_rows(): pl.pallas_call(functools.partial(gather_kernel, chunks), out_shape=jax.Sh...  158 us
    pallas_call x1, Pallas kernels, expert_backward(): pl.pallas_call(expert_backward_kernel, grid_spec=pltpu.PrefetchScalarGrid...  83.1 us
    pallas_call x1, Pallas kernels, expert_forward(): pl.pallas_call(expert_forward_kernel, grid_spec=pltpu.PrefetchScalarGridS...  47.7 us
    pallas_call x1, Pallas kernels, attend_backward(): pl.pallas_call(attend_backward_kernel, grid=(series,), in_specs=[ser(rows...  44.9 us
    pallas_call x1, Pallas kernels, attend_forward(): pl.pallas_call(attend_forward_kernel, grid=(series,), in_specs=[ser(1), f...  43.3 us
    pallas_call x2, Pallas kernels, all_blocks(): pl.pallas_call(functools.partial(all_kernel, n_dp), out_shape=jax.ShapeDt...  19.8 us

profile of v1, /device:TPU:0, one launch (start us, length us, event | category | flops | bytes accessed | tf_op | source)
XLA Modules:
  0.0 901.1 jit_solution(8916708170050445816)
XLA Ops:
  0.7 0.7 fusion.13
  1.4 2.3 reduce-window.6
  4.8 3.7 fusion
  8.6 0.6 fusion.24.source
  9.3 0.6 reshape.161.x_ref
  10.2 0.6 pad_bitcast_fusion.own
  10.9 21.5 %gather_rows.2 = bf16[1,384,896]{2,1,0:T(8,128)(2,1)} custom-call(bf16[1,24,896]{2,1,0:T(8,128)(2,1)} %pad_bitcast_fusion.own), custom_call_target="tpu_custom_call" | custom-call | tf_op jit(solution)/shard_map/gather_rows/pallas_call | solution.py:849
  32.4 1.4 copy.105
  33.8 0.6 fusion.49
  34.5 0.7 maximum_maximum_fusion.rows_ref
  35.2 0.8 slice_bitcast_fusion.wj_ref
  36.0 0.7 slice_bitcast_fusion.1.wo_ref.wo
  36.6 1.0 fusion.19
  37.6 43.3 %attend_forward.1 = (f32[2048,384]{1,0:T(8,128)}, bf16[2048,384]{1,0:T(8,128)(2,1)}, bf16[2,576,1024]{2,1,0:T(8,128)(2,1)}, f32[2,8,1024]{2,1,0:T(8,128)}, bf16[...) custom-call(f32[2,1,1024]{2,1,0:T(1,128)} %reshape.161.x_ref, f32[8,384]{1,0:T(8,128)} %maximum_maximum_fusion.rows_ref, ...), custom_call_target="tpu_custom_call" | custom-call | tf_op jit(solution)/shard_map/attend_forward/pallas_call | solution.py:145
  81.1 0.7 pad.40.clone.router
  81.8 11.3 %mid_forward.1 = (f32[2048,384]{1,0:T(8,128)}, bf16[2048,384]{1,0:T(8,128)(2,1)}, f32[2048,128]{1,0:T(8,128)}, f32[1,128]{1,0:T(1,128)}) custom-call(f32[2048,384]{1,0:T(8,128)} %get-tuple-element.47.part, f32[2048,384]{1,0:T(8,128)} %get-tuple-element.48.x0, f32[1,384]{1,0:T(1,128)} %get-tuple-element.207.gain, bf16[384,128]{1,0:T(8,128)(2,1)} %pad.40.clone.router), custom_call_target="tpu_custom_call" | custom-call | tf_op jit(solution)/shard_map/mid_forward/pallas_call | solution.py:523
  94.1 1.0 pad_maximum_fusion.own
  95.1 137.0 %gather_rows.3.w_ref = bf16[9,384,2304]{2,1,0:T(8,128)(2,1)} custom-call(bf16[9,24,2304]{2,1,0:T(8,128)(2,1)} %pad_maximum_fusion.own), custom_call_target="tpu_custom_call" | custom-call | tf_op jit(solution)/shard_map/gather_rows/pallas_call | solution.py:849
  232.1 47.7 %expert_forward.1 = (bf16[8,1024,384]{2,1,0:T(8,128)(2,1)}, f32[8,1024,384]{2,1,0:T(8,128)}, f32[2048,384]{1,0:T(8,128)}, f32[2048,384]{1,0:T(8,128)}) custom-call(s32[8]{0:T(128)} %copy-done.21, s32[8192]{0:T(1024)} %fusion.24.source, bf16[2048,384]{1,0:T(8,128)(2,1)} %get-tuple-element.49.b_ref.b, f32[2048,128]{1,0:T(8,128)} %get-tuple-element.50.pc_ref.pc, ...), custom_call_target="tpu_custom_call" | custom-call | tf_op jit(solution)/shard_map/expert_forward/pallas_call | solution.py:341
  280.2 0.8 copy.107.heads
  281.0 0.7 fusion.52.heads_t
  282.1 0.6 pad_maximum_fusion.1
  282.7 0.6 multiply_reduce_fusion.1
  283.3 2.7 concatenate.41
  286.0 0.6 broadcast_in_dim.65.value
  286.6 10.7 %all_blocks.2 = f32[32,8,128]{2,1,0:T(8,128)} custom-call(f32[8,128]{1,0:T(8,128)} %broadcast_in_dim.65.value), custom_call_target="tpu_custom_call" | custom-call | tf_op jit(solution)/shard_map/all_blocks/pallas_call | solution.py:1035
  297.3 1.0 slice_reduce_fusion.2
  298.2 0.6 fusion.51
  301.6 0.6 fusion.40.weight
  302.2 13.5 %loss_stage.1 = (f32[2048,384]{1,0:T(8,128)}, f32[128,384]{1,0:T(8,128)}, f32[1,384]{1,0:T(1,128)}, f32[1,128]{1,0:T(1,128)}) custom-call(f32[2048,384]{1,0:T(8,128)} %get-tuple-element.51.part, f32[2048,384]{1,0:T(8,128)} %get-tuple-element.52.x1, f32[1,384]{1,0:T(1,128)} %get-tuple-element.206.gain, bf16[384,128]{1,0:T(8,128)(2,1)} %copy.107.heads, ...), custom_call_target="tpu_custom_call" | custom-call | tf_op jit(solution)/shard_map/loss_stage/pallas_call | solution.py:585
  315.7 1.2 reduce_sum.129
  317.0 0.6 multiply_reduce_fusion.5
  318.9 83.1 %expert_backward.1 = (f32[9,384,2304]{2,1,0:T(8,128)}, f32[2048,512]{1,0:T(8,128)}) custom-call(s32[8]{0:T(128)} %copy-done.21, s32[8192]{0:T(1024)} %fusion.24.source, bf16[2048,384]{1,0:T(8,128)(2,1)} %get-tuple-element.49.b_ref.b, f32[2048,128]{1,0:T(8,128)} %get-tuple-element.50.pc_ref.pc, f32[2048,384]{1,0:T(8,128)} %get-tuple-element.53.dx_ref.dx2, ...), custom_call_target="tpu_custom_call" | custom-call | tf_op jit(solution)/shard_map/expert_backward/pallas_call | solution.py:449
  401.9 339.4 %reduce_rows.2 = f32[9,24,2304]{2,1,0:T(8,128)} custom-call(f32[9,4,2,2,24,2304]{5,4,3,2,1,0:T(8,128)} %bitcast.112), custom_call_target="tpu_custom_call" | custom-call | tf_op jit(solution)/shard_map/reduce_rows/pallas_call | solution.py:992
  741.4 2.7 multiply_reduce_fusion
  744.1 0.6 pad_bitcast_fusion.1.router_t
  744.7 0.5 pad_bitcast_fusion.2.balance
  745.2 15.3 %mid_backward.1 = (f32[2048,384]{1,0:T(8,128)}, bf16[2,192,1024]{2,1,0:T(8,128)(2,1)}, f32[128,384]{1,0:T(8,128)}, f32[192,384]{1,0:T(8,128)}, f32[1,384]{1,0:T(1,128)}) custom-call(f32[2048,512]{1,0:T(8,128)} %get-tuple-element.59.part, f32[2048,384]{1,0:T(8,128)} %get-tuple-element.53.dx_ref.dx2, f32[2048,384]{1,0:T(8,128)} %get-tuple-element.52.x1, ...), custom_call_target="tpu_custom_call" | custom-call | tf_op jit(solution)/shard_map/mid_backward/pallas_call | solution.py:638
  760.5 44.9 %attend_backward.1 = (f32[576,384]{1,0:T(8,128)}, f32[2048,384]{1,0:T(8,128)}) custom-call(bf16[2,576,1024]{2,1,0:T(8,128)(2,1)} %get-tuple-element.58.qkv_ref, bf16[2,192,1024]{2,1,0:T(8,128)(2,1)} %get-tuple-element.61.do_ref, f32[2,8,1024]{2,1,0:T(8,128)} %get-tuple-element.62.lse_ref, bf16[2048,384]{1,0:T(8,128)(2,1)} %get-tuple-element.63.a_ref, ...), custom_call_target="tpu_custom_call" | custom-call | tf_op jit(solution)/shard_map/attend_backward/pallas_call | solution.py:217
  805.4 0.7 slice_bitcast_fusion.5
  806.5 9.8 %embed_backward.1 = f32[8,384]{1,0:T(8,128)} custom-call(f32[2048,384]{1,0:T(8,128)} %get-tuple-element.68.part, f32[2048,384]{1,0:T(8,128)} %get-tuple-element.69.dx1, f32[2,1,1024]{2,1,0:T(1,128)} %reshape.161.x_ref, f32[8,384]{1,0:T(8,128)} %maximum_maximum_fusion.rows_ref), custom_call_target="tpu_custom_call" | custom-call | tf_op jit(solution)/shard_map/embed_backward/pallas_call | solution.py:684
  816.4 0.7 slice.210
  817.1 0.7 slice.209
  817.8 0.8 concatenate.44
  819.1 1.2 pad.47.clone
  820.3 41.4 %reduce_rows.3 = f32[1,24,896]{2,1,0:T(8,128)} custom-call(f32[1,4,2,2,24,896]{5,4,3,2,1,0:T(8,128)} %bitcast.113), custom_call_target="tpu_custom_call" | custom-call | tf_op jit(solution)/shard_map/reduce_rows/pallas_call | solution.py:992
  861.7 1.5 fusion.18
  864.5 1.3 fusion.35
  866.6 0.6 broadcast_in_dim.68.value
  867.2 9.1 %all_blocks.3 = f32[32,8,128]{2,1,0:T(8,128)} custom-call(f32[8,128]{1,0:T(8,128)} %broadcast_in_dim.68.value), custom_call_target="tpu_custom_call" | custom-call | tf_op jit(solution)/shard_map/all_blocks/pallas_call | solution.py:1035
  876.3 1.0 slice_reduce_fusion.1
  877.3 0.6 fusion.50
  879.3 0.9 slice_bitcast_fusion.4
  880.3 0.7 multiply_subtract_fusion.2
  881.0 1.5 multiply_subtract_fusion.3
  882.5 1.2 slice_multiply_fusion
  883.7 3.1 mul.324
  886.8 7.0 multiply_subtract_fusion
  893.9 1.6 multiply_subtract_fusion.1
  895.5 1.3 multiply_subtract_fusion.5
  897.1 0.8 multiply_subtract_fusion.4
  897.9 0.7 copy.114
  898.6 0.7 copy.115
  899.3 0.7 copy.116
  (125 shorter events, 4.6 us)
Async XLA Ops:
  4.5 4.0 copy-start.21
  4.7 4.5 copy-start.15
  4.8 4.5 copy-start.23
  4.8 5.2 copy-start.8
  4.8 5.2 copy-start.11
  4.8 5.2 copy-start.14
  4.8 5.2 copy-start.18
  81.8 11.3 %copy-start.3 = (f32[9,768,24]{1,2,0:T(8,128)S(1)}, f32[9,768,24]{1,2,0:T(8,128)}, u32[]{:S(2)}) copy-start(f32[9,768,24]{1,2,0:T(8,128)} %param.35) | copy-start | bytes 1990660
  81.8 11.4 %copy-start.1 = (f32[9,24,2,768]{3,2,1,0:T(2,128)S(1)}, f32[9,24,2,768]{3,2,1,0:T(2,128)}, u32[]{:S(2)}) copy-start(f32[9,24,2,768]{3,2,1,0:T(2,128)} %param.32) | copy-start | bytes 3981316
  232.1 50.6 %copy-start.22 = (s32[8]{0:T(128)S(1)}, s32[8]{0:T(128)}, u32[]{:S(2)}) copy-start(s32[8]{0:T(128)} %copy-done.21) | copy-start | bytes 100
  302.2 14.7 %copy-start.28 = (f32[1,128]{1,0:T(1,128)S(1)}, f32[1,128]{1,0:T(1,128)}, u32[]{:S(2)}) copy-start(f32[1,128]{1,0:T(1,128)} %get-tuple-element.73) | copy-start | bytes 1540
  760.5 45.7 %copy-start.10 = (f32[128,384]{1,0:T(8,128)S(1)}, f32[128,384]{1,0:T(8,128)}, u32[]{:S(2)}) copy-start(f32[128,384]{1,0:T(8,128)} %get-tuple-element.67) | copy-start | bytes 589828
  806.5 11.3 %copy-start.26 = (f32[1,384]{1,0:T(1,128)S(1)}, f32[1,384]{1,0:T(1,128)}, u32[]{:S(2)}) copy-start(f32[1,384]{1,0:T(1,128)} %get-tuple-element.71) | copy-start | bytes 4612
  806.5 11.3 %copy-start.27 = (f32[1,384]{1,0:T(1,128)S(1)}, f32[1,384]{1,0:T(1,128)}, u32[]{:S(2)}) copy-start(f32[1,384]{1,0:T(1,128)} %get-tuple-element.70) | copy-start | bytes 4612
  806.5 11.3 %copy-start.5 = (f32[576,384]{1,0:T(8,128)S(1)}, f32[576,384]{1,0:T(8,128)}, u32[]{:S(2)}) copy-start(f32[576,384]{1,0:T(8,128)} %get-tuple-element.64) | copy-start | bytes 2654212
  806.5 11.3 %copy-start.9 = (f32[192,384]{1,0:T(8,128)S(1)}, f32[192,384]{1,0:T(8,128)}, u32[]{:S(2)}) copy-start(f32[192,384]{1,0:T(8,128)} %get-tuple-element.65) | copy-start | bytes 884740
  819.1 61.2 %copy-start.12 = (f32[3,24,192]{2,1,0:T(8,128)S(1)}, f32[3,24,192]{2,1,0:T(8,128)}, u32[]{:S(2)}) copy-start(f32[3,24,192]{2,1,0:T(8,128)} %param.28) | copy-start | bytes 165892
  819.1 61.2 %copy-start.13 = (f32[3,24,192]{2,1,0:T(8,128)S(1)}, f32[3,24,192]{2,1,0:T(8,128)}, u32[]{:S(2)}) copy-start(f32[3,24,192]{2,1,0:T(8,128)} %param.27) | copy-start | bytes 165892
  820.3 60.7 %copy-start.16 = (f32[192,24]{0,1:T(8,128)S(1)}, f32[192,24]{0,1:T(8,128)}, u32[]{:S(2)}) copy-start(f32[192,24]{0,1:T(8,128)} %param.31) | copy-start | bytes 55300
  820.3 60.7 %copy-start.17 = (f32[192,24]{0,1:T(8,128)S(1)}, f32[192,24]{0,1:T(8,128)}, u32[]{:S(2)}) copy-start(f32[192,24]{0,1:T(8,128)} %param.30) | copy-start | bytes 55300
  820.3 62.2 %copy-start = (f32[9,24,2304]{2,1,0:T(8,128)S(1)}, f32[9,24,2304]{2,1,0:T(8,128)}, u32[]{:S(2)}) copy-start(f32[9,24,2304]{2,1,0:T(8,128)} %reduce_rows.2) | copy-start | bytes 5971972
  883.7 3.1 copy-start.2
  886.8 7.1 copy-start.4
  886.8 7.1 copy-start.6
  886.8 7.1 copy-start.7
  893.9 1.7 copy-start.19
  893.9 1.6 copy-start.20
  893.9 3.1 copy-start.24
  893.9 3.1 copy-start.25

commit v2 on v1

--- a/solution.py
+++ b/solution.py
@@ -273,24 +273,30 @@
     return jnp.sum(jnp.where(lanes == lane, block, 0.0), axis=1, keepdims=True)
 
 
-def expert_forward_kernel(
-    counts, source, b_ref, pc_ref, w_ref, x_ref, y_ref, ys_ref, mix_ref, rows8, acc8, tile8
-):
+def lay_rows(values, pc_ref, rows8, acc8):
+    tokens = values.shape[0]
+
+    def lay(i, carry):
+        r = pl.ds(pl.multiple_of(i * TILE, TILE), TILE)
+        spread_rows(rows8, values[r, :].astype(F32), i * TILE, TILE)
+        rows8[pl.ds(i * TILE * 8 + 3, TILE, stride=8), :] = pc_ref[r, :]
+        acc8[pl.ds(pl.multiple_of(i * TILE * 8, 8), TILE * 8), :] = jnp.zeros((TILE * 8, LANES), F32)
+        return carry
+
+    lax.fori_loop(0, tokens // TILE, lay, 0)
+    rows8[pl.ds(tokens * 8, 8), :] = jnp.zeros((8, LANES), F32)
+    acc8[pl.ds(tokens * 8, 8), :] = jnp.zeros((8, LANES), F32)
+
+
+def expert_forward_kernel(counts, source, b_ref, pc_ref, w_ref, x_ref, y_ref, mix_ref, rows8, acc8, tile8):
     e = pl.program_id(0)
-    tokens = b_ref.shape[0]
     hidden = w_ref.shape[2] // 3
+    capacity = y_ref.shape[1]
+    tiles = capacity // TILE
 
     @pl.when(e == 0)
     def _():
-        def lay(i, carry):
-            r = pl.ds(pl.multiple_of(i * TILE, TILE), TILE)
-            spread_rows(rows8, b_ref[r, :].astype(F32), i * TILE, TILE)
-            rows8[pl.ds(i * TILE * 8 + 3, TILE, stride=8), :] = pc_ref[r, :]
-            acc8[pl.ds(pl.multiple_of(i * TILE * 8, 8), TILE * 8), :] = jnp.zeros((TILE * 8, LANES), F32)
-            return carry
-        lax.fori_loop(0, tokens // TILE, lay, 0)
-        rows8[pl.ds(tokens * 8, 8), :] = jnp.zeros((8, LANES), F32)
-        acc8[pl.ds(tokens * 8, 8), :] = jnp.zeros((8, LANES), F32)
+        lay_rows(b_ref, pc_ref, rows8, acc8)
 
     def run(x):
         g = dot(x, w_ref[0, :, : 2 * hidden])
@@ -300,7 +306,7 @@
 
     @pl.when(e < ROUTED_EXPERTS)
     def _():
-        capacity = y_ref.shape[1]
+        used = (counts[e] + TILE - 1) // TILE
 
         def step(i, carry):
             base = e * capacity + i * TILE
@@ -315,46 +321,65 @@
             add_rows(acc8, tile8, source, base)
             return carry
 
-        lax.fori_loop(0, (counts[e] + TILE - 1) // TILE, step, 0)
-
-    @pl.when(e == ROUTED_EXPERTS)
+        def blank(i, carry):
+            x_ref[0, pl.ds(pl.multiple_of(i * TILE, TILE), TILE), :] = jnp.zeros((TILE, D), BF16)
+            return carry
+
+        lax.fori_loop(0, used, step, 0)
+        lax.fori_loop(used, tiles, blank, 0)
+
+    @pl.when(e >= ROUTED_EXPERTS)
     def _():
         def step(i, carry):
-            r = pl.ds(pl.multiple_of(i * TILE, TILE), TILE)
-            y = run(b_ref[r, :])
-            ys_ref[r, :] = y
+            t = (e - ROUTED_EXPERTS) * tiles + i
+            here = pl.ds(pl.multiple_of(i * TILE, TILE), TILE)
+            r = pl.ds(pl.multiple_of(t * TILE, TILE), TILE)
+            x = b_ref[r, :]
+            x_ref[0, here, :] = x
+            y = run(x)
+            y_ref[0, here, :] = y
             shared = y * lane_of(pc_ref[r, :], ROUTED_EXPERTS)
             for c in range(D // LANES):
                 cols = slice(c * LANES, (c + 1) * LANES)
-                mix_ref[r, cols] = acc8[pl.ds(i * TILE * 8 + c, TILE, stride=8), :] + shared[:, cols]
+                mix_ref[r, cols] = acc8[pl.ds(t * TILE * 8 + c, TILE, stride=8), :] + shared[:, cols]
             return carry
 
-        lax.fori_loop(0, tokens // TILE, step, 0)
+        lax.fori_loop(0, tiles, step, 0)
+
+
+def expert_blocks(capacity, w):
+    return pl.BlockSpec((1, capacity, w), lambda e, *_: (e, 0, 0))
+
+
+def expert_weights(weights):
+    return pl.BlockSpec((1,) + weights.shape[1:], lambda e, *_: (jnp.minimum(e, ROUTED_EXPERTS), 0, 0))
+
+
+def expert_scratch(tokens):
+    return [
+        pltpu.VMEM(((tokens + 1) * 8, LANES), F32),
+        pltpu.VMEM(((tokens + 1) * 8, LANES), F32),
+        pltpu.VMEM((TILE * 8, LANES), F32),
+    ]
 
 
 def expert_forward(counts, source, b, pc, weights):
     tokens = b.shape[0]
     capacity = tokens // 2
-    last = ROUTED_EXPERTS - 1
-    full = lambda shape: pl.BlockSpec(shape, lambda e, *_: (0,) * len(shape))
-    exp = lambda w: pl.BlockSpec((1, capacity, w), lambda e, *_: (jnp.minimum(e, last), 0, 0))
+    blocks = ROUTED_EXPERTS + 2
+    full = lambda shape: pl.BlockSpec(shape, lambda e, *_: (0,) * len(shape), pipeline_mode=pl.Buffered(1))
     return pl.pallas_call(
         expert_forward_kernel,
         grid_spec=pltpu.PrefetchScalarGridSpec(
             num_scalar_prefetch=2,
-            grid=(ROUTED_EXPERTS + 1,),
-            in_specs=[full(b.shape), full(pc.shape), pl.BlockSpec((1,) + weights.shape[1:], lambda e, *_: (e, 0, 0))],
-            out_specs=[exp(D), exp(D), full((tokens, D)), full((tokens, D))],
-            scratch_shapes=[
-                pltpu.VMEM(((tokens + 1) * 8, LANES), F32),
-                pltpu.VMEM(((tokens + 1) * 8, LANES), F32),
-                pltpu.VMEM((TILE * 8, LANES), F32),
-            ],
+            grid=(blocks,),
+            in_specs=[full(b.shape), full(pc.shape), expert_weights(weights)],
+            out_specs=[expert_blocks(capacity, D), expert_blocks(capacity, D), full((tokens, D))],
+            scratch_shapes=expert_scratch(tokens),
         ),
         out_shape=[
-            jax.ShapeDtypeStruct((ROUTED_EXPERTS, capacity, D), BF16),
-            jax.ShapeDtypeStruct((ROUTED_EXPERTS, capacity, D), F32),
-            jax.ShapeDtypeStruct((tokens, D), F32),
+            jax.ShapeDtypeStruct((blocks, capacity, D), BF16),
+            jax.ShapeDtypeStruct((blocks, capacity, D), F32),
             jax.ShapeDtypeStruct((tokens, D), F32),
         ],
         compiler_params=params(),
@@ -363,44 +388,38 @@
 
 
 def expert_backward_kernel(
-    counts, source, b_ref, pc_ref, dx_ref, w_ref, x_ref, y_ref, ys_ref, dw_ref, acc_ref, rows8, acc8, tile8
+    counts, source, pc_ref, dx_ref, w_ref, x_ref, y_ref, dy_ref, dg_ref, h_ref, acc_ref, rows8, acc8, tile8
 ):
     e = pl.program_id(0)
-    tokens = b_ref.shape[0]
     hidden = w_ref.shape[2] // 3
+    capacity = y_ref.shape[1]
+    tiles = capacity // TILE
 
     @pl.when(e == 0)
     def _():
-        def lay(i, carry):
-            r = pl.ds(pl.multiple_of(i * TILE, TILE), TILE)
-            spread_rows(rows8, dx_ref[r, :], i * TILE, TILE)
-            rows8[pl.ds(i * TILE * 8 + 3, TILE, stride=8), :] = pc_ref[r, :]
-            acc8[pl.ds(pl.multiple_of(i * TILE * 8, 8), TILE * 8), :] = jnp.zeros((TILE * 8, LANES), F32)
-            return carry
-        lax.fori_loop(0, tokens // TILE, lay, 0)
-        rows8[pl.ds(tokens * 8, 8), :] = jnp.zeros((8, LANES), F32)
-        acc8[pl.ds(tokens * 8, 8), :] = jnp.zeros((8, LANES), F32)
-
-    dw_ref[...] = jnp.zeros_like(dw_ref)
-
-    def run(x, dy):
+        lay_rows(dx_ref, pc_ref, rows8, acc8)
+
+    def run(r, dy):
+        x = x_ref[0, r, :]
+        dy_ref[0, r, :] = dy
         u = w_ref[0, :, : 2 * hidden]
         g = dot(x, u)
         gate, up = g[:, :hidden], g[:, hidden:]
         s = sigmoid(gate)
         silu = gate * s
-        h = (silu * up).astype(BF16)
+        h_ref[0, r, :] = (silu * up).astype(BF16)
         dh = dot(dy, w_ref[0, :, 2 * hidden:])
         d_up = (dh * silu).astype(BF16)
         d_gate = (dh * up * (s * (1.0 + gate * (1.0 - s)))).astype(BF16)
-        dg = jnp.concatenate([d_gate, d_up], axis=1)
-        dw_ref[0, :, : 2 * hidden] += dot(x, dg, 0, 0)
-        dw_ref[0, :, 2 * hidden:] += dot(dy, h, 0, 0)
-        return dot(dg, u, 1, 1)
+        dg_ref[0, r, :hidden] = d_gate
+        dg_ref[0, r, hidden:] = d_up
+        return dot(d_gate, u[:, :hidden], 1, 1) + dot(d_up, u[:, hidden:], 1, 1)
+
+    lanes = lax.broadcasted_iota(jnp.int32, (TILE, LANES), 1)
 
     @pl.when(e < ROUTED_EXPERTS)
     def _():
-        capacity = y_ref.shape[1]
+        used = (counts[e] + TILE - 1) // TILE
 
         def step(i, carry):
             base = e * capacity + i * TILE
@@ -409,63 +428,69 @@
             c0, c1, c2, pc = gathered_columns(tile8, 4)
             dx = jnp.concatenate([c0, c1, c2], axis=1)
             d_gate = jnp.sum(y_ref[0, r, :] * dx, axis=1, keepdims=True)
-            dy = (dx * lane_of(pc, e)).astype(BF16)
-            back = run(x_ref[0, r, :], dy)
+            back = run(r, (dx * lane_of(pc, e)).astype(BF16))
             spread_rows(tile8, back, 0, TILE)
-            lanes = lax.broadcasted_iota(jnp.int32, (TILE, LANES), 1)
             tile8[pl.ds(3, TILE, stride=8), :] = jnp.where(lanes == e, d_gate, 0.0)
             add_rows(acc8, tile8, source, base)
             return carry
 
-        lax.fori_loop(0, (counts[e] + TILE - 1) // TILE, step, 0)
-
-    @pl.when(e == ROUTED_EXPERTS)
+        def blank(i, carry):
+            r = pl.ds(pl.multiple_of(i * TILE, TILE), TILE)
+            dy_ref[0, r, :] = jnp.zeros((TILE, D), BF16)
+            dg_ref[0, r, :] = jnp.zeros((TILE, 2 * hidden), BF16)
+            h_ref[0, r, :] = jnp.zeros((TILE, hidden), BF16)
+            return carry
+
+        lax.fori_loop(0, used, step, 0)
+        lax.fori_loop(used, tiles, blank, 0)
+
+    @pl.when(e >= ROUTED_EXPERTS)
     def _():
         def step(i, carry):
-            r = pl.ds(pl.multiple_of(i * TILE, TILE), TILE)
+            t = (e - ROUTED_EXPERTS) * tiles + i
+            here = pl.ds(pl.multiple_of(i * TILE, TILE), TILE)
+            r = pl.ds(pl.multiple_of(t * TILE, TILE), TILE)
             dx = dx_ref[r, :]
-            d_gate = jnp.sum(ys_ref[r, :] * dx, axis=1, keepdims=True)
-            dy = (dx * lane_of(pc_ref[r, :], ROUTED_EXPERTS)).astype(BF16)
-            back = run(b_ref[r, :], dy)
+            d_gate = jnp.sum(y_ref[0, here, :] * dx, axis=1, keepdims=True)
+            back = run(here, (dx * lane_of(pc_ref[r, :], ROUTED_EXPERTS)).astype(BF16))
             for c in range(D // LANES):
                 cols = slice(c * LANES, (c + 1) * LANES)
-                acc_ref[r, cols] = acc8[pl.ds(i * TILE * 8 + c, TILE, stride=8), :] + back[:, cols]
-            lanes = lax.broadcasted_iota(jnp.int32, (TILE, LANES), 1)
+                acc_ref[r, cols] = acc8[pl.ds(t * TILE * 8 + c, TILE, stride=8), :] + back[:, cols]
             acc_ref[r, D:] = jnp.where(
-                lanes == ROUTED_EXPERTS, d_gate, acc8[pl.ds(i * TILE * 8 + 3, TILE, stride=8), :])
+                lanes == ROUTED_EXPERTS, d_gate, acc8[pl.ds(t * TILE * 8 + 3, TILE, stride=8), :])
             return carry
 
-        lax.fori_loop(0, tokens // TILE, step, 0)
-
-
-def expert_backward(counts, source, b, pc, dx, weights, x, y, ys):
-    tokens = b.shape[0]
+        lax.fori_loop(0, tiles, step, 0)
+
+
+def expert_backward(counts, source, pc, dx, weights, x, y):
+    tokens = dx.shape[0]
     capacity = tokens // 2
-    last = ROUTED_EXPERTS - 1
-    once = pl.Buffered(1)
-    full = lambda shape: pl.BlockSpec(shape, lambda e, *_: (0,) * len(shape), pipeline_mode=once)
-    exp = lambda w: pl.BlockSpec((1, capacity, w), lambda e, *_: (jnp.minimum(e, last), 0, 0))
-    wide = pl.BlockSpec((1,) + weights.shape[1:], lambda e, *_: (e, 0, 0))
+    blocks = ROUTED_EXPERTS + 2
+    hidden = weights.shape[2] // 3
+    full = lambda shape: pl.BlockSpec(shape, lambda e, *_: (0,) * len(shape), pipeline_mode=pl.Buffered(1))
     return pl.pallas_call(
         expert_backward_kernel,
         grid_spec=pltpu.PrefetchScalarGridSpec(
             num_scalar_prefetch=2,
-            grid=(ROUTED_EXPERTS + 1,),
-            in_specs=[full(b.shape), full(pc.shape), full(dx.shape), wide, exp(D), exp(D), full(ys.shape)],
-            out_specs=[wide, full((tokens, D + LANES))],
-            scratch_shapes=[
-                pltpu.VMEM(((tokens + 1) * 8, LANES), F32),
-                pltpu.VMEM(((tokens + 1) * 8, LANES), F32),
-                pltpu.VMEM((TILE * 8, LANES), F32),
-            ],
+            grid=(blocks,),
+            in_specs=[
+                full(pc.shape), full(dx.shape), expert_weights(weights),
+                expert_blocks(capacity, D), expert_blocks(capacity, D)],
+            out_specs=[
+                expert_blocks(capacity, D), expert_blocks(capacity, 2 * hidden), expert_blocks(capacity, hidden),
+                full((tokens, D + LANES))],
+            scratch_shapes=expert_scratch(tokens),
         ),
         out_shape=[
-            jax.ShapeDtypeStruct(weights.shape, F32),
+            jax.ShapeDtypeStruct((blocks, capacity, D), BF16),
+            jax.ShapeDtypeStruct((blocks, capacity, 2 * hidden), BF16),
+            jax.ShapeDtypeStruct((blocks, capacity, hidden), BF16),
             jax.ShapeDtypeStruct((tokens, D + LANES), F32),
         ],
         compiler_params=params(),
         name="expert_backward",
-    )(counts, source, b, pc, dx, weights, x, y, ys)
+    )(counts, source, pc, dx, weights, x, y)
 
 
 def exchange(part, other, send_sem, recv_sem):
@@ -1043,6 +1068,255 @@
     )(value)
 
 
+I16 = jnp.int16
+SLOTS = 3
+
+
+def encode(dest, v):
+    width = v.shape[1]
+    top = jnp.max(jnp.abs(v), axis=1, keepdims=True)
+    power = jnp.ceil(jnp.log2(jnp.maximum(top, 1e-30) * (1.001 / 32767.0)))
+    power = jnp.broadcast_to(power, (v.shape[0], LANES))
+    inverse = jnp.exp2(-power)
+    dest[:, width:] = power.astype(jnp.int32).astype(I16)
+    for c in range(width // LANES):
+        cols = slice(c * LANES, (c + 1) * LANES)
+        dest[:, cols] = jnp.round(v[:, cols] * inverse).astype(jnp.int32).astype(I16)
+
+
+def decode(source):
+    width = source.shape[1] - LANES
+    unit = jnp.exp2(source[:, width:].astype(jnp.int32).astype(F32))
+    return jnp.concatenate(
+        [source[:, c * LANES:(c + 1) * LANES].astype(jnp.int32).astype(F32) * unit for c in range(width // LANES)],
+        axis=1)
+
+
+def gradient_kernel(
+    xs, dys, dgs, hs, out,
+    x_in, dy_in, dg_in, h_in, xt, dyt, dw, acc, send1, recv1, send2, recv2, zs_up, zs_dn, up, dn,
+    load_sem, sem_s1, sem_r1, sem_s2, sem_r2, sem_su, sem_sd, sem_ru, sem_rd,
+):
+    dp, mp, x, y, z = place()
+    count = out.shape[0]
+    blocks = xs.shape[0]
+    hidden = hs.shape[2]
+
+    def loads(block):
+        return [
+            pltpu.make_async_copy(src.at[block], dst, load_sem.at[i])
+            for i, (src, dst) in enumerate(((xs, x_in), (dys, dy_in), (dgs, dg_in), (hs, h_in)))]
+
+    for copy in loads(0):
+        copy.start()
+    xp, yp = greet(dp, mp, x, y, z)
+
+    def remote(src, dst, send, recv, peer):
+        return pltpu.make_async_remote_copy(
+            src_ref=src, dst_ref=dst, send_sem=send, recv_sem=recv, device_id=(peer, mp), device_id_type=MESH)
+
+    def done(view, sem):
+        pltpu.make_async_copy(view, view, sem).wait()
+
+    def shard(slot, s):
+        return dw.at[slot, pl.ds(pl.multiple_of(s * SHARD, 8), SHARD), :]
+
+    def weights(block, slot, more):
+        for copy in loads(block):
+            copy.wait()
+        xt[...] = jnp.transpose(x_in[...])
+        dyt[...] = jnp.transpose(dy_in[...])
+
+        def wide(j, carry):
+            cols = pl.ds(pl.multiple_of(j * TILE, TILE), TILE)
+            v = dot(xt[...], dg_in[:, cols])
+            dw[slot, :, cols] = dw[slot, :, cols] + v if more else v
+            return carry
+
+        def tall(j, carry):
+            cols = pl.ds(pl.multiple_of(j * TILE, TILE), TILE)
+            there = pl.ds(pl.multiple_of(2 * hidden + j * TILE, TILE), TILE)
+            v = dot(dyt[...], h_in[:, cols])
+            dw[slot, :, there] = dw[slot, :, there] + v if more else v
+            return carry
+
+        lax.fori_loop(0, 2 * hidden // TILE, wide, 0)
+        lax.fori_loop(0, hidden // TILE, tall, 0)
+
+        @pl.when(block + 1 < blocks)
+        def _():
+            for copy in loads(block + 1):
+                copy.start()
+
+    def begin(c):
+        k, slot = lax.rem(c, 2), lax.rem(c, SLOTS)
+        weights(c, slot, False)
+
+        @pl.when(c == count - 1)
+        def _():
+            weights(c + 1, slot, True)
+
+        @pl.when(c >= SLOTS)
+        def _():
+            done(send1.at[slot], sem_s1.at[slot])
+
+        def pack(i, carry):
+            a, b = i // 2, lax.rem(i, 2)
+            s = a * 4 + jnp.where(k == 0, b * 2 + 1 - x, (1 - y) * 2 + b)
+            encode(send1.at[slot, i], shard(slot, s)[...])
+            return carry
+
+        lax.fori_loop(0, 8, pack, 0)
+        remote(send1.at[slot], recv1.at[c], sem_s1.at[slot], sem_r1.at[c], jnp.where(k == 0, xp, yp)).start()
+
+    def fold(c):
+        k, slot = lax.rem(c, 2), lax.rem(c, SLOTS)
+        o = jnp.where(k == 0, y, x)
+        done(recv1.at[c], sem_r1.at[c])
+
+        @pl.when(c >= SLOTS)
+        def _():
+            done(send2.at[slot], sem_s2.at[slot])
+
+        def add(a, carry):
+            s = a * 4 + jnp.where(k == 0, (1 - y) * 2 + x, y * 2 + 1 - x)
+            encode(send2.at[slot, a], shard(slot, s)[...] + decode(recv1.at[c, a * 2 + 1 - o]))
+            acc[lax.rem(c, 5), a] = shard(slot, a * 4 + y * 2 + x)[...] + decode(recv1.at[c, a * 2 + o])
+            return carry
+
+        lax.fori_loop(0, 4, add, 0)
+        remote(send2.at[slot], recv2.at[c], sem_s2.at[slot], sem_r2.at[c], jnp.where(k == 0, yp, xp)).start()
+
+    def climb(c, t, relay):
+        slot = lax.rem(c, SLOTS)
+        v = acc[lax.rem(c, 5), t]
+        if relay:
+            done(up.at[c, t - 1], sem_ru.at[c, t - 1])
+            v = v + decode(up.at[c, t - 1])
+
+        @pl.when(c >= SLOTS)
+        def _():
+            done(zs_up.at[slot, t - 1], sem_su.at[slot, t - 1])
+        encode(zs_up.at[slot, t - 1], v)
+        remote(zs_up.at[slot, t - 1], up.at[c, t - 1], sem_su.at[slot, t - 1], sem_ru.at[c, t - 1], dp + 4).start()
+
+    def drop(c, t, relay):
+        slot = lax.rem(c, SLOTS)
+        v = acc[lax.rem(c, 5), t]
+        if relay:
+            done(dn.at[c, t], sem_rd.at[c, t])
+            v = v + decode(dn.at[c, t])
+
+        @pl.when(c >= SLOTS)
+        def _():
+            done(zs_dn.at[slot, t], sem_sd.at[slot, t])
+        encode(zs_dn.at[slot, t], v)
+        remote(zs_dn.at[slot, t], dn.at[c, t], sem_sd.at[slot, t], sem_rd.at[c, t], dp - 4).start()
+
+    def line_a(c):
+        done(recv2.at[c], sem_r2.at[c])
+
+        def add(a, carry):
+            acc[lax.rem(c, 5), a] = acc[lax.rem(c, 5), a] + decode(recv2.at[c, a])
+            return carry
+
+        lax.fori_loop(0, 4, add, 0)
+        out[c] = acc[lax.rem(c, 5), z]
+
+        @pl.when(z == 0)
+        def _():
+            for t in (3, 2, 1):
+                climb(c, t, False)
+
+        @pl.when(z == 3)
+        def _():
+            for t in (0, 1, 2):
+                drop(c, t, False)
+
+    def line_b(c):
+        @pl.when(z == 1)
+        def _():
+            for t in (3, 2):
+                climb(c, t, True)
+
+        @pl.when(z == 2)
+        def _():
+            for t in (0, 1):
+                drop(c, t, True)
+
+    def line_c(c):
+        @pl.when(z == 2)
+        def _():
+            climb(c, 3, True)
+
+        @pl.when(z == 1)
+        def _():
+            drop(c, 0, True)
+
+    def finish(c):
+        @pl.when(z > 0)
+        def _():
+            done(up.at[c, z - 1], sem_ru.at[c, z - 1])
+            out[c] = out[c] + decode(up.at[c, z - 1])
+
+        @pl.when(z < 3)
+        def _():
+            done(dn.at[c, z], sem_rd.at[c, z])
+            out[c] = out[c] + decode(dn.at[c, z])
+
+    stages = ((begin, 0), (fold, 2), (line_a, 4), (line_b, 5), (line_c, 6), (finish, 7))
+
+    def step(i, carry):
+        for stage, lag in stages:
+            @pl.when((i >= lag) & (i < count + lag))
+            def _(stage=stage, lag=lag):
+                stage(i - lag)
+        return carry
+
+    lax.fori_loop(0, count + stages[-1][1], step, 0)
+
+    for slot in range(SLOTS):
+        done(send1.at[slot], sem_s1.at[slot])
+        done(send2.at[slot], sem_s2.at[slot])
+        for t in (1, 2, 3):
+            @pl.when(z < t)
+            def _():
+                done(zs_up.at[slot, t - 1], sem_su.at[slot, t - 1])
+        for t in (0, 1, 2):
+            @pl.when(z > t)
+            def _():
+                done(zs_dn.at[slot, t], sem_sd.at[slot, t])
+
+
+def gradient_sums(xs, dys, dgs, hs, ident):
+    capacity, hidden = hs.shape[1], hs.shape[2]
+    count = ROUTED_EXPERTS + 1
+    width = 3 * hidden
+    coded = width + LANES
+    dma = pltpu.SemaphoreType.DMA
+    return pl.pallas_call(
+        gradient_kernel,
+        in_specs=[ANY] * 4,
+        out_specs=VMEM,
+        out_shape=jax.ShapeDtypeStruct((count, SHARD, width), F32),
+        scratch_shapes=[
+            pltpu.VMEM((capacity, D), BF16), pltpu.VMEM((capacity, D), BF16),
+            pltpu.VMEM((capacity, 2 * hidden), BF16), pltpu.VMEM((capacity, hidden), BF16),
+            pltpu.VMEM((D, capacity), BF16), pltpu.VMEM((D, capacity), BF16),
+            pltpu.VMEM((SLOTS, D, width), F32),
+            pltpu.VMEM((5, 4, SHARD, width), F32),
+            pltpu.VMEM((SLOTS, 8, SHARD, coded), I16), pltpu.VMEM((count, 8, SHARD, coded), I16),
+            pltpu.VMEM((SLOTS, 4, SHARD, coded), I16), pltpu.VMEM((count, 4, SHARD, coded), I16),
+            pltpu.VMEM((SLOTS, 3, SHARD, coded), I16), pltpu.VMEM((SLOTS, 3, SHARD, coded), I16),
+            pltpu.VMEM((count, 3, SHARD, coded), I16), pltpu.VMEM((count, 3, SHARD, coded), I16),
+            dma((4,)), dma((SLOTS,)), dma((count,)), dma((SLOTS,)), dma((count,)),
+            dma((SLOTS, 3)), dma((SLOTS, 3)), dma((count, 3)), dma((count, 3)),
+        ],
+        compiler_params=params(63, collective_id=ident, has_side_effects=True),
+        name="gradient_sums",
+    )(xs, dys, dgs, hs)
+
+
 def rope_tables(length):
     halfway = HEAD // 2
     frequency = rope_base ** (-2.0 * jnp.arange(halfway, dtype=F32) / HEAD)
@@ -1165,13 +1439,13 @@
 
     x0, a, qkv, lse, o, part = attend_forward(x, rows, wj, wo, cos, sin)
     x1, b, pc, pr_total = mid_forward(part, x0, vec[1:2], router, 3)
-    xs, ys, shared, mixed = expert_forward(expert_here, source, b, pc, big)
+    xs, ys, mixed = expert_forward(expert_here, source, b, pc, big)
     head_weight = jnp.concatenate(
         [jnp.zeros((horizon,), F32) + 0.25 / head_count[3 - index] for index, horizon in enumerate(horizons[::-1])])
     head_weight = jnp.pad(head_weight, (0, LANES - head_weight.shape[0]))[None]
     dx2, d_heads, d_gain3, fit = loss_stage(
         mixed, x1, vec[2:3], heads, heads.T, hankel_rows(series), hankel_rows(marks), head_weight, 4)
-    d_big, back = expert_backward(expert_here, source, b, pc, dx2, big, xs, ys, shared)
+    dys, dgs, hs, back = expert_backward(expert_here, source, pc, dx2, big, xs, ys)
     balance = aux_factor * ROUTED_EXPERTS * expert_count / total_tokens / total_tokens
     balance = jnp.pad(balance, (0, LANES - ROUTED_EXPERTS))[None]
     local_loss = jnp.sum(fit) + jnp.sum(pr_total * balance)
@@ -1186,9 +1460,13 @@
     d_small = pack_small(
         [d_wj[:, k * width:(k + 1) * width] for k in range(3)], d_wo.T, d_read, d_vec)
     if near:
-        big_red = reduce_rows(d_big, 2, 7)
+        big_red = gradient_sums(xs, dys, dgs, hs, 7)
         small_red = reduce_rows(d_small[None], 1, 8)[0]
     else:
+        d_up = jnp.einsum("ekd,ekf->edf", xs, dgs, preferred_element_type=F32)
+        d_down = jnp.einsum("ekd,ekf->edf", dys, hs, preferred_element_type=F32)
+        d_big = jnp.concatenate([d_up, d_down], axis=2)
+        d_big = jnp.concatenate([d_big[:ROUTED_EXPERTS], jnp.sum(d_big[ROUTED_EXPERTS:], axis=0, keepdims=True)], axis=0)
         big_red = lax.psum_scatter(d_big, "dp", scatter_dimension=1, tiled=True)
         small_red = lax.psum_scatter(d_small, "dp", scatter_dimension=0, tiled=True)
     attn_red = small_red[:, :4 * width]

time: 903 us -> 727 us (0.81)
  Pallas kernels: 828 us -> 655 us
    pallas_call x2 -> x1, Pallas kernels: 381 us -> 44.8 us  [reduce_rows(): pl.pallas_call(functools.partial(reduce_kernel, count, halves), out_shape...]
    pallas_call x0 -> x1, Pallas kernels: none -> 174 us  [gradient_sums(): pl.pallas_call(gradient_kernel, in_specs=[ANY] * 4, out_specs=VMEM, out_s...]
    pallas_call x1, Pallas kernels: 83.1 us -> 72 us  [expert_backward(): pl.pallas_call(expert_backward_kernel, grid_spec=pltpu.PrefetchScalarGrid...]
where the time goes in v2:
time: 727 us; the launch traced here: 728 us
  Pallas kernels  655 us (90%)
  other arithmetic  33.5 us (5%)
  local copies, waits for them, and re-layouts  25.8 us (4%)
  between operations  9.93 us (1%)
    pallas_call x1, Pallas kernels, gradient_sums(): pl.pallas_call(gradient_kernel, in_specs=[ANY] * 4, out_specs=VMEM, out_s...  174 us
    pallas_call x2, Pallas kernels, gather_rows(): pl.pallas_call(functools.partial(gather_kernel, chunks), out_shape=jax.Sh...  158 us
    pallas_call x1, Pallas kernels, expert_backward(): pl.pallas_call(expert_backward_kernel, grid_spec=pltpu.PrefetchScalarGrid...  72 us
    pallas_call x1, Pallas kernels, expert_forward(): pl.pallas_call(expert_forward_kernel, grid_spec=pltpu.PrefetchScalarGridS...  50 us
    pallas_call x1, Pallas kernels, attend_backward(): pl.pallas_call(attend_backward_kernel, grid=(series,), in_specs=[ser(rows...  44.9 us
    pallas_call x1, Pallas kernels, reduce_rows(): pl.pallas_call(functools.partial(reduce_kernel, count, halves), out_shape...  44.8 us
    pallas_call x1, Pallas kernels, attend_forward(): pl.pallas_call(attend_forward_kernel, grid=(series,), in_specs=[ser(1), f...  43.3 us
    pallas_call x2, Pallas kernels, all_blocks(): pl.pallas_call(functools.partial(all_kernel, n_dp), out_shape=jax.ShapeDt...  17.7 us

profile of v2, /device:TPU:0, one launch (start us, length us, event | category | flops | bytes accessed | tf_op | source)
XLA Modules:
  0.0 728.2 jit_solution(14794275133596792541)
XLA Ops:
  0.7 0.7 fusion.13
  1.4 2.3 reduce-window.6
  4.8 3.7 fusion
  8.6 0.6 fusion.24.source
  9.3 0.6 reshape.158.x_ref
  10.2 0.6 pad_bitcast_fusion.own
  10.9 21.5 %gather_rows.2 = bf16[1,384,896]{2,1,0:T(8,128)(2,1)} custom-call(bf16[1,24,896]{2,1,0:T(8,128)(2,1)} %pad_bitcast_fusion.own), custom_call_target="tpu_custom_call" | custom-call | tf_op jit(solution)/shard_map/gather_rows/pallas_call | solution.py:874
  32.4 1.4 copy.105
  33.8 0.6 fusion.49
  34.5 0.7 maximum_maximum_fusion.rows_ref
  35.2 0.8 slice_bitcast_fusion.wj_ref
  36.0 0.7 slice_bitcast_fusion.1.wo_ref.wo
  36.6 1.0 fusion.19
  37.6 43.3 %attend_forward.1 = (f32[2048,384]{1,0:T(8,128)}, bf16[2048,384]{1,0:T(8,128)(2,1)}, bf16[2,576,1024]{2,1,0:T(8,128)(2,1)}, f32[2,8,1024]{2,1,0:T(8,128)}, bf16[...) custom-call(f32[2,1,1024]{2,1,0:T(1,128)} %reshape.158.x_ref, f32[8,384]{1,0:T(8,128)} %maximum_maximum_fusion.rows_ref, ...), custom_call_target="tpu_custom_call" | custom-call | tf_op jit(solution)/shard_map/attend_forward/pallas_call | solution.py:145
  81.1 0.7 pad.40.clone.router
  81.8 11.3 %mid_forward.1 = (f32[2048,384]{1,0:T(8,128)}, bf16[2048,384]{1,0:T(8,128)(2,1)}, f32[2048,128]{1,0:T(8,128)}, f32[1,128]{1,0:T(1,128)}) custom-call(f32[2048,384]{1,0:T(8,128)} %get-tuple-element.48.part, f32[2048,384]{1,0:T(8,128)} %get-tuple-element.49.x0, f32[1,384]{1,0:T(1,128)} %get-tuple-element.209.gain, bf16[384,128]{1,0:T(8,128)(2,1)} %pad.40.clone.router), custom_call_target="tpu_custom_call" | custom-call | tf_op jit(solution)/shard_map/mid_forward/pallas_call | solution.py:548
  94.1 1.0 pad_maximum_fusion.own
  95.1 137.0 %gather_rows.3.w_ref = bf16[9,384,2304]{2,1,0:T(8,128)(2,1)} custom-call(bf16[9,24,2304]{2,1,0:T(8,128)(2,1)} %pad_maximum_fusion.own), custom_call_target="tpu_custom_call" | custom-call | tf_op jit(solution)/shard_map/gather_rows/pallas_call | solution.py:874
  232.1 50.0 %expert_forward.1 = (bf16[10,1024,384]{2,1,0:T(8,128)(2,1)}, f32[10,1024,384]{2,1,0:T(8,128)}, f32[2048,384]{1,0:T(8,128)}) custom-call(s32[8]{0:T(128)} %copy-done.21, s32[8192]{0:T(1024)} %fusion.24.source, bf16[2048,384]{1,0:T(8,128)(2,1)} %get-tuple-element.50.b_ref.b, f32[2048,128]{1,0:T(8,128)} %get-tuple-element.51.pc_ref.pc, ...), custom_call_target="tpu_custom_call" | custom-call | tf_op jit(solution)/shard_map/expert_forward/pallas_call | solution.py:371
  282.5 0.8 copy.107.heads
  283.3 0.7 fusion.52.heads_t
  284.3 0.6 pad_maximum_fusion.1
  285.0 0.6 multiply_reduce_fusion.1
  285.6 2.7 concatenate.41
  288.3 0.6 broadcast_in_dim.65.value
  288.9 8.9 %all_blocks.2 = f32[32,8,128]{2,1,0:T(8,128)} custom-call(f32[8,128]{1,0:T(8,128)} %broadcast_in_dim.65.value), custom_call_target="tpu_custom_call" | custom-call | tf_op jit(solution)/shard_map/all_blocks/pallas_call | solution.py:1060
  297.7 1.0 slice_reduce_fusion.2
  298.7 0.6 fusion.51
  302.1 0.6 fusion.40.weight
  302.7 13.5 %loss_stage.1 = (f32[2048,384]{1,0:T(8,128)}, f32[128,384]{1,0:T(8,128)}, f32[1,384]{1,0:T(1,128)}, f32[1,128]{1,0:T(1,128)}) custom-call(f32[2048,384]{1,0:T(8,128)} %get-tuple-element.53.part, f32[2048,384]{1,0:T(8,128)} %get-tuple-element.54.x1, f32[1,384]{1,0:T(1,128)} %get-tuple-element.208.gain, bf16[384,128]{1,0:T(8,128)(2,1)} %copy.107.heads, ...), custom_call_target="tpu_custom_call" | custom-call | tf_op jit(solution)/shard_map/loss_stage/pallas_call | solution.py:610
  316.2 1.2 reduce_sum.129
  317.4 0.6 multiply_reduce_fusion.5
  319.3 72.0 %expert_backward.1 = (bf16[10,1024,384]{2,1,0:T(8,128)(2,1)}, bf16[10,1024,1536]{2,1,0:T(8,128)(2,1)}, bf16[10,1024,768]{2,1,0:T(8,128)(2,1)}, f32[2048,512]{1,0:T(8,128)}) custom-call(s32[8]{0:T(128)} %copy-done.21, s32[8192]{0:T(1024)} %fusion.24.source, f32[2048,128]{1,0:T(8,128)} %get-tuple-element.51.pc_ref.pc, ...), custom_call_target="tpu_custom_call" | custom-call | tf_op jit(solution)/shard_map/expert_backward/pallas_call | solution.py:472
  391.2 174.2 %gradient_sums.1 = f32[9,24,2304]{2,1,0:T(8,128)} custom-call(bf16[10,1024,384]{2,1,0:T(8,128)(2,1)} %get-tuple-element.52.x_ref.xs, bf16[10,1024,384]{2,1,0:T(8,128)(2,1)} %get-tuple-element.57.dys, bf16[10,1024,1536]{2,1,0:T(8,128)(2,1)} %get-tuple-element.58.dgs, bf16[10,1024,768]{2,1,0:T(8,128)(2,1)} %get-tuple-element.59.hs), custom_call_target="tpu_custom_call" | custom-call | tf_op jit(solution)/shard_map/gradient_sums/pallas_call | solution.py:1297
  565.5 2.7 multiply_reduce_fusion
  568.2 0.6 pad_bitcast_fusion.1.router_t
  568.8 0.5 pad_bitcast_fusion.2.balance
  569.3 15.2 %mid_backward.1 = (f32[2048,384]{1,0:T(8,128)}, bf16[2,192,1024]{2,1,0:T(8,128)(2,1)}, f32[128,384]{1,0:T(8,128)}, f32[192,384]{1,0:T(8,128)}, f32[1,384]{1,0:T(1,128)}) custom-call(f32[2048,512]{1,0:T(8,128)} %get-tuple-element.61.part, f32[2048,384]{1,0:T(8,128)} %get-tuple-element.55.dx_ref.dx2, f32[2048,384]{1,0:T(8,128)} %get-tuple-element.54.x1, ...), custom_call_target="tpu_custom_call" | custom-call | tf_op jit(solution)/shard_map/mid_backward/pallas_call | solution.py:663
  584.5 44.9 %attend_backward.1 = (f32[576,384]{1,0:T(8,128)}, f32[2048,384]{1,0:T(8,128)}) custom-call(bf16[2,576,1024]{2,1,0:T(8,128)(2,1)} %get-tuple-element.60.qkv_ref, bf16[2,192,1024]{2,1,0:T(8,128)(2,1)} %get-tuple-element.63.do_ref, f32[2,8,1024]{2,1,0:T(8,128)} %get-tuple-element.64.lse_ref, bf16[2048,384]{1,0:T(8,128)(2,1)} %get-tuple-element.65.a_ref, ...), custom_call_target="tpu_custom_call" | custom-call | tf_op jit(solution)/shard_map/attend_backward/pallas_call | solution.py:217
  629.5 0.7 slice_bitcast_fusion.5
  630.6 9.9 %embed_backward.1 = f32[8,384]{1,0:T(8,128)} custom-call(f32[2048,384]{1,0:T(8,128)} %get-tuple-element.70.part, f32[2048,384]{1,0:T(8,128)} %get-tuple-element.71.dx1, f32[2,1,1024]{2,1,0:T(1,128)} %reshape.158.x_ref, f32[8,384]{1,0:T(8,128)} %maximum_maximum_fusion.rows_ref), custom_call_target="tpu_custom_call" | custom-call | tf_op jit(solution)/shard_map/embed_backward/pallas_call | solution.py:709
  640.4 0.7 slice.210
  641.1 0.7 slice.209
  641.9 0.8 concatenate.44
  643.1 1.2 pad.47.clone
  644.3 44.8 %reduce_rows.1 = f32[1,24,896]{2,1,0:T(8,128)} custom-call(f32[1,4,2,2,24,896]{5,4,3,2,1,0:T(8,128)} %bitcast.111), custom_call_target="tpu_custom_call" | custom-call | tf_op jit(solution)/shard_map/reduce_rows/pallas_call | solution.py:1017
  689.1 1.5 fusion.18
  691.9 1.3 fusion.35
  694.0 0.6 broadcast_in_dim.68.value
  694.6 8.9 %all_blocks.3 = f32[32,8,128]{2,1,0:T(8,128)} custom-call(f32[8,128]{1,0:T(8,128)} %broadcast_in_dim.68.value), custom_call_target="tpu_custom_call" | custom-call | tf_op jit(solution)/shard_map/all_blocks/pallas_call | solution.py:1060
  703.5 1.0 slice_reduce_fusion.1
  704.4 0.6 fusion.50
  706.5 0.9 slice_bitcast_fusion.4
  707.4 0.7 multiply_subtract_fusion.2
  708.1 1.5 multiply_subtract_fusion.3
  709.6 1.2 slice_multiply_fusion
  710.8 3.1 mul.324
  714.0 7.0 multiply_subtract_fusion
  721.1 1.6 multiply_subtract_fusion.1
  722.7 1.3 multiply_subtract_fusion.5
  724.3 0.8 multiply_subtract_fusion.4
  725.1 0.7 copy.114
  725.8 0.7 copy.115
  726.4 0.7 copy.116
  (125 shorter events, 4.6 us)
Async XLA Ops:
  4.5 4.0 copy-start.21
  4.7 4.5 copy-start.15
  4.8 4.5 copy-start.23
  4.8 5.2 copy-start.8
  4.8 5.2 copy-start.11
  4.8 5.2 copy-start.14
  4.8 5.2 copy-start.18
  81.8 11.3 %copy-start.3 = (f32[9,768,24]{1,2,0:T(8,128)S(1)}, f32[9,768,24]{1,2,0:T(8,128)}, u32[]{:S(2)}) copy-start(f32[9,768,24]{1,2,0:T(8,128)} %param.35) | copy-start | bytes 1990660
  81.8 11.4 %copy-start.1 = (f32[9,24,2,768]{3,2,1,0:T(2,128)S(1)}, f32[9,24,2,768]{3,2,1,0:T(2,128)}, u32[]{:S(2)}) copy-start(f32[9,24,2,768]{3,2,1,0:T(2,128)} %param.32) | copy-start | bytes 3981316
  232.0 52.9 %copy-start.22 = (s32[8]{0:T(128)S(1)}, s32[8]{0:T(128)}, u32[]{:S(2)}) copy-start(s32[8]{0:T(128)} %copy-done.21) | copy-start | bytes 100
  302.7 14.7 %copy-start.28 = (f32[1,128]{1,0:T(1,128)S(1)}, f32[1,128]{1,0:T(1,128)}, u32[]{:S(2)}) copy-start(f32[1,128]{1,0:T(1,128)} %get-tuple-element.75) | copy-start | bytes 1540
  584.5 45.7 %copy-start.10 = (f32[128,384]{1,0:T(8,128)S(1)}, f32[128,384]{1,0:T(8,128)}, u32[]{:S(2)}) copy-start(f32[128,384]{1,0:T(8,128)} %get-tuple-element.69) | copy-start | bytes 589828
  630.5 11.3 %copy-start.26 = (f32[1,384]{1,0:T(1,128)S(1)}, f32[1,384]{1,0:T(1,128)}, u32[]{:S(2)}) copy-start(f32[1,384]{1,0:T(1,128)} %get-tuple-element.73) | copy-start | bytes 4612
  630.5 11.3 %copy-start.27 = (f32[1,384]{1,0:T(1,128)S(1)}, f32[1,384]{1,0:T(1,128)}, u32[]{:S(2)}) copy-start(f32[1,384]{1,0:T(1,128)} %get-tuple-element.72) | copy-start | bytes 4612
  630.5 11.3 %copy-start.5 = (f32[576,384]{1,0:T(8,128)S(1)}, f32[576,384]{1,0:T(8,128)}, u32[]{:S(2)}) copy-start(f32[576,384]{1,0:T(8,128)} %get-tuple-element.66) | copy-start | bytes 2654212
  630.6 11.3 %copy-start.9 = (f32[192,384]{1,0:T(8,128)S(1)}, f32[192,384]{1,0:T(8,128)}, u32[]{:S(2)}) copy-start(f32[192,384]{1,0:T(8,128)} %get-tuple-element.67) | copy-start | bytes 884740
  643.1 64.3 %copy-start.12 = (f32[3,24,192]{2,1,0:T(8,128)S(1)}, f32[3,24,192]{2,1,0:T(8,128)}, u32[]{:S(2)}) copy-start(f32[3,24,192]{2,1,0:T(8,128)} %param.28) | copy-start | bytes 165892
  643.1 64.3 %copy-start.13 = (f32[3,24,192]{2,1,0:T(8,128)S(1)}, f32[3,24,192]{2,1,0:T(8,128)}, u32[]{:S(2)}) copy-start(f32[3,24,192]{2,1,0:T(8,128)} %param.27) | copy-start | bytes 165892
  644.3 63.8 %copy-start.16 = (f32[192,24]{0,1:T(8,128)S(1)}, f32[192,24]{0,1:T(8,128)}, u32[]{:S(2)}) copy-start(f32[192,24]{0,1:T(8,128)} %param.31) | copy-start | bytes 55300
  644.3 63.8 %copy-start.17 = (f32[192,24]{0,1:T(8,128)S(1)}, f32[192,24]{0,1:T(8,128)}, u32[]{:S(2)}) copy-start(f32[192,24]{0,1:T(8,128)} %param.30) | copy-start | bytes 55300
  644.3 65.3 %copy-start = (f32[9,24,2304]{2,1,0:T(8,128)S(1)}, f32[9,24,2304]{2,1,0:T(8,128)}, u32[]{:S(2)}) copy-start(f32[9,24,2304]{2,1,0:T(8,128)} %gradient_sums.1) | copy-start | bytes 5971972
  710.8 3.1 copy-start.2
  713.9 7.1 copy-start.4
  713.9 7.1 copy-start.6
  713.9 7.1 copy-start.7
  721.0 1.7 copy-start.19
  721.0 1.6 copy-start.20
  721.0 3.1 copy-start.24
  721.1 3.1 copy-start.25

commit v3 on v0

--- a/solution.py
+++ b/solution.py
@@ -1,12 +1,20 @@
+import functools
 import jax
 import jax.numpy as jnp
 from jax import lax
+from jax.experimental import pallas as pl
+from jax.experimental.pallas import tpu as pltpu
 from jax.sharding import PartitionSpec as P
 
 D = 384
 HEAD = 32
 ROUTED_EXPERTS = 8
-
+LANES = 128
+TILE = 256
+SHARD = 24
+ROUTER = 112
+SHARED = ROUTER + ROUTED_EXPERTS
+VECTOR = SHARED + 1
 
 horizons = (1, 8, 32, 64)
 quadratic_cutoff = 2.0
@@ -21,6 +29,1496 @@
 norm_eps = 1e-06
 rope_base = 10000.0
 
+F32 = jnp.float32
+BF16 = jnp.bfloat16
+I16 = jnp.int16
+MESH = pl.DeviceIdType.MESH
+VMEM = pl.BlockSpec(memory_space=pltpu.VMEM)
+ANY = pl.BlockSpec(memory_space=pl.ANY)
+DMA = pltpu.SemaphoreType.DMA
+
+
+def dot(a, b, da=1, db=0):
+    return lax.dot_general(a, b, (((da,), (db,)), ((), ())), preferred_element_type=F32)
+
+
+def params(megabytes=60, **more):
+    return pltpu.CompilerParams(vmem_limit_bytes=megabytes * 1024 * 1024, **more)
+
+
+def sigmoid(v):
+    return 1.0 / (1.0 + jnp.exp(-v))
+
+
+def block(index, size, step=8):
+    return pl.ds(pl.multiple_of(index * size, step), size)
+
+
+def place():
+    dp = lax.axis_index("dp")
+    return dp, lax.axis_index("mp"), lax.rem(dp, 2), lax.rem(dp // 2, 2), dp // 4
+
+
+def meet_everyone(dp, mp):
+    barrier = pltpu.get_barrier_semaphore()
+    me, n = dp * 2 + mp, 32
+
+    def signal(k, carry):
+        peer = lax.rem(me + k, n)
+        pl.semaphore_signal(barrier, inc=1, device_id=(peer // 2, lax.rem(peer, 2)), device_id_type=MESH)
+        return carry
+
+    lax.fori_loop(1, n, signal, 0)
+    pl.semaphore_wait(barrier, n - 1)
+
+
+def remote(src, dst, send, recv, dp, mp):
+    return pltpu.make_async_remote_copy(
+        src_ref=src, dst_ref=dst, send_sem=send, recv_sem=recv, device_id=(dp, mp), device_id_type=MESH)
+
+
+def done(view, sem):
+    pltpu.make_async_copy(view, view, sem).wait()
+
+
+def column(row, length):
+    return jnp.transpose(jnp.broadcast_to(row, (LANES, length)))
+
+
+def rotated(t, cos, sin):
+    half = HEAD // 2
+    front, back = t[:half], t[half:]
+    return jnp.concatenate([front * cos - back * sin, back * cos + front * sin], axis=0)
+
+
+def unrotated(t, cos, sin):
+    half = HEAD // 2
+    front, back = t[:half], t[half:]
+    return jnp.concatenate([front * cos + back * sin, back * cos - front * sin], axis=0)
+
+
+def score_block(k_rows, q_cols, low):
+    s = dot(k_rows, q_cols)
+    keys = lax.broadcasted_iota(jnp.int32, s.shape, 0)
+    queries = lax.broadcasted_iota(jnp.int32, s.shape, 1) + low
+    return jnp.where(keys <= queries, s, -1e30)
+
+
+def flip(t):
+    return jnp.transpose(t.astype(F32)).astype(BF16)
+
+
+def embed_piece(x_row, vec, x0_ref, a_ref, r):
+    xb = column(x_row, TILE)
+    cuts, square = [], None
+    for c in range(D // LANES):
+        cols = slice(c * LANES, (c + 1) * LANES)
+        u = xb * vec[3:4, cols]
+        v = u * sigmoid(u) * (xb * vec[4:5, cols])
+        x0_ref[r, cols] = v
+        square = v * v if square is None else square + v * v
+        cuts.append(v)
+    scale = lax.rsqrt(jnp.sum(square, axis=1, keepdims=True) / D + norm_eps)
+    for c in range(D // LANES):
+        cols = slice(c * LANES, (c + 1) * LANES)
+        a_ref[r, cols] = (cuts[c] * scale * vec[0:1, cols]).astype(BF16)
+
+
+def project_piece(wt, a, cos, sin, qkv, width):
+    for part in range(3):
+        t = dot(wt[part * width:(part + 1) * width, :], a, 1, 1)
+        for h in range(width // HEAD):
+            u = t[h * HEAD:(h + 1) * HEAD]
+            if part < 2:
+                u = rotated(u, cos, sin)
+            qkv[part * width + h * HEAD:part * width + (h + 1) * HEAD, :] = u.astype(BF16)
+
+
+def forward_head(h, width, qkv, lse, o):
+    length = qkv.shape[1]
+    scale = HEAD ** (-0.5)
+    q_rows = block(h, HEAD)
+    k_rows = pl.ds(pl.multiple_of(width + h * HEAD, HEAD), HEAD)
+    v_rows = pl.ds(pl.multiple_of(2 * width + h * HEAD, HEAD), HEAD)
+    k = flip(qkv[k_rows, :])
+    for j in range(length // TILE):
+        n = TILE * (j + 1)
+        cols = slice(j * TILE, (j + 1) * TILE)
+        s = score_block(k[:n], qkv[q_rows, cols], j * TILE)
+        peak = jnp.max(s, axis=0, keepdims=True)
+        e = jnp.exp((s - peak) * scale)
+        mass = jnp.sum(e, axis=0, keepdims=True)
+        weights = (e * (1.0 / mass)).astype(BF16)
+        o[q_rows, cols] = dot(qkv[v_rows, :n], weights).astype(BF16)
+        lse[pl.ds(h, 1), cols] = peak * scale + jnp.log(mass)
+
+
+def backward_head(h, width, qkv, do_t, lse, cos, sin, dqkv, dk_ref, dv_ref):
+    length = qkv.shape[1]
+    scale = HEAD ** (-0.5)
+    q_rows = block(h, HEAD)
+    k_rows = pl.ds(pl.multiple_of(width + h * HEAD, HEAD), HEAD)
+    v_rows = pl.ds(pl.multiple_of(2 * width + h * HEAD, HEAD), HEAD)
+    q, k, v, do = flip(qkv[q_rows, :]), flip(qkv[k_rows, :]), flip(qkv[v_rows, :]), flip(do_t[q_rows, :])
+    dk_ref[...] = jnp.zeros_like(dk_ref)
+    dv_ref[...] = jnp.zeros_like(dv_ref)
+    for j in range(length // TILE):
+        n = TILE * (j + 1)
+        cols = slice(j * TILE, (j + 1) * TILE)
+        s = score_block(k[:n], qkv[q_rows, cols], j * TILE)
+        w = jnp.exp(s * scale - lse[pl.ds(h, 1), cols])
+        dv_ref[:n] += dot(w.astype(BF16), do[cols])
+        dw = dot(v[:n], do_t[q_rows, cols])
+        mean = jnp.sum(w * dw, axis=0, keepdims=True)
+        ds = (w * (dw - mean) * scale).astype(BF16)
+        dk_ref[:n] += dot(ds, q[cols])
+        dq = dot(qkv[k_rows, :n], ds)
+        dqkv[q_rows, cols] = unrotated(dq, cos[:, cols], sin[:, cols]).astype(BF16)
+    dqkv[k_rows, :] = unrotated(jnp.transpose(dk_ref[...]), cos, sin).astype(BF16)
+    dqkv[v_rows, :] = jnp.transpose(dv_ref[...]).astype(BF16)
+
+
+def mid_forward_piece(x, gain, table):
+    scale = lax.rsqrt(jnp.mean(x * x, axis=1, keepdims=True) + norm_eps)
+    low = (x * scale * gain).astype(BF16)
+    logits = dot(low, table)
+    lanes = lax.broadcasted_iota(jnp.int32, logits.shape, 1)
+    routed = (lanes >= ROUTER) & (lanes < SHARED)
+    peak = jnp.max(jnp.where(routed, logits, -jnp.inf), axis=1, keepdims=True)
+    e = jnp.where(routed, jnp.exp(jnp.where(routed, logits - peak, 0.0)), 0.0)
+    probability = e / jnp.sum(e, axis=1, keepdims=True)
+    gates = jnp.where(lanes == SHARED, sigmoid(jnp.where(lanes == SHARED, logits, 0.0)), probability)
+    return low, gates, jnp.sum(probability, axis=0, keepdims=True)
+
+
+def embed_backward_piece(x_row, da, dx1, vec):
+    xb = column(x_row, TILE)
+    xb = jnp.concatenate([xb] * (D // LANES), axis=1)
+    u = xb * vec[3:4, :]
+    up = xb * vec[4:5, :]
+    s = sigmoid(u)
+    silu = u * s
+    x = silu * up
+    scale = lax.rsqrt(jnp.mean(x * x, axis=1, keepdims=True) + norm_eps)
+    unit = x * scale
+    dn = da * vec[0:1, :]
+    dx = dx1 + scale * (dn - unit * jnp.mean(dn * unit, axis=1, keepdims=True))
+    du = dx * up * (s * (1.0 + u * (1.0 - s)))
+    total = lambda v: jnp.sum(v, axis=0, keepdims=True)
+    return total(da * unit), total(du * xb), total(dx * silu * xb)
+
+
+def forward_kernel(
+    small_own, big_own, tally, x_ref, cos_ref, sin_ref,
+    big, wt, vec, table, a, qkv, lse, o, x1, b, pc, total, tallies,
+    stage, small, x0, part, other,
+    in_sem, own_sem, send_xy, send_up, send_dn, z_sem, p2_sem, p3_sem,
+    small_send, small_z, small_y, small_x, tally_send, tally_recv, pair_send, pair_recv,
+):
+    dp, mp, x, y, z = place()
+    xp, yp = dp + 1 - 2 * x, dp + 2 - 4 * y
+    count = big_own.shape[0]
+    series, _, length = x_ref.shape
+    width = o.shape[1]
+    per = length // TILE
+    load = pltpu.make_async_copy(big_own, stage, in_sem)
+    load.start()
+    meet_everyone(dp, mp)
+
+    def home(zs):
+        return zs * 4 + 2 * y + x
+
+    def small_put(src, slot, recv, peer):
+        remote(src, small.at[slot], small_send, recv, peer, mp).start()
+
+    for dist in (1, 2, 3):
+        @pl.when(z >= dist)
+        def _():
+            small_put(small_own, dp, small_z.at[z], dp - 4 * dist)
+
+        @pl.when(z + dist <= 3)
+        def _():
+            small_put(small_own, dp, small_z.at[z], dp + 4 * dist)
+    small_put(small_own, dp, small_y.at[z], yp)
+    small_put(small_own, dp, small_x, xp)
+    small[dp] = small_own[...]
+    me = dp * 2 + mp
+
+    def tell(k, carry):
+        peer = lax.rem(me + k, 32)
+        remote(tally, tallies.at[me], tally_send, tally_recv, peer // 2, lax.rem(peer, 2)).start()
+        return carry
+
+    lax.fori_loop(1, 32, tell, 0)
+    tallies[me] = tally[...]
+
+    load.wait()
+
+    def rows(c, slot):
+        return big.at[c, block(slot, SHARD), :]
+
+    def put(src, c, slot, send, recv, peer):
+        remote(src, rows(c, slot), send, recv, peer, mp).start()
+
+    def climb(c, zs, src):
+        put(src, c, home(zs), send_up, z_sem.at[c, zs], dp + 4)
+
+    def drop(c, zs, src):
+        put(src, c, home(zs), send_dn, z_sem.at[c, zs], dp - 4)
+
+    def ends(c):
+        k = lax.rem(c, 2)
+        return jnp.where(k == 0, yp, xp), jnp.where(k == 0, xp, yp)
+
+    def spread(c, zs, src):
+        first, second = ends(c)
+        put(src, c, home(zs), send_xy, p2_sem.at[c, zs], first)
+        put(src, c, home(zs), send_xy, p3_sem, second)
+
+    def own_z(c, carry):
+        @pl.when(z < 3)
+        def _():
+            climb(c, z, stage.at[c])
+
+        @pl.when(z > 0)
+        def _():
+            drop(c, z, stage.at[c])
+        pltpu.make_async_copy(stage.at[c], rows(c, dp), own_sem).start()
+        return carry
+
+    lax.fori_loop(0, count, own_z, 0)
+
+    for dist in (1, 2, 3):
+        for sign in (-1, 1):
+            zs = z + sign * dist
+
+            @pl.when((zs >= 0) & (zs <= 3))
+            def _():
+                done(small.at[home(zs)], small_z.at[zs])
+                small_put(small.at[home(zs)], home(zs), small_y.at[zs], yp)
+                small_put(small.at[home(zs)], home(zs), small_x, xp)
+    for turn in range(4):
+        zs = lax.rem(z + turn, 4)
+        slot = zs * 4 + 2 * (1 - y) + x
+        done(small.at[slot], small_y.at[zs])
+        small_put(small.at[slot], slot, small_x, xp)
+    done(small.at[pl.ds(0, 8)], small_x)
+
+    def own_xy(c, carry):
+        spread(c, z, stage.at[c])
+        return carry
+
+    lax.fori_loop(0, count, own_xy, 0)
+
+    whole = small[...].astype(F32).reshape(D, -1)
+    table[...] = whole[:, 4 * width:].astype(BF16)
+    turned = jnp.transpose(whole)
+    wt[...] = turned.astype(BF16)
+    vec[...] = jnp.concatenate(
+        [turned[4 * width + VECTOR:4 * width + VECTOR + 5], jnp.zeros((3, D), F32)], axis=0)
+    total[...] = jnp.zeros_like(total)
+
+    def relay(c, dist):
+        def second(zs):
+            k = lax.rem(c, 2)
+            slot = zs * 4 + jnp.where(k == 0, 2 * (1 - y) + x, 2 * y + 1 - x)
+            done(rows(c, slot), p2_sem.at[c, zs])
+            put(rows(c, slot), c, slot, send_xy, p3_sem, ends(c)[1])
+
+        @pl.when(z >= dist)
+        def _():
+            zs = z - dist
+            done(rows(c, home(zs)), z_sem.at[c, zs])
+
+            @pl.when(z < 3)
+            def _():
+                climb(c, zs, rows(c, home(zs)))
+            spread(c, zs, rows(c, home(zs)))
+
+        @pl.when(z + dist <= 3)
+        def _():
+            zs = z + dist
+            done(rows(c, home(zs)), z_sem.at[c, zs])
+
+            @pl.when(z > 0)
+            def _():
+                drop(c, zs, rows(c, home(zs)))
+            spread(c, zs, rows(c, home(zs)))
+
+        @pl.when(z - (dist - 1) >= 0)
+        def _():
+            second(z - (dist - 1))
+
+        @pl.when((dist > 1) & (z + dist - 1 <= 3))
+        def _():
+            second(z + dist - 1)
+
+    def pair(n):
+        r = block(n, length)
+        return remote(part.at[r], other.at[r], pair_send.at[n], pair_recv.at[n], dp, 1 - mp)
+
+    heads = width // HEAD
+    pieces = heads + 2
+
+    def attention(i):
+        n, j = i // pieces, lax.rem(i, pieces)
+        r = block(n, length)
+
+        @pl.when(j == 0)
+        def _():
+            def tile(m, carry):
+                t = pl.ds(pl.multiple_of(n * length + m * TILE, TILE), TILE)
+                embed_piece(x_ref[n, :, block(m, TILE, TILE)], vec, x0, a, t)
+                return carry
+            lax.fori_loop(0, per, tile, 0)
+
+        @pl.when(j == 1)
+        def _():
+            project_piece(wt, a[r, :], cos_ref[...], sin_ref[...], qkv.at[n], width)
+
+        @pl.when(j >= 2)
+        def _():
+            forward_head(j - 2, width, qkv.at[n], lse.at[n], o.at[n])
+
+        @pl.when(j == pieces - 1)
+        def _():
+            part[r, :] = dot(o[n], wt[3 * width:4 * width, :], 0, 0)
+            pair(n).start()
+
+    def middle(m):
+        r = block(m, TILE)
+
+        @pl.when(lax.rem(m, per) == 0)
+        def _():
+            pair(m // per).wait()
+        v = x0[r, :] + (part[r, :] + other[r, :])
+        x1[r, :] = v
+        low, gates, sums = mid_forward_piece(v, vec[1:2, :], table[...])
+        b[r, :] = low
+        pc[r, :] = gates
+        total[...] += sums
+
+    def step(i, carry):
+        relay(lax.rem(i, count), i // count + 1)
+
+        @pl.when(i < series * pieces)
+        def _():
+            attention(i)
+
+        for n in range(series):
+            begin = (n + 1) * pieces + 4
+
+            @pl.when((i >= begin) & (i < begin + per))
+            def _():
+                middle(n * per + i - begin)
+        return carry
+
+    lax.fori_loop(0, 4 * count, step, 0)
+
+    def whole_wait(n, sem):
+        done(big.at[:, pl.ds(0, n * SHARD), :], sem)
+    whole_wait(8, p3_sem)
+    whole_wait(12, send_xy)
+    whole_wait(1, own_sem)
+    done(small.at[pl.ds(0, 15)], small_send)
+    done(tallies.at[pl.ds(0, 31)], tally_recv)
+    done(tallies.at[pl.ds(0, 31)], tally_send)
+    for k in range(4):
+        @pl.when(z == k)
+        def _():
+            if k < 3:
+                whole_wait(k + 1, send_up)
+            if k > 0:
+                whole_wait(4 - k, send_dn)
+
+
+def forward_near(small_own, big_own, tally, x, cos, sin, width, ident):
+    series, _, length = x.shape
+    tokens = series * length
+    count, shard, columns = big_own.shape
+    shape = jax.ShapeDtypeStruct
+    return pl.pallas_call(
+        forward_kernel,
+        in_specs=[VMEM, ANY, VMEM, VMEM, VMEM, VMEM],
+        out_specs=[ANY] + [VMEM] * 12,
+        out_shape=[
+            shape((count, D, columns), BF16),
+            shape((small_own.shape[1], D), BF16), shape((8, D), F32), shape((D, LANES), BF16),
+            shape((tokens, D), BF16), shape((series, 3 * width, length), BF16), shape((series, 8, length), F32),
+            shape((series, width, length), BF16),
+            shape((tokens, D), F32), shape((tokens, D), BF16), shape((tokens, LANES), F32), shape((1, LANES), F32),
+            shape((32,) + tally.shape, F32),
+        ],
+        scratch_shapes=[
+            pltpu.VMEM(big_own.shape, BF16), pltpu.VMEM((16,) + small_own.shape, BF16),
+            pltpu.VMEM((tokens, D), F32), pltpu.VMEM((tokens, D), F32), pltpu.VMEM((tokens, D), F32),
+            DMA, DMA, DMA, DMA, DMA, DMA((count, 4)), DMA((count, 4)), DMA,
+            DMA, DMA((4,)), DMA((4,)), DMA, DMA, DMA, DMA((series,)), DMA((series,)),
+        ],
+        compiler_params=params(collective_id=ident, has_side_effects=True),
+        name="forward_near",
+    )(small_own, big_own, tally, x, cos, sin)
+
+
+GROUP = 16
+
+
+def spread_rows(dest, value, start, count):
+    for c in range(value.shape[1] // LANES):
+        dest[pl.ds(start * 8 + c, count, stride=8), :] = value[:, c * LANES:(c + 1) * LANES]
+
+
+def pick_rows(source, tile, index_ref, base):
+    def body(i, carry):
+        values = []
+        for k in range(GROUP):
+            t = index_ref[base + i * GROUP + k]
+            values.append(source[pl.ds(pl.multiple_of(t * 8, 8), 8), :])
+        for k in range(GROUP):
+            tile[pl.ds(pl.multiple_of((i * GROUP + k) * 8, 8), 8), :] = values[k]
+        return carry
+
+    lax.fori_loop(0, TILE // GROUP, body, 0)
+
+
+def add_rows(dest, tile, index_ref, base):
+    def body(i, carry):
+        places, values = [], []
+        for k in range(GROUP):
+            t = index_ref[base + i * GROUP + k]
+            place = pl.ds(pl.multiple_of(t * 8, 8), 8)
+            places.append(place)
+            values.append(dest[place, :] + tile[pl.ds(pl.multiple_of((i * GROUP + k) * 8, 8), 8), :])
+        for k in range(GROUP):
+            dest[places[k], :] = values[k]
+        return carry
+
+    lax.fori_loop(0, TILE // GROUP, body, 0)
+
+
+def gathered_columns(tile, columns):
+    return [tile[pl.ds(c, TILE, stride=8), :] for c in range(columns)]
+
+
+def lane_of(block, lane):
+    lanes = lax.broadcasted_iota(jnp.int32, block.shape, 1)
+    return jnp.sum(jnp.where(lanes == lane, block, 0.0), axis=1, keepdims=True)
+
+
+def lay_rows(values, pc_ref, rows8, acc8):
+    tokens = values.shape[0]
+
+    def lay(i, carry):
+        r = pl.ds(pl.multiple_of(i * TILE, TILE), TILE)
+        spread_rows(rows8, values[r, :].astype(F32), i * TILE, TILE)
+        rows8[pl.ds(i * TILE * 8 + 3, TILE, stride=8), :] = pc_ref[r, :]
+        acc8[pl.ds(pl.multiple_of(i * TILE * 8, 8), TILE * 8), :] = jnp.zeros((TILE * 8, LANES), F32)
+        return carry
+
+    lax.fori_loop(0, tokens // TILE, lay, 0)
+    rows8[pl.ds(tokens * 8, 8), :] = jnp.zeros((8, LANES), F32)
+    acc8[pl.ds(tokens * 8, 8), :] = jnp.zeros((8, LANES), F32)
+
+
+def expert_forward_kernel(counts, source, b_ref, pc_ref, w_ref, x_ref, y_ref, mix_ref, rows8, acc8, tile8):
+    e = pl.program_id(0)
+    hidden = w_ref.shape[2] // 3
+    capacity = y_ref.shape[1]
+    tiles = capacity // TILE
+
+    @pl.when(e == 0)
+    def _():
+        lay_rows(b_ref, pc_ref, rows8, acc8)
+
+    def run(x):
+        g = dot(x, w_ref[0, :, : 2 * hidden])
+        gate, up = g[:, :hidden], g[:, hidden:]
+        h = (gate * sigmoid(gate) * up).astype(BF16)
+        return dot(h, w_ref[0, :, 2 * hidden:], 1, 1)
+
+    @pl.when(e < ROUTED_EXPERTS)
+    def _():
+        used = (counts[e] + TILE - 1) // TILE
+
+        def step(i, carry):
+            base = e * capacity + i * TILE
+            r = pl.ds(pl.multiple_of(i * TILE, TILE), TILE)
+            pick_rows(rows8, tile8, source, base)
+            c0, c1, c2, pc = gathered_columns(tile8, 4)
+            x = jnp.concatenate([c0, c1, c2], axis=1).astype(BF16)
+            x_ref[0, r, :] = x
+            y = run(x)
+            y_ref[0, r, :] = y
+            spread_rows(tile8, y * lane_of(pc, ROUTER + e), 0, TILE)
+            add_rows(acc8, tile8, source, base)
+            return carry
+
+        def blank(i, carry):
+            x_ref[0, pl.ds(pl.multiple_of(i * TILE, TILE), TILE), :] = jnp.zeros((TILE, D), BF16)
+            return carry
+
+        lax.fori_loop(0, used, step, 0)
+        lax.fori_loop(used, tiles, blank, 0)
+
+    @pl.when(e >= ROUTED_EXPERTS)
+    def _():
+        def step(i, carry):
+            t = (e - ROUTED_EXPERTS) * tiles + i
+            here = pl.ds(pl.multiple_of(i * TILE, TILE), TILE)
+            r = pl.ds(pl.multiple_of(t * TILE, TILE), TILE)
+            x = b_ref[r, :]
+            x_ref[0, here, :] = x
+            y = run(x)
+            y_ref[0, here, :] = y
+            shared = y * lane_of(pc_ref[r, :], SHARED)
+            for c in range(D // LANES):
+                cols = slice(c * LANES, (c + 1) * LANES)
+                mix_ref[r, cols] = acc8[pl.ds(t * TILE * 8 + c, TILE, stride=8), :] + shared[:, cols]
+            return carry
+
+        lax.fori_loop(0, tiles, step, 0)
+
+
+def expert_blocks(capacity, w):
+    return pl.BlockSpec((1, capacity, w), lambda e, *_: (e, 0, 0))
+
+
+def expert_weights(weights):
+    return pl.BlockSpec((1,) + weights.shape[1:], lambda e, *_: (jnp.minimum(e, ROUTED_EXPERTS), 0, 0))
+
+
+def expert_scratch(tokens):
+    return [
+        pltpu.VMEM(((tokens + 1) * 8, LANES), F32),
+        pltpu.VMEM(((tokens + 1) * 8, LANES), F32),
+        pltpu.VMEM((TILE * 8, LANES), F32),
+    ]
+
+
+def expert_forward(counts, source, b, pc, weights):
+    tokens = b.shape[0]
+    capacity = tokens // 2
+    blocks = ROUTED_EXPERTS + 2
+    full = lambda shape: pl.BlockSpec(shape, lambda e, *_: (0,) * len(shape), pipeline_mode=pl.Buffered(1))
+    return pl.pallas_call(
+        expert_forward_kernel,
+        grid_spec=pltpu.PrefetchScalarGridSpec(
+            num_scalar_prefetch=2,
+            grid=(blocks,),
+            in_specs=[full(b.shape), full(pc.shape), expert_weights(weights)],
+            out_specs=[expert_blocks(capacity, D), expert_blocks(capacity, D), full((tokens, D))],
+            scratch_shapes=expert_scratch(tokens),
+        ),
+        out_shape=[
+            jax.ShapeDtypeStruct((blocks, capacity, D), BF16),
+            jax.ShapeDtypeStruct((blocks, capacity, D), F32),
+            jax.ShapeDtypeStruct((tokens, D), F32),
+        ],
+        compiler_params=params(),
+        name="expert_forward",
+    )(counts, source, b, pc, weights)
+
+
+def expert_backward_kernel(
+    counts, source, pc_ref, dx_ref, w_ref, x_ref, y_ref, dy_ref, dg_ref, h_ref, acc_ref, rows8, acc8, tile8
+):
+    e = pl.program_id(0)
+    hidden = w_ref.shape[2] // 3
+    capacity = y_ref.shape[1]
+    tiles = capacity // TILE
+
+    @pl.when(e == 0)
+    def _():
+        lay_rows(dx_ref, pc_ref, rows8, acc8)
+
+    def run(r, dy):
+        x = x_ref[0, r, :]
+        dy_ref[0, r, :] = dy
+        u = w_ref[0, :, : 2 * hidden]
+        g = dot(x, u)
+        gate, up = g[:, :hidden], g[:, hidden:]
+        s = sigmoid(gate)
+        silu = gate * s
+        h_ref[0, r, :] = (silu * up).astype(BF16)
+        dh = dot(dy, w_ref[0, :, 2 * hidden:])
+        d_up = (dh * silu).astype(BF16)
+        d_gate = (dh * up * (s * (1.0 + gate * (1.0 - s)))).astype(BF16)
+        dg_ref[0, r, :hidden] = d_gate
+        dg_ref[0, r, hidden:] = d_up
+        return dot(d_gate, u[:, :hidden], 1, 1) + dot(d_up, u[:, hidden:], 1, 1)
+
+    lanes = lax.broadcasted_iota(jnp.int32, (TILE, LANES), 1)
+
+    @pl.when(e < ROUTED_EXPERTS)
+    def _():
+        used = (counts[e] + TILE - 1) // TILE
+
+        def step(i, carry):
+            base = e * capacity + i * TILE
+            r = pl.ds(pl.multiple_of(i * TILE, TILE), TILE)
+            pick_rows(rows8, tile8, source, base)
+            c0, c1, c2, pc = gathered_columns(tile8, 4)
+            dx = jnp.concatenate([c0, c1, c2], axis=1)
+            d_gate = jnp.sum(y_ref[0, r, :] * dx, axis=1, keepdims=True)
+            back = run(r, (dx * lane_of(pc, ROUTER + e)).astype(BF16))
+            spread_rows(tile8, back, 0, TILE)
+            tile8[pl.ds(3, TILE, stride=8), :] = jnp.where(lanes == ROUTER + e, d_gate, 0.0)
+            add_rows(acc8, tile8, source, base)
+            return carry
+
+        def blank(i, carry):
+            r = pl.ds(pl.multiple_of(i * TILE, TILE), TILE)
+            dy_ref[0, r, :] = jnp.zeros((TILE, D), BF16)
+            dg_ref[0, r, :] = jnp.zeros((TILE, 2 * hidden), BF16)
+            h_ref[0, r, :] = jnp.zeros((TILE, hidden), BF16)
+            return carry
+
+        lax.fori_loop(0, used, step, 0)
+        lax.fori_loop(used, tiles, blank, 0)
+
+    @pl.when(e >= ROUTED_EXPERTS)
+    def _():
+        def step(i, carry):
+            t = (e - ROUTED_EXPERTS) * tiles + i
+            here = pl.ds(pl.multiple_of(i * TILE, TILE), TILE)
+            r = pl.ds(pl.multiple_of(t * TILE, TILE), TILE)
+            dx = dx_ref[r, :]
+            d_gate = jnp.sum(y_ref[0, here, :] * dx, axis=1, keepdims=True)
+            back = run(here, (dx * lane_of(pc_ref[r, :], SHARED)).astype(BF16))
+            for c in range(D // LANES):
+                cols = slice(c * LANES, (c + 1) * LANES)
+                acc_ref[r, cols] = acc8[pl.ds(t * TILE * 8 + c, TILE, stride=8), :] + back[:, cols]
+            acc_ref[r, D:] = jnp.where(
+                lanes == SHARED, d_gate, acc8[pl.ds(t * TILE * 8 + 3, TILE, stride=8), :])
+            return carry
+
+        lax.fori_loop(0, tiles, step, 0)
+
+
+def expert_backward(counts, source, pc, dx, weights, x, y):
+    tokens = dx.shape[0]
+    capacity = tokens // 2
+    blocks = ROUTED_EXPERTS + 2
+    hidden = weights.shape[2] // 3
+    full = lambda shape: pl.BlockSpec(shape, lambda e, *_: (0,) * len(shape), pipeline_mode=pl.Buffered(1))
+    return pl.pallas_call(
+        expert_backward_kernel,
+        grid_spec=pltpu.PrefetchScalarGridSpec(
+            num_scalar_prefetch=2,
+            grid=(blocks,),
+            in_specs=[
+                full(pc.shape), full(dx.shape), expert_weights(weights),
+                expert_blocks(capacity, D), expert_blocks(capacity, D)],
+            out_specs=[
+                expert_blocks(capacity, D), expert_blocks(capacity, 2 * hidden), expert_blocks(capacity, hidden),
+                full((tokens, D + LANES))],
+            scratch_shapes=expert_scratch(tokens),
+        ),
+        out_shape=[
+            jax.ShapeDtypeStruct((blocks, capacity, D), BF16),
+            jax.ShapeDtypeStruct((blocks, capacity, 2 * hidden), BF16),
+            jax.ShapeDtypeStruct((blocks, capacity, hidden), BF16),
+            jax.ShapeDtypeStruct((tokens, D + LANES), F32),
+        ],
+        compiler_params=params(),
+        name="expert_backward",
+    )(counts, source, pc, dx, weights, x, y)
+
+
+def exchange(part, other, send_sem, recv_sem):
+    dp, mp = lax.axis_index("dp"), lax.axis_index("mp")
+    barrier = pltpu.get_barrier_semaphore()
+    pl.semaphore_signal(barrier, inc=1, device_id=(dp, 1 - mp), device_id_type=MESH)
+    pl.semaphore_wait(barrier, 1)
+
+    def copy(i):
+        r = block(i, TILE)
+        return remote(part.at[r], other.at[r], send_sem.at[i], recv_sem.at[i], dp, 1 - mp)
+
+    def begin(i, carry):
+        copy(i).start()
+        return carry
+
+    lax.fori_loop(0, part.shape[0] // TILE, begin, 0)
+    return lambda i: copy(i).wait()
+
+
+def exchange_scratch(part):
+    tiles = part.shape[0] // TILE
+    return [pltpu.VMEM(part.shape, F32), DMA((tiles,)), DMA((tiles,))]
+
+
+def hankel(base):
+    block_rows = jnp.broadcast_to(base, (LANES, 2 * LANES))
+    m = pltpu.roll(block_rows, 0, 1, stride=1, stride_axis=0)[:, :LANES]
+    lanes = lax.broadcasted_iota(jnp.int32, (LANES, LANES), 1)
+    out = pltpu.roll(m, 41, 1)
+    out = jnp.where(lanes < 104, pltpu.roll(m, 40, 1), out)
+    out = jnp.where(lanes < 96, pltpu.roll(m, 32, 1), out)
+    return jnp.where(lanes < 64, m, out)
+
+
+def loss_piece(x, gain, table, table_t, value_rows, mark_rows, weight):
+    scale = lax.rsqrt(jnp.mean(x * x, axis=1, keepdims=True) + norm_eps)
+    unit = x * scale
+    low = (unit * gain).astype(BF16)
+    z = dot(low, table)
+    target = jnp.concatenate([hankel(row) for row in value_rows], axis=0)
+    valid = jnp.concatenate([hankel(row) for row in mark_rows], axis=0)
+    factor = valid * weight
+    miss = z - target
+    size = jnp.abs(miss)
+    huber = jnp.where(
+        size <= quadratic_cutoff, 0.5 * miss * miss, quadratic_cutoff * (size - 0.5 * quadratic_cutoff))
+    dz = (jnp.clip(miss, -quadratic_cutoff, quadratic_cutoff) * factor).astype(BF16)
+    df = dot(dz, table_t)
+    dn = df * gain
+    dx = scale * (dn - unit * jnp.mean(dn * unit, axis=1, keepdims=True))
+    total = lambda v: jnp.sum(v, axis=0, keepdims=True)
+    return dx, dot(dz, low, 0, 0), total(df * unit), total(huber * factor)
+
+
+def loss_kernel(part, x1, vec, table, table_t, values, marks, weight, dx2, d_table, d_gain, loss,
+                other, send_sem, recv_sem):
+    wait = exchange(part, other, send_sem, recv_sem)
+    d_table[...] = jnp.zeros_like(d_table)
+    d_gain[...] = jnp.zeros_like(d_gain)
+    loss[...] = jnp.zeros_like(loss)
+    per = TILE // LANES
+
+    def step(i, carry):
+        r = block(i, TILE)
+        wait(i)
+        dx, dt, dg, fit = loss_piece(
+            x1[r, :] + (part[r, :] + other[r, :]), vec[2:3, :], table[...], table_t[...],
+            [values[pl.ds(per * i + k, 1), :] for k in range(per)],
+            [marks[pl.ds(per * i + k, 1), :] for k in range(per)], weight[...])
+        dx2[r, :] = dx
+        d_table[...] += dt
+        d_gain[...] += dg
+        loss[...] += fit
+        return carry
+
+    lax.fori_loop(0, part.shape[0] // TILE, step, 0)
+
+
+def loss_stage(part, x1, vec, table, table_t, values, marks, weight, ident):
+    tokens = part.shape[0]
+    return pl.pallas_call(
+        loss_kernel,
+        in_specs=[VMEM] * 8,
+        out_specs=[VMEM] * 4,
+        out_shape=[
+            jax.ShapeDtypeStruct((tokens, D), F32), jax.ShapeDtypeStruct((LANES, D), F32),
+            jax.ShapeDtypeStruct((1, D), F32), jax.ShapeDtypeStruct((1, LANES), F32),
+        ],
+        scratch_shapes=exchange_scratch(part),
+        compiler_params=params(collective_id=ident, has_side_effects=True),
+        name="loss_stage",
+    )(part, x1, vec, table, table_t, values, marks, weight)
+
+
+def mid_backward_kernel(part, dx2, x1, b, pc, vec, table_t, balance, wo, o, d_table, d_gain3, dx1, do, rest,
+                        other, send_sem, recv_sem):
+    wait = exchange(part, other, send_sem, recv_sem)
+    width = wo.shape[0]
+    rest[:width, :] = jnp.zeros((width, D), F32)
+    rest[width:, :] = d_table[...]
+    rest[width + VECTOR + 2:width + VECTOR + 3, :] = d_gain3[...]
+    per = o.shape[2] // TILE
+
+    def step(i, carry):
+        r = block(i, TILE)
+        wait(i)
+        dp = part[r, D:] + other[r, D:] + balance[...]
+        p = pc[r, :]
+        lanes = lax.broadcasted_iota(jnp.int32, p.shape, 1)
+        routed = (lanes >= ROUTER) & (lanes < SHARED)
+        weighted = jnp.sum(jnp.where(routed, p * dp, 0.0), axis=1, keepdims=True)
+        dl = jnp.where(routed, p * (dp - weighted), jnp.where(lanes == SHARED, dp * p * (1.0 - p), 0.0))
+        dl = dl.astype(BF16)
+        low = b[r, :]
+        rest[width:, :] += dot(dl, low, 0, 0)
+        db = part[r, :D] + other[r, :D] + dot(dl, table_t[...])
+        x = x1[r, :]
+        scale = lax.rsqrt(jnp.mean(x * x, axis=1, keepdims=True) + norm_eps)
+        unit = x * scale
+        g2 = width + VECTOR + 1
+        rest[g2:g2 + 1, :] += jnp.sum(db * unit, axis=0, keepdims=True)
+        dn = db * vec[1:2, :]
+        dx = dx2[r, :] + scale * (dn - unit * jnp.mean(dn * unit, axis=1, keepdims=True))
+        dx1[r, :] = dx
+        d_low = dx.astype(BF16)
+        n, cols = i // per, block(lax.rem(i, per), TILE, TILE)
+        do[n, :, cols] = dot(wo[...], d_low, 1, 1).astype(BF16)
+        rest[:width, :] += dot(o[n, :, cols], d_low)
+        return carry
+
+    lax.fori_loop(0, part.shape[0] // TILE, step, 0)
+
+
+def mid_backward(part, dx2, x1, b, pc, vec, table_t, balance, wo, o, d_table, d_gain3, ident):
+    tokens = part.shape[0]
+    return pl.pallas_call(
+        mid_backward_kernel,
+        in_specs=[VMEM] * 12,
+        out_specs=[VMEM] * 3,
+        out_shape=[
+            jax.ShapeDtypeStruct((tokens, D), F32), jax.ShapeDtypeStruct(o.shape, BF16),
+            jax.ShapeDtypeStruct((wo.shape[0] + LANES, D), F32),
+        ],
+        scratch_shapes=exchange_scratch(part),
+        compiler_params=params(collective_id=ident, has_side_effects=True),
+        name="mid_backward",
+    )(part, dx2, x1, b, pc, vec, table_t, balance, wo, o, d_table, d_gain3)
+
+
+SLOTS = 3
+HOPS = 2
+ACCS = 5
+
+
+def encode(dest, v):
+    width = v.shape[1]
+    top = jnp.max(jnp.abs(v), axis=1, keepdims=True)
+    power = jnp.ceil(jnp.log2(jnp.maximum(top, 1e-30) * (1.001 / 32767.0)))
+    power = jnp.broadcast_to(power, (v.shape[0], LANES))
+    inverse = jnp.exp2(-power)
+    dest[:, width:] = power.astype(jnp.int32).astype(I16)
+    for c in range(width // LANES):
+        cols = slice(c * LANES, (c + 1) * LANES)
+        dest[:, cols] = jnp.round(v[:, cols] * inverse).astype(jnp.int32).astype(I16)
+
+
+def decode(source):
+    width = source.shape[1] - LANES
+    unit = jnp.exp2(source[:, width:].astype(jnp.int32).astype(F32))
+    return jnp.concatenate(
+        [source[:, c * LANES:(c + 1) * LANES].astype(jnp.int32).astype(F32) * unit for c in range(width // LANES)],
+        axis=1)
+
+
+def backward_kernel(
+    xs, dys, dgs, hs, qkvs, dos, lses, a_all, dx1_all, rest, x_ref, wt, vec, cos_ref, sin_ref,
+    out, out_small,
+    x_in, dy_in, dg_in, h_in, xt, dyt, temp, dw, acc, send1, recv1, send2, recv2, zs_up, zs_dn, up, dn,
+    qkv, do_t, lse, a, dx1, dqkv, dk, dv, stack, part, other,
+    sm, small_a1, small_b1, small_a2, small_b2, small_up, small_dn,
+    load_sem, sem_s1, sem_r1, sem_s2, sem_r2, sem_su, sem_sd, sem_ru, sem_rd,
+    attn_sem, dx1_sem, rest_sem, pair_send, pair_recv,
+    small_send, small_sa, small_sb, small_r, small_su, small_sd, small_ru, small_rd,
+):
+    dp, mp, x, y, z = place()
+    xp, yp = dp + 1 - 2 * x, dp + 2 - 4 * y
+    count = out.shape[0]
+    blocks = xs.shape[0]
+    hidden = hs.shape[2]
+    series, _, length = x_ref.shape
+    width = do_t.shape[0]
+    heads = width // HEAD
+    per = length // TILE
+
+    def loads(n):
+        return [
+            pltpu.make_async_copy(src.at[n], dst, load_sem.at[i])
+            for i, (src, dst) in enumerate(((xs, x_in), (dys, dy_in), (dgs, dg_in), (hs, h_in)))]
+
+    def attn_loads(n):
+        pairs = ((qkvs.at[n], qkv), (dos.at[n], do_t), (lses.at[n], lse), (a_all.at[block(n, length)], a))
+        return [pltpu.make_async_copy(src, dst, attn_sem.at[i]) for i, (src, dst) in enumerate(pairs)]
+
+    def dx1_load(n):
+        return pltpu.make_async_copy(dx1_all.at[block(n, length)], dx1, dx1_sem)
+
+    rest_load = pltpu.make_async_copy(rest, stack.at[pl.ds(3 * width, width + LANES)], rest_sem)
+    for copy in loads(0) + attn_loads(0) + [dx1_load(0), rest_load]:
+        copy.start()
+
+    barrier = pltpu.get_barrier_semaphore()
+    for peer, core in ((xp, mp), (yp, mp), (dp, 1 - mp)):
+        pl.semaphore_signal(barrier, inc=1, device_id=(peer, core), device_id_type=MESH)
+
+    @pl.when(z > 0)
+    def _():
+        pl.semaphore_signal(barrier, inc=1, device_id=(dp - 4, mp), device_id_type=MESH)
+
+    @pl.when(z < 3)
+    def _():
+        pl.semaphore_signal(barrier, inc=1, device_id=(dp + 4, mp), device_id_type=MESH)
+
+    @pl.when((z > 0) & (z < 3))
+    def _():
+        pl.semaphore_wait(barrier, 5)
+
+    @pl.when((z == 0) | (z == 3))
+    def _():
+        pl.semaphore_wait(barrier, 4)
+
+    stack[0:3 * width, :] = jnp.zeros((3 * width, D), F32)
+
+    def shard(slot, i):
+        return dw.at[slot, i]
+
+
+    def weights(n, more):
+        for copy in loads(n):
+            copy.wait()
+        xt[...] = jnp.transpose(x_in[...])
+        dyt[...] = jnp.transpose(dy_in[...])
+
+        def wide(j, carry):
+            cols = block(j, TILE, TILE)
+            v = dot(xt[...], dg_in[:, cols])
+            temp[:, cols] = temp[:, cols] + v if more else v
+            return carry
+
+        def tall(j, carry):
+            there = pl.ds(pl.multiple_of(2 * hidden + j * TILE, TILE), TILE)
+            v = dot(dyt[...], h_in[:, block(j, TILE, TILE)])
+            temp[:, there] = temp[:, there] + v if more else v
+            return carry
+
+        lax.fori_loop(0, 2 * hidden // TILE, wide, 0)
+        lax.fori_loop(0, hidden // TILE, tall, 0)
+
+        @pl.when(n + 1 < blocks)
+        def _():
+            for copy in loads(n + 1):
+                copy.start()
+
+    def begin(c):
+        k, slot = lax.rem(c, 2), lax.rem(c, SLOTS)
+        weights(c, False)
+
+        @pl.when(c == count - 1)
+        def _():
+            weights(c + 1, True)
+
+        @pl.when(c >= SLOTS)
+        def _():
+            done(send1.at[slot], sem_s1.at[slot])
+
+        def pack(i, carry):
+            m, n = i // 2, lax.rem(i, 2)
+            gone = m * 4 + jnp.where(k == 0, n * 2 + 1 - x, (1 - y) * 2 + n)
+            kept = m * 4 + jnp.where(k == 0, n * 2 + x, y * 2 + n)
+            encode(send1.at[slot, i], temp[block(gone, SHARD), :])
+            dw[slot, i] = temp[block(kept, SHARD), :]
+            return carry
+
+        lax.fori_loop(0, 8, pack, 0)
+        remote(send1.at[slot], recv1.at[c], sem_s1.at[slot], sem_r1.at[c], jnp.where(k == 0, xp, yp), mp).start()
+
+    def fold(c):
+        k, slot, hop = lax.rem(c, 2), lax.rem(c, SLOTS), lax.rem(c, HOPS)
+        o = jnp.where(k == 0, y, x)
+        done(recv1.at[c], sem_r1.at[c])
+
+        @pl.when(c >= HOPS)
+        def _():
+            done(send2.at[hop], sem_s2.at[hop])
+
+        def add(m, carry):
+            gone, kept = m * 2 + 1 - o, m * 2 + o
+            encode(send2.at[hop, m], dw[slot, gone] + decode(recv1.at[c, gone]))
+            acc[lax.rem(c, ACCS), m] = dw[slot, kept] + decode(recv1.at[c, kept])
+            return carry
+
+        lax.fori_loop(0, 4, add, 0)
+        remote(send2.at[hop], recv2.at[c], sem_s2.at[hop], sem_r2.at[c], jnp.where(k == 0, yp, xp), mp).start()
+
+    def climb(c, t, relay):
+        slot = lax.rem(c, HOPS)
+        v = acc[lax.rem(c, ACCS), t]
+        if relay:
+            done(up.at[c, t - 1], sem_ru.at[c, t - 1])
+            v = v + decode(up.at[c, t - 1])
+
+        @pl.when(c >= HOPS)
+        def _():
+            done(zs_up.at[slot, t - 1], sem_su.at[slot, t - 1])
+        encode(zs_up.at[slot, t - 1], v)
+        remote(zs_up.at[slot, t - 1], up.at[c, t - 1], sem_su.at[slot, t - 1], sem_ru.at[c, t - 1], dp + 4, mp).start()
+
+    def drop(c, t, relay):
+        slot = lax.rem(c, HOPS)
+        v = acc[lax.rem(c, ACCS), t]
+        if relay:
+            done(dn.at[c, t], sem_rd.at[c, t])
+            v = v + decode(dn.at[c, t])
+
+        @pl.when(c >= HOPS)
+        def _():
+            done(zs_dn.at[slot, t], sem_sd.at[slot, t])
+        encode(zs_dn.at[slot, t], v)
+        remote(zs_dn.at[slot, t], dn.at[c, t], sem_sd.at[slot, t], sem_rd.at[c, t], dp - 4, mp).start()
+
+    def line_a(c):
+        done(recv2.at[c], sem_r2.at[c])
+        there = lax.rem(c, ACCS)
+
+        def add(m, carry):
+            acc[there, m] = acc[there, m] + decode(recv2.at[c, m])
+            return carry
+
+        lax.fori_loop(0, 4, add, 0)
+        out[c] = acc[there, z]
+
+        @pl.when(z == 0)
+        def _():
+            for t in (3, 2, 1):
+                climb(c, t, False)
+
+        @pl.when(z == 3)
+        def _():
+            for t in (0, 1, 2):
+                drop(c, t, False)
+
+    def line_b(c):
+        @pl.when(z == 1)
+        def _():
+            for t in (3, 2):
+                climb(c, t, True)
+
+        @pl.when(z == 2)
+        def _():
+            for t in (0, 1):
+                drop(c, t, True)
+
+    def line_c(c):
+        @pl.when(z == 2)
+        def _():
+            climb(c, 3, True)
+
+        @pl.when(z == 1)
+        def _():
+            drop(c, 0, True)
+
+    def finish(c):
+        @pl.when(z > 0)
+        def _():
+            done(up.at[c, z - 1], sem_ru.at[c, z - 1])
+            out[c] = out[c] + decode(up.at[c, z - 1])
+
+        @pl.when(z < 3)
+        def _():
+            done(dn.at[c, z], sem_rd.at[c, z])
+            out[c] = out[c] + decode(dn.at[c, z])
+
+
+    def pair(n):
+        r = block(n, length)
+        return remote(part, other.at[r], pair_send.at[n], pair_recv.at[n], dp, 1 - mp)
+
+    def head(p):
+        n, h = p // heads, lax.rem(p, heads)
+
+        @pl.when(h == 0)
+        def _():
+            for copy in attn_loads(n):
+                copy.wait()
+        backward_head(h, width, qkv, do_t, lse, cos_ref[...], sin_ref[...], dqkv, dk, dv)
+
+        @pl.when(h == heads - 1)
+        def _():
+            stack[0:3 * width, :] = stack[0:3 * width, :] + dot(dqkv[...], a[...])
+            part[...] = dot(dqkv[...], wt[0:3 * width, :], 0, 0)
+            pair(n).start()
+
+            @pl.when(n + 1 < series)
+            def _():
+                for copy in attn_loads(n + 1):
+                    copy.start()
+
+    def embed(m):
+        n, i = m // per, lax.rem(m, per)
+        t = block(i, TILE, TILE)
+
+        @pl.when(m == 0)
+        def _():
+            rest_load.wait()
+
+        @pl.when(i == 0)
+        def _():
+            pair(n).wait()
+            dx1_load(n).wait()
+        da = part[t, :] + other[block(m, TILE), :]
+        sums = embed_backward_piece(x_ref[n, :, t], da, dx1[t, :], vec)
+        for row, value in zip((0, 3, 4), sums):
+            there = slice(4 * width + VECTOR + row, 4 * width + VECTOR + row + 1)
+            stack[there, :] = stack[there, :] + value
+
+        @pl.when((i == per - 1) & (n + 1 < series))
+        def _():
+            dx1_load(n + 1).start()
+
+
+    half = 512
+    total_width = sm.shape[-1]
+    ca, cb = pl.ds(0, half), pl.ds(half, total_width - half)
+
+    def small_begin():
+        sm[...] = jnp.transpose(stack[...]).reshape(sm.shape)
+        remote(sm.at[:, :, 1 - x, :, ca], small_a1, small_sa, small_r.at[0], xp, mp).start()
+        remote(sm.at[:, 1 - y, :, :, cb], small_b1, small_sb, small_r.at[1], yp, mp).start()
+
+    def small_fold():
+        done(small_a1, small_r.at[0])
+        done(small_b1, small_r.at[1])
+        for m in range(4):
+            for n in range(2):
+                sm[m, n, x, :, ca] = sm[m, n, x, :, ca] + small_a1[m, n]
+                sm[m, y, n, :, cb] = sm[m, y, n, :, cb] + small_b1[m, n]
+        remote(sm.at[:, 1 - y, x, :, ca], small_a2, small_send.at[0], small_r.at[2], yp, mp).start()
+        remote(sm.at[:, y, 1 - x, :, cb], small_b2, small_send.at[1], small_r.at[3], xp, mp).start()
+
+    def small_climb(t, relay):
+        if relay:
+            done(small_up.at[t - 1], small_ru.at[t - 1])
+            sm[t, y, x] = sm[t, y, x] + small_up[t - 1]
+        remote(sm.at[t, y, x], small_up.at[t - 1], small_su.at[t - 1], small_ru.at[t - 1], dp + 4, mp).start()
+
+    def small_drop(t, relay):
+        if relay:
+            done(small_dn.at[t], small_rd.at[t])
+            sm[t, y, x] = sm[t, y, x] + small_dn[t]
+        remote(sm.at[t, y, x], small_dn.at[t], small_sd.at[t], small_rd.at[t], dp - 4, mp).start()
+
+    def small_a():
+        done(small_a2, small_r.at[2])
+        done(small_b2, small_r.at[3])
+        for m in range(4):
+            sm[m, y, x, :, ca] = sm[m, y, x, :, ca] + small_a2[m]
+            sm[m, y, x, :, cb] = sm[m, y, x, :, cb] + small_b2[m]
+        out_small[...] = sm[z, y, x]
+
+        @pl.when(z == 0)
+        def _():
+            for t in (3, 2, 1):
+                small_climb(t, False)
+
+        @pl.when(z == 3)
+        def _():
+            for t in (0, 1, 2):
+                small_drop(t, False)
+
+    def small_b():
+        @pl.when(z == 1)
+        def _():
+            for t in (3, 2):
+                small_climb(t, True)
+
+        @pl.when(z == 2)
+        def _():
+            for t in (0, 1):
+                small_drop(t, True)
+
+    def small_c():
+        @pl.when(z == 2)
+        def _():
+            small_climb(3, True)
+
+        @pl.when(z == 1)
+        def _():
+            small_drop(0, True)
+
+    def small_finish():
+        @pl.when(z > 0)
+        def _():
+            done(small_up.at[z - 1], small_ru.at[z - 1])
+            out_small[...] = out_small[...] + small_up[z - 1]
+
+        @pl.when(z < 3)
+        def _():
+            done(small_dn.at[z], small_rd.at[z])
+            out_small[...] = out_small[...] + small_dn[z]
+
+
+    def at(i, first, number, run):
+        @pl.when((i >= first) & (i < first + number))
+        def _():
+            run(i - first)
+
+    small_first = count
+
+    def step(i, carry):
+        at(i, 0, count, begin)
+
+        @pl.when(i < series * heads // 2)
+        def _():
+            def two(q, carry):
+                head(2 * i + q)
+                return carry
+            lax.fori_loop(0, 2, two, 0)
+
+        for n in range(series):
+            @pl.when((i >= 3 + n * 3) & (i < 3 + n * 3 + per // 2))
+            def _():
+                def two(q, carry):
+                    embed(n * per + 2 * (i - 3 - n * 3) + q)
+                    return carry
+                lax.fori_loop(0, 2, two, 0)
+        at(i, small_first, 1, lambda _: small_begin())
+        at(i, 2, count, fold)
+        at(i, small_first + 1, 1, lambda _: small_fold())
+        at(i, 4, count, line_a)
+        at(i, small_first + 2, 1, lambda _: small_a())
+        at(i, 5, count, line_b)
+        at(i, small_first + 3, 1, lambda _: small_b())
+        at(i, 6, count, line_c)
+        at(i, small_first + 4, 1, lambda _: small_c())
+        at(i, 7, count, finish)
+        at(i, small_first + 5, 1, lambda _: small_finish())
+        return carry
+
+    lax.fori_loop(0, count + 7, step, 0)
+
+    for slot in range(SLOTS):
+        done(send1.at[slot], sem_s1.at[slot])
+    for slot in range(HOPS):
+        done(send2.at[slot], sem_s2.at[slot])
+        for t in (1, 2, 3):
+            @pl.when(z < t)
+            def _():
+                done(zs_up.at[slot, t - 1], sem_su.at[slot, t - 1])
+        for t in (0, 1, 2):
+            @pl.when(z > t)
+            def _():
+                done(zs_dn.at[slot, t], sem_sd.at[slot, t])
+    done(small_a1, small_sa)
+    done(small_b1, small_sb)
+    done(small_a2, small_send.at[0])
+    done(small_b2, small_send.at[1])
+    for t in (1, 2, 3):
+        @pl.when(z < t)
+        def _():
+            done(small_up.at[t - 1], small_su.at[t - 1])
+    for t in (0, 1, 2):
+        @pl.when(z > t)
+        def _():
+            done(small_dn.at[t], small_sd.at[t])
+
+
+def backward_near(xs, dys, dgs, hs, qkv, do, lse, a, dx1, rest, x, wt, vec, cos, sin, ident):
+    capacity, hidden = hs.shape[1], hs.shape[2]
+    series, rows, length = qkv.shape
+    heads_width = rows // 3
+    count = ROUTED_EXPERTS + 1
+    width = 3 * hidden
+    coded = width + LANES
+    small = 4 * heads_width + LANES
+    tokens = series * length
+    v = pltpu.VMEM
+    return pl.pallas_call(
+        backward_kernel,
+        in_specs=[ANY] * 10 + [VMEM] * 5,
+        out_specs=[VMEM] * 2,
+        out_shape=[
+            jax.ShapeDtypeStruct((count, SHARD, width), F32), jax.ShapeDtypeStruct((SHARD, small), F32)],
+        scratch_shapes=[
+            v((capacity, D), BF16), v((capacity, D), BF16), v((capacity, 2 * hidden), BF16), v((capacity, hidden), BF16),
+            v((D, capacity), BF16), v((D, capacity), BF16),
+            v((D, width), F32), v((SLOTS, 8, SHARD, width), F32), v((ACCS, 4, SHARD, width), F32),
+            v((SLOTS, 8, SHARD, coded), I16), v((count, 8, SHARD, coded), I16),
+            v((HOPS, 4, SHARD, coded), I16), v((count, 4, SHARD, coded), I16),
+            v((HOPS, 3, SHARD, coded), I16), v((HOPS, 3, SHARD, coded), I16),
+            v((count, 3, SHARD, coded), I16), v((count, 3, SHARD, coded), I16),
+            v((rows, length), BF16), v((heads_width, length), BF16), v((8, length), F32), v((length, D), BF16),
+            v((length, D), F32), v((rows, length), BF16), v((length, HEAD), F32), v((length, HEAD), F32),
+            v((small, D), F32), v((length, D), F32), v((tokens, D), F32),
+            v((4, 2, 2, SHARD, small), F32),
+            v((4, 2, SHARD, 512), F32), v((4, 2, SHARD, small - 512), F32),
+            v((4, SHARD, 512), F32), v((4, SHARD, small - 512), F32),
+            v((3, SHARD, small), F32), v((3, SHARD, small), F32),
+            DMA((4,)), DMA((SLOTS,)), DMA((count,)), DMA((HOPS,)), DMA((count,)),
+            DMA((HOPS, 3)), DMA((HOPS, 3)), DMA((count, 3)), DMA((count, 3)),
+            DMA((4,)), DMA, DMA, DMA((series,)), DMA((series,)),
+            DMA((2,)), DMA, DMA, DMA((4,)), DMA((3,)), DMA((3,)), DMA((3,)), DMA((3,)),
+        ],
+        compiler_params=pltpu.CompilerParams(
+            vmem_limit_bytes=67_000_000, collective_id=ident, has_side_effects=True),
+        name="backward_near",
+    )(xs, dys, dgs, hs, qkv, do, lse, a, dx1, rest, x, wt, vec, cos, sin)
+
+
+def all_kernel(value, out, send_sem, recv_sem):
+    dp, mp = lax.axis_index("dp"), lax.axis_index("mp")
+    me = dp * 2 + mp
+    meet_everyone(dp, mp)
+
+    def tell(k, carry):
+        peer = lax.rem(me + k, 32)
+        remote(value, out.at[me], send_sem, recv_sem, peer // 2, lax.rem(peer, 2)).start()
+        return carry
+
+    lax.fori_loop(1, 32, tell, 0)
+    out[me] = value[...]
+    view = out.at[pl.ds(0, 31)]
+    done(view, recv_sem)
+    done(view, send_sem)
+
+
+def all_blocks(value, ident):
+    return pl.pallas_call(
+        all_kernel,
+        in_specs=[VMEM],
+        out_specs=VMEM,
+        out_shape=jax.ShapeDtypeStruct((32,) + value.shape, value.dtype),
+        scratch_shapes=[DMA, DMA],
+        compiler_params=pltpu.CompilerParams(collective_id=ident, has_side_effects=True),
+        name="all_blocks",
+    )(value)
+
+
+def rope_rows(length):
+    halfway = HEAD // 2
+    frequency = rope_base ** (-2.0 * jnp.arange(halfway, dtype=F32) / HEAD)
+    angles = frequency[:, None] * jnp.arange(length, dtype=F32)[None, :]
+    return jnp.cos(angles), jnp.sin(angles)
+
+
+def hankel_rows(track):
+    length = track.shape[1]
+    padded = jnp.pad(track, ((0, 0), (63, 2 * LANES)))
+    first = padded[:, :length].reshape(-1, LANES)[:, ::-1]
+    second = padded[:, LANES:LANES + length].reshape(-1, LANES)[:, ::-1]
+    return jnp.concatenate([first, second], axis=1)
+
+
+def table_columns(read, vec):
+    parts, end = [], read.shape[1]
+    for horizon in horizons[::-1]:
+        parts.append(read[:, end - horizon:end][:, ::-1])
+        end -= horizon
+    gap = jnp.zeros((read.shape[0], ROUTER - sum(horizons)), read.dtype)
+    tail = jnp.zeros((read.shape[0], LANES - VECTOR - vec.shape[1]), read.dtype)
+    return jnp.concatenate(parts + [gap, read[:, :ROUTED_EXPERTS + 1], vec, tail], axis=1)
+
+
+def table_columns_back(table):
+    parts, begin = [], 0
+    for horizon in horizons[::-1]:
+        parts.append(table[:, begin:begin + horizon][:, ::-1])
+        begin += horizon
+    return jnp.concatenate([table[:, ROUTER:VECTOR]] + parts[::-1], axis=1)
+
+
+def dispatch(route_rows, capacity):
+    tokens = route_rows.shape[0]
+    experts = jnp.arange(ROUTED_EXPERTS, dtype=jnp.int32)
+    member = jnp.any(route_rows[:, :, None] == experts[None, None, :], axis=1)
+    count = jnp.cumsum(member.astype(jnp.int32), axis=0)
+    total = count[-1]
+    place = jnp.where(member, count - 1, -1)
+    high = (place[:, :, None] // LANES == jnp.arange(capacity // LANES)[None, None, :]) & member[:, :, None]
+    low = (place[:, :, None] % LANES == jnp.arange(LANES)[None, None, :]).astype(BF16)
+    token = jnp.arange(tokens, dtype=jnp.int32)
+    left = jnp.concatenate(
+        [jnp.where(high, part[:, None, None], 0).astype(BF16) for part in (token // 16, token % 16)], axis=2)
+    found = jnp.einsum("teh,tel->ehl", left, low, preferred_element_type=F32)
+    half = capacity // LANES
+    source = (found[:, :half] * 16.0 + found[:, half:]).reshape(ROUTED_EXPERTS, capacity).astype(jnp.int32)
+    slots = jnp.arange(capacity, dtype=jnp.int32)
+    source = jnp.where(slots[None, :] < total[:, None], source, tokens)
+    return total, source.reshape(-1)
+
+
+def adam_update(master, moment, square, gradient, factor, bias_one, bias_two, step_rate):
+    clipped = gradient * factor
+    new_moment = beta_one * moment + (1.0 - beta_one) * clipped
+    new_square = beta_two * square + (1.0 - beta_two) * clipped * clipped
+    updated = master - step_rate * (
+        new_moment / bias_one / (jnp.sqrt(new_square / bias_two) + adam_eps) + decay_rate * master
+    )
+    return (updated, new_moment, new_square)
+
+
+def on_device(
+    series, observed, routes, step_count,
+    joint_proj, joint_moment, joint_square,
+    mixer_proj, mixer_moment, mixer_square,
+    upward_proj, upward_moment, upward_square,
+    downward_proj, downward_moment, downward_square,
+    readout, readout_moment, readout_square,
+    vectors, vectors_moment, vectors_square,
+):
+    dp_count = lax.axis_size("dp")
+    mp_count = lax.axis_size("mp")
+    shard = joint_proj.shape[1]
+    width = joint_proj.shape[2]
+    hidden = upward_proj.shape[3]
+    experts = upward_proj.shape[0]
+    series_count, length = series.shape
+    tokens = series_count * length
+    capacity = tokens // 2
+
+    small_own = jnp.concatenate(
+        [joint_proj[k].astype(BF16) for k in range(3)]
+        + [mixer_proj.T.astype(BF16), table_columns(readout.astype(BF16), vectors.T.astype(BF16))], axis=1)
+    big_own = jnp.concatenate(
+        [upward_proj.astype(BF16).reshape(experts, shard, 2 * hidden), downward_proj.transpose(0, 2, 1).astype(BF16)],
+        axis=2)
+    marks = observed.astype(F32)
+    expert_here, source = dispatch(routes.reshape(tokens, 2), capacity)
+    point = jnp.arange(length, dtype=F32)
+    head_here = jnp.stack(
+        [jnp.sum(jnp.sum(marks, axis=0) * jnp.minimum(point, float(horizon))) for horizon in horizons])
+    tally = jnp.pad(jnp.concatenate([expert_here.astype(F32), head_here]), (0, LANES - 12))
+    tally = jnp.broadcast_to(tally[None], (8, LANES))
+    cos, sin = rope_rows(length)
+    x = (series * marks).reshape(series_count, 1, length)
+
+    big, wt, vec, table, a, qkv, lse, o, x1, b, pc, pr_total, tallies = forward_near(
+        small_own, big_own, tally, x, cos, sin, width, 0)
+    wo, table_t = wt[3 * width:4 * width], wt[4 * width:]
+    tally = jnp.sum(tallies[:, 0], axis=0) / mp_count
+    expert_count, head_count = tally[:ROUTED_EXPERTS], tally[ROUTED_EXPERTS:ROUTED_EXPERTS + 4]
+    total_tokens = tokens * dp_count
+
+    xs, ys, mixed = expert_forward(expert_here, source, b, pc, big)
+    head_weight = jnp.concatenate(
+        [jnp.zeros((horizon,), F32) + 0.25 / head_count[3 - index] for index, horizon in enumerate(horizons[::-1])])
+    head_weight = jnp.pad(head_weight, (0, LANES - head_weight.shape[0]))[None]
+    dx2, d_table, d_gain3, fit = loss_stage(
+        mixed, x1, vec, table, table_t, hankel_rows(series), hankel_rows(marks), head_weight, 1)
+    dys, dgs, hs, back = expert_backward(expert_here, source, pc, dx2, big, xs, ys)
+    balance = aux_factor * ROUTED_EXPERTS * expert_count / total_tokens / total_tokens
+    balance = jnp.pad(balance, (ROUTER, LANES - SHARED))[None]
+    local_loss = jnp.sum(fit) + jnp.sum(pr_total * balance)
+    dx1, do, rest = mid_backward(back, dx2, x1, b, pc, vec, table_t, balance, wo, o, d_table, d_gain3, 2)
+    big_red, small_red = backward_near(xs, dys, dgs, hs, qkv, do, lse, a, dx1, rest, x, wt, vec, cos, sin, 3)
+
+    attn_red, table_red = small_red[:, :4 * width], small_red[:, 4 * width:]
+    squares = (
+        jnp.sum(big_red * big_red) + jnp.sum(attn_red * attn_red) + jnp.sum(table_red * table_red) / mp_count
+    )
+    pair = jnp.pad(jnp.stack([squares, local_loss / mp_count]), (0, LANES - 2))
+    pair = jnp.sum(all_blocks(jnp.broadcast_to(pair[None], (8, LANES)), 4)[:, 0], axis=0)
+    grad_norm, loss_total = jnp.sqrt(pair[0]), pair[1]
+
+    factor = clip_limit / (grad_norm + 1e-06)
+    steps_taken = step_count[0].astype(F32)
+    bias_one = 1.0 - beta_one**steps_taken
+    bias_two = 1.0 - beta_two**steps_taken
+
+    def update(master, moment, square, gradient, rate=matrix_rate):
+        return adam_update(master, moment, square, gradient, factor, bias_one, bias_two, rate)
+
+    joint_red = jnp.stack([attn_red[:, k * width:(k + 1) * width] for k in range(3)], axis=0)
+    mixer_red = attn_red[:, 3 * width:].T
+    upward_red = big_red[:, :, :2 * hidden].reshape(upward_proj.shape)
+    downward_red = big_red[:, :, 2 * hidden:].transpose(0, 2, 1)
+    return (
+        loss_total,
+        grad_norm,
+        *update(joint_proj, joint_moment, joint_square, joint_red),
+        *update(mixer_proj, mixer_moment, mixer_square, mixer_red),
+        *update(upward_proj, upward_moment, upward_square, upward_red),
+        *update(downward_proj, downward_moment, downward_square, downward_red),
+        *update(readout, readout_moment, readout_square, table_columns_back(table_red)),
+        *update(vectors, vectors_moment, vectors_square, table_red[:, VECTOR:VECTOR + 5].T, vector_rate),
+    )
+
 
 def rms_scale(tensor, gain_row):
     return (
@@ -109,16 +1607,6 @@
         .set(jnp.arange(entries, dtype=jnp.int32))
     )
     return (slot_index, source)
-
-
-def adam_update(master, moment, square, gradient, factor, bias_one, bias_two, step_rate):
-    clipped = gradient * factor
-    new_moment = beta_one * moment + (1.0 - beta_one) * clipped
-    new_square = beta_two * square + (1.0 - beta_two) * clipped * clipped
-    updated = master - step_rate * (
-        new_moment / bias_one / (jnp.sqrt(new_square / bias_two) + adam_eps) + decay_rate * master
-    )
-    return (updated, new_moment, new_square)
 
 
 def split_heads(matrix, series_count, length):
@@ -209,7 +1697,7 @@
     return lax.psum(partial_sum, "mp")
 
 
-def on_device(
+def on_device_wide(
     series,
     observed,
     routes,
@@ -526,54 +2014,16 @@
 
 
 def solution(mesh):
+    token = [P("dp", None), P("dp", None), P("dp", None, None), P()]
+    weights = [
+        P(None, "dp", "mp"), P("mp", "dp"), P(None, "dp", None, "mp"), P(None, "mp", "dp"), P("dp", None), P(None, "dp"),
+    ]
+    triple = tuple(spec for spec in weights for _ in range(3))
+    near = mesh.shape["dp"] == 16 and mesh.shape["mp"] == 2
     return jax.shard_map(
-        on_device,
+        on_device if near else on_device_wide,
         mesh=mesh,
-        in_specs=(
-            P("dp", None),
-            P("dp", None),
-            P("dp", None, None),
-            P(),
-            P(None, "dp", "mp"),
-            P(None, "dp", "mp"),
-            P(None, "dp", "mp"),
-            P("mp", "dp"),
-            P("mp", "dp"),
-            P("mp", "dp"),
-            P(None, "dp", None, "mp"),
-            P(None, "dp", None, "mp"),
-            P(None, "dp", None, "mp"),
-            P(None, "mp", "dp"),
-            P(None, "mp", "dp"),
-            P(None, "mp", "dp"),
-            P("dp", None),
-            P("dp", None),
-            P("dp", None),
-            P(None, "dp"),
-            P(None, "dp"),
-            P(None, "dp"),
-        ),
-        out_specs=(
-            P(),
-            P(),
-            P(None, "dp", "mp"),
-            P(None, "dp", "mp"),
-            P(None, "dp", "mp"),
-            P("mp", "dp"),
-            P("mp", "dp"),
-            P("mp", "dp"),
-            P(None, "dp", None, "mp"),
-            P(None, "dp", None, "mp"),
-            P(None, "dp", None, "mp"),
-            P(None, "mp", "dp"),
-            P(None, "mp", "dp"),
-            P(None, "mp", "dp"),
-            P("dp", None),
-            P("dp", None),
-            P("dp", None),
-            P(None, "dp"),
-            P(None, "dp"),
-            P(None, "dp"),
-        ),
+        in_specs=tuple(token) + triple,
+        out_specs=(P(), P()) + triple,
         check_vma=False,
     )

time: 2260 us -> 575 us (0.25)
  waiting for transfers between devices: 657 us -> 0 us
  matrix products: 556 us -> 3.7 us
  Pallas kernels: 0 us -> 513 us
  blocking collectives: 361 us -> 0 us
  local copies, waits for them, and re-layouts: 367 us -> 18.3 us
  other arithmetic: 239 us -> 28.9 us
  between operations: 69.7 us -> 9.74 us
    dot_general x52 -> x1, matrix products: 556 us -> 3.7 us  [dispatch(): found = jnp.einsum('teh,tel->ehl', left, low, preferred_element_type=F32)]
    pallas_call x0 -> x7, Pallas kernels: none -> 513 us  [the longest x1 202 us: backward_near(): pl.pallas_call(backward_kernel, in_specs=[ANY] * 10 + [VMEM] * 5, out_spe...]
    unnamed x12 -> x0, waiting for transfers between devices: 400 us -> none
    psum x5 -> x0, blocking collectives: 204 us -> none  [the longest x1 81.5 us: on_device(): loss_total = lax.psum(local_loss, 'dp')]
    reduce_scatter x2 -> x0, waiting for transfers between devices: 200 us -> none  [the longest x1 200 us: on_device(): lax.psum_scatter(downward_grad, 'dp', scatter_dimension=2, tiled=True)]
    all_gather x4 -> x0, blocking collectives: 158 us -> none  [the longest x1 42.6 us: on_device(): lax.all_gather(vectors.astype(jnp.bfloat16), 'dp', axis=1, tiled=True)]
    gather x5 -> x0, local copies, waits for them, and re-layouts: 154 us -> none  [the longest x1 45.5 us: on_device(): gates_padded[source][:, None] * residual_padded[token_of]]
    reduce_sum x33 -> x8, other arithmetic: 153 us -> 8.52 us  [the longest x1 2.82 us: on_device(): jnp.sum(big_red * big_red) + jnp.sum(attn_red * attn_red)]
  transfers between devices with their start and end apart: 10 -> 0, of which waited for: 6 -> 0; matrix products, arithmetic and copies ran while one was open for 19% -> 0% of each run, Pallas kernels for 0% -> 0%
where the time goes in v3:
time: 575 us; the launch traced here: 574 us
  Pallas kernels  513 us (89%)
  other arithmetic  28.9 us (5%)
  local copies, waits for them, and re-layouts  18.3 us (3%)
  between operations  9.74 us (2%)
    pallas_call x1, Pallas kernels, backward_near(): pl.pallas_call(backward_kernel, in_specs=[ANY] * 10 + [VMEM] * 5, out_spe...  202 us
    pallas_call x1, Pallas kernels, forward_near(): pl.pallas_call(forward_kernel, in_specs=[VMEM, ANY, VMEM, VMEM, VMEM, VME...  160 us
    pallas_call x1, Pallas kernels, expert_backward(): pl.pallas_call(expert_backward_kernel, grid_spec=pltpu.PrefetchScalarGrid...  67.7 us
    pallas_call x1, Pallas kernels, expert_forward(): pl.pallas_call(expert_forward_kernel, grid_spec=pltpu.PrefetchScalarGridS...  46.6 us
    pallas_call x1, Pallas kernels, mid_backward(): pl.pallas_call(mid_backward_kernel, in_specs=[VMEM] * 12, out_specs=[VMEM...  15.3 us
    pallas_call x1, Pallas kernels, loss_stage(): pl.pallas_call(loss_kernel, in_specs=[VMEM] * 8, out_specs=[VMEM] * 4, ou...  12.9 us

profile of v3, /device:TPU:0, one launch (start us, length us, event | category | flops | bytes accessed | tf_op | source)
XLA Modules:
  0.0 573.7 jit_solution(14682617453964021267)
XLA Ops:
  0.7 0.7 fusion.9
  1.4 2.3 reduce-window.6
  3.7 0.3 slice_reduce_fusion
  4.0 0.2 reduce-window.9
  4.2 0.1 add_bitcast_fusion
  4.3 0.2 slice_reduce_fusion.3.counts
  4.5 0.1 add_select_fusion.1
  4.6 0.2 select_convert_fusion.1
  4.8 3.7 fusion
  8.5 0.1 fusion.17
  8.6 0.6 fusion.16.source
  9.4 0.1 rev.30
  9.5 0.1 rev.31
  9.7 0.1 rev.32
  9.9 0.1 copy.88
  10.0 0.7 concatenate.25.small_own
  10.8 0.5 convert_element_type.89
  11.2 0.4 reshape.161
  11.7 1.0 pad_maximum_fusion.big_own
  12.7 0.1 pad_slice_fusion.3
  12.8 0.6 multiply_reduce_fusion.3
  13.4 2.7 concatenate.27
  16.1 0.6 broadcast_in_dim.65.tally
  16.7 0.6 reshape.162.x_ref
  17.3 1.0 fusion.11
  18.3 159.7 %forward_near.1 = (bf16[9,384,2304]{2,1,0:T(8,128)(2,1)}, bf16[896,384]{1,0:T(8,128)(2,1)}, f32[8,384]{1,0:T(8,128)}, bf16[384,128]{1,0:T(8,128)(2,1)}, bf16[204...) custom-call(bf16[24,896]{1,0:T(8,128)(2,1)} %concatenate.25.small_ow, ...), custom_call_target="tpu_custom_call" | custom-call | tf_op jit(solution)/shard_map/forward_near/pallas_call | solution.py:440
  178.0 46.6 %expert_forward.1 = (bf16[10,1024,384]{2,1,0:T(8,128)(2,1)}, f32[10,1024,384]{2,1,0:T(8,128)}, f32[2048,384]{1,0:T(8,128)}) custom-call(s32[8]{0:T(128)} %copy-done.20, s32[8192]{0:T(1024)} %fusion.16.source, bf16[2048,384]{1,0:T(8,128)(2,1)} %get-tuple-element.49.b_ref.b, f32[2048,128]{1,0:T(8,128)} %get-tuple-element.50.pc_ref.pc, ...), custom_call_target="tpu_custom_call" | custom-call | tf_op jit(solution)/shard_map/expert_forward/pallas_call | solution.py:603
  224.5 1.5 slice.157.table_t
  226.3 0.1 pad_slice_fusion.1
  226.5 0.6 pad_maximum_fusion.1
  227.1 1.0 slice_reduce_fusion.2
  228.1 0.6 fusion.43
  231.5 0.6 fusion.31.weight
  232.1 12.9 %loss_stage.1 = (f32[2048,384]{1,0:T(8,128)}, f32[128,384]{1,0:T(8,128)}, f32[1,384]{1,0:T(1,128)}, f32[1,128]{1,0:T(1,128)}) custom-call(f32[2048,384]{1,0:T(8,128)} %get-tuple-element.53.part, f32[2048,384]{1,0:T(8,128)} %get-tuple-element.54.x1, f32[8,384]{1,0:T(8,128)} %get-tuple-element.55.vec, bf16[384,128]{1,0:T(8,128)(2,1)} %get-tuple-element.56.table, ...), custom_call_target="tpu_custom_call" | custom-call | tf_op jit(solution)/shard_map/loss_stage/pallas_call | solution.py:807
  244.9 1.3 reduce_sum.129
  246.2 0.7 multiply_reduce_fusion.7
  248.2 67.7 %expert_backward.1 = (bf16[10,1024,384]{2,1,0:T(8,128)(2,1)}, bf16[10,1024,1536]{2,1,0:T(8,128)(2,1)}, bf16[10,1024,768]{2,1,0:T(8,128)(2,1)}, f32[2048,512]{1,0:T(8,128)}) custom-call(s32[8]{0:T(128)} %copy-done.20, s32[8192]{0:T(1024)} %fusion.16.source, f32[2048,128]{1,0:T(8,128)} %get-tuple-element.50.pc_ref.pc, ...), custom_call_target="tpu_custom_call" | custom-call | tf_op jit(solution)/shard_map/expert_backward/pallas_call | solution.py:704
  315.9 0.6 pad_bitcast_fusion.balance
  316.5 1.6 slice.168.wo
  318.1 15.3 %mid_backward.1 = (f32[2048,384]{1,0:T(8,128)}, bf16[2,192,1024]{2,1,0:T(8,128)(2,1)}, f32[320,384]{1,0:T(8,128)}) custom-call(f32[2048,512]{1,0:T(8,128)} %get-tuple-element.65.part, f32[2048,384]{1,0:T(8,128)} %get-tuple-element.59.dx_ref.dx2, f32[2048,384]{1,0:T(8,128)} %get-tuple-element.54.x1, bf16[2048,384]{1,0:T(8,128)(2,1)} %get-tuple-element.49.b_ref.b, ...), custom_call_target="tpu_custom_call" | custom-call | tf_op jit(solution)/shard_map/mid_backward/pallas_call | solution.py:862
  333.4 202.1 %backward_near.1 = (f32[9,24,2304]{2,1,0:T(8,128)}, f32[24,896]{1,0:T(8,128)}) custom-call(bf16[10,1024,384]{2,1,0:T(8,128)(2,1)} %get-tuple-element.52.x_ref.xs, bf16[10,1024,384]{2,1,0:T(8,128)(2,1)} %get-tuple-element.61.dys, bf16[10,1024,1536]{2,1,0:T(8,128)(2,1)} %get-tuple-element.62.dgs, bf16[10,1024,768]{2,1,0:T(8,128)(2,1)} %get-tuple-element.63.hs, ...), custom_call_target="tpu_custom_call" | custom-call | tf_op jit(solution)/shard_map/backward_near/pallas_call | solution.py:1312
  535.6 2.8 multiply_reduce_fusion
  538.4 0.6 multiply_reduce_fusion.1
  540.3 0.6 multiply_reduce_fusion.2
  541.6 0.1 fusion.30
  541.6 0.6 broadcast_in_dim.68.value
  542.2 8.9 %all_blocks.1 = f32[32,8,128]{2,1,0:T(8,128)} custom-call(f32[8,128]{1,0:T(8,128)} %broadcast_in_dim.68.value), custom_call_target="tpu_custom_call" | custom-call | tf_op jit(solution)/shard_map/all_blocks/pallas_call | solution.py:1362
  551.2 1.0 slice_reduce_fusion.1
  552.1 0.6 fusion.42
  554.2 0.7 multiply_subtract_fusion.2
  555.0 0.7 multiply_subtract_fusion.3
  555.7 1.2 slice_multiply_fusion
  556.9 3.1 mul.324
  560.0 7.3 %multiply_subtract_fusion = (f32[9,24,2,768]{3,2,1,0:T(2,128)}, f32[9,24,2,768]{3,2,1,0:T(2,128)}, f32[9,24,2,768]{3,2,1,0:T(2,128)}) fusion(f32[9,24,2,768]{3,2,1,0:T(2,128)S(1)} %copy-done.2, f32[]{:T(128)} %bitcast.28, f32[]{:T(128)} %bitcast.27, f32[9,24,2,768]{3,2,1,0:T(2,128)} %mul.324, f32[9,24,2,768]{3,2,1,0:T(2,128)} %param.34, ...), kind=kLoop, calls=%fused_computation.6 | loop fusion | flops 4976640 | bytes 9289736 | tf_op jit(solution)/shard_map/sub | solution.py:1430
  567.4 1.6 multiply_subtract_fusion.1
  569.5 0.1 concatenate.31
  569.6 0.6 multiply_subtract_fusion.5
  570.2 0.1 copy.93
  570.3 0.1 copy.91
  570.4 0.1 copy.89
  570.5 0.1 multiply_subtract_fusion.4
  570.6 0.7 copy.94
  571.3 0.7 copy.95
  571.9 0.7 copy.96
  (92 shorter events, 1.5 us)
Async XLA Ops:
  4.5 8.2 %copy-start.20 = (s32[8]{0:T(128)}, s32[8]{0:T(128)S(1)}, u32[]{:S(2)}) copy-start(s32[8]{0:T(128)S(1)} %slice_reduce_fusion.3.counts) | copy-start | bytes 100
  4.7 4.5 copy-start.8
  4.8 4.5 copy-start.10
  4.8 4.5 copy-start.13
  4.8 5.1 copy-start.17
  4.8 5.9 %copy-start.3 = (f32[9,768,24]{1,2,0:T(8,128)S(1)}, f32[9,768,24]{1,2,0:T(8,128)}, u32[]{:S(2)}) copy-start(f32[9,768,24]{1,2,0:T(8,128)} %param.35) | copy-start | bytes 1990660
  8.5 2.3 copy-start.1
  11.7 1.0 copy-start.14
  11.7 1.0 copy-start.21
  232.1 14.2 %copy-start.24 = (f32[1,128]{1,0:T(1,128)S(1)}, f32[1,128]{1,0:T(1,128)}, u32[]{:S(2)}) copy-start(f32[1,128]{1,0:T(1,128)} %get-tuple-element.77) | copy-start | bytes 1540
  535.5 2.9 copy-start.5
  535.5 18.7 %copy-start.9 = (f32[3,24,192]{2,1,0:T(8,128)S(1)}, f32[3,24,192]{2,1,0:T(8,128)}, u32[]{:S(2)}) copy-start(f32[3,24,192]{2,1,0:T(8,128)} %param.26) | copy-start | bytes 165892
  535.5 18.7 %copy-start.11 = (f32[3,24,192]{2,1,0:T(8,128)S(1)}, f32[3,24,192]{2,1,0:T(8,128)}, u32[]{:S(2)}) copy-start(f32[3,24,192]{2,1,0:T(8,128)} %param.28) | copy-start | bytes 165892
  535.5 18.7 %copy-start.12 = (f32[3,24,192]{2,1,0:T(8,128)S(1)}, f32[3,24,192]{2,1,0:T(8,128)}, u32[]{:S(2)}) copy-start(f32[3,24,192]{2,1,0:T(8,128)} %param.27) | copy-start | bytes 165892
  535.5 19.4 %copy-start.15 = (f32[192,24]{0,1:T(8,128)S(1)}, f32[192,24]{0,1:T(8,128)}, u32[]{:S(2)}) copy-start(f32[192,24]{0,1:T(8,128)} %param.31) | copy-start | bytes 55300
  535.5 19.4 %copy-start.16 = (f32[192,24]{0,1:T(8,128)S(1)}, f32[192,24]{0,1:T(8,128)}, u32[]{:S(2)}) copy-start(f32[192,24]{0,1:T(8,128)} %param.30) | copy-start | bytes 55300
  535.6 20.1 %copy-start = (f32[9,24,2304]{2,1,0:T(8,128)S(1)}, f32[9,24,2304]{2,1,0:T(8,128)}, u32[]{:S(2)}) copy-start(f32[9,24,2304]{2,1,0:T(8,128)} %get-tuple-element.74) | copy-start | bytes 5971972
  556.9 3.1 copy-start.2
  560.0 7.3 %copy-start.4 = (f32[9,768,24]{1,2,0:T(8,128)S(1)}, f32[9,768,24]{1,2,0:T(8,128)}, u32[]{:S(2)}) copy-start(f32[9,768,24]{1,2,0:T(8,128)} %param.35) | copy-start | bytes 1990660
  560.0 7.3 %copy-start.6 = (f32[9,768,24]{1,2,0:T(8,128)S(1)}, f32[9,768,24]{1,2,0:T(8,128)}, u32[]{:S(2)}) copy-start(f32[9,768,24]{1,2,0:T(8,128)} %param.37) | copy-start | bytes 1990660
  560.0 7.3 %copy-start.7 = (f32[9,768,24]{1,2,0:T(8,128)S(1)}, f32[9,768,24]{1,2,0:T(8,128)}, u32[]{:S(2)}) copy-start(f32[9,768,24]{1,2,0:T(8,128)} %param.36) | copy-start | bytes 1990660
  567.3 2.3 copy-start.18
  567.3 2.3 copy-start.19
  567.3 3.0 copy-start.22
  567.3 3.0 copy-start.23

commit v4 on v3

--- a/solution.py
+++ b/solution.py
@@ -468,67 +468,65 @@
         dest[pl.ds(start * 8 + c, count, stride=8), :] = value[:, c * LANES:(c + 1) * LANES]
 
 
+def rows_at(ref, index):
+    return ref[pl.ds(pl.multiple_of(index, 8), 8), :]
+
+
 def pick_rows(source, tile, index_ref, base):
-    def body(i, carry):
-        values = []
-        for k in range(GROUP):
-            t = index_ref[base + i * GROUP + k]
-            values.append(source[pl.ds(pl.multiple_of(t * 8, 8), 8), :])
-        for k in range(GROUP):
-            tile[pl.ds(pl.multiple_of((i * GROUP + k) * 8, 8), 8), :] = values[k]
-        return carry
-
-    lax.fori_loop(0, TILE // GROUP, body, 0)
-
-
-def add_rows(dest, tile, index_ref, base):
-    def body(i, carry):
-        places, values = [], []
-        for k in range(GROUP):
-            t = index_ref[base + i * GROUP + k]
-            place = pl.ds(pl.multiple_of(t * 8, 8), 8)
-            places.append(place)
-            values.append(dest[place, :] + tile[pl.ds(pl.multiple_of((i * GROUP + k) * 8, 8), 8), :])
-        for k in range(GROUP):
-            dest[places[k], :] = values[k]
-        return carry
-
-    lax.fori_loop(0, TILE // GROUP, body, 0)
+    for i in range(0, TILE, GROUP):
+        values = [rows_at(source, index_ref[base + k]) for k in range(i, i + GROUP)]
+        for k in range(i, i + GROUP):
+            tile[k * 8:k * 8 + 8, :] = values[k - i]
+
+
+def sum_rows(results, tile, index_ref, base, tokens):
+    for i in range(0, TILE, GROUP):
+        values = [
+            rows_at(results, index_ref[base + k]) + rows_at(results, index_ref[tokens + base + k])
+            for k in range(i, i + GROUP)]
+        for k in range(i, i + GROUP):
+            tile[k * 8:k * 8 + 8, :] = values[k - i]
 
 
 def gathered_columns(tile, columns):
     return [tile[pl.ds(c, TILE, stride=8), :] for c in range(columns)]
 
 
-def lane_of(block, lane):
-    lanes = lax.broadcasted_iota(jnp.int32, block.shape, 1)
-    return jnp.sum(jnp.where(lanes == lane, block, 0.0), axis=1, keepdims=True)
-
-
-def lay_rows(values, pc_ref, rows8, acc8):
+def lane_of(value, lane):
+    lanes = lax.broadcasted_iota(jnp.int32, value.shape, 1)
+    return jnp.sum(jnp.where(lanes == lane, value, 0.0), axis=1, keepdims=True)
+
+
+def lay_rows(values, pc_ref, rows8):
     tokens = values.shape[0]
 
     def lay(i, carry):
-        r = pl.ds(pl.multiple_of(i * TILE, TILE), TILE)
+        r = block(i, TILE)
         spread_rows(rows8, values[r, :].astype(F32), i * TILE, TILE)
         rows8[pl.ds(i * TILE * 8 + 3, TILE, stride=8), :] = pc_ref[r, :]
-        acc8[pl.ds(pl.multiple_of(i * TILE * 8, 8), TILE * 8), :] = jnp.zeros((TILE * 8, LANES), F32)
         return carry
 
     lax.fori_loop(0, tokens // TILE, lay, 0)
     rows8[pl.ds(tokens * 8, 8), :] = jnp.zeros((8, LANES), F32)
-    acc8[pl.ds(tokens * 8, 8), :] = jnp.zeros((8, LANES), F32)
-
-
-def expert_forward_kernel(counts, source, b_ref, pc_ref, w_ref, x_ref, y_ref, mix_ref, rows8, acc8, tile8):
-    e = pl.program_id(0)
+
+
+def expert_of(s, tokens):
+    return jnp.minimum(s // (tokens // 2 // TILE), ROUTED_EXPERTS)
+
+
+def expert_forward_kernel(
+    order, after, source, slots, b_ref, pc_ref, w_ref, x_ref, y_ref, mix_ref, rows8, done8, tile8, sum8
+):
+    s = pl.program_id(0)
+    tokens = b_ref.shape[0]
     hidden = w_ref.shape[2] // 3
-    capacity = y_ref.shape[1]
-    tiles = capacity // TILE
-
-    @pl.when(e == 0)
+    routed = ROUTED_EXPERTS * (tokens // 2 // TILE)
+    e = expert_of(s, tokens)
+
+    @pl.when(s == 0)
     def _():
-        lay_rows(b_ref, pc_ref, rows8, acc8)
+        lay_rows(b_ref, pc_ref, rows8)
+        pick_rows(rows8, tile8, source, after[pl.num_programs(0)])
 
     def run(x):
         g = dot(x, w_ref[0, :, : 2 * hidden])
@@ -536,193 +534,153 @@
         h = (gate * sigmoid(gate) * up).astype(BF16)
         return dot(h, w_ref[0, :, 2 * hidden:], 1, 1)
 
-    @pl.when(e < ROUTED_EXPERTS)
+    @pl.when(order[s] >= 0)
     def _():
-        used = (counts[e] + TILE - 1) // TILE
-
-        def step(i, carry):
-            base = e * capacity + i * TILE
-            r = pl.ds(pl.multiple_of(i * TILE, TILE), TILE)
-            pick_rows(rows8, tile8, source, base)
-            c0, c1, c2, pc = gathered_columns(tile8, 4)
-            x = jnp.concatenate([c0, c1, c2], axis=1).astype(BF16)
-            x_ref[0, r, :] = x
-            y = run(x)
-            y_ref[0, r, :] = y
-            spread_rows(tile8, y * lane_of(pc, ROUTER + e), 0, TILE)
-            add_rows(acc8, tile8, source, base)
-            return carry
-
-        def blank(i, carry):
-            x_ref[0, pl.ds(pl.multiple_of(i * TILE, TILE), TILE), :] = jnp.zeros((TILE, D), BF16)
-            return carry
-
-        lax.fori_loop(0, used, step, 0)
-        lax.fori_loop(used, tiles, blank, 0)
-
-    @pl.when(e >= ROUTED_EXPERTS)
+        c0, c1, c2, pc = gathered_columns(tile8, 4)
+        x = jnp.concatenate([c0, c1, c2], axis=1).astype(BF16)
+        x_ref[...] = x
+        gate_column = lane_of(pc, ROUTER + e)
+        pick_rows(rows8, tile8, source, after[s])
+        y = run(x)
+        y_ref[...] = y
+        spread_rows(done8, y * gate_column, order[s] * TILE, TILE)
+
+    @pl.when((order[s] < 0) & (s < routed))
     def _():
-        def step(i, carry):
-            t = (e - ROUTED_EXPERTS) * tiles + i
-            here = pl.ds(pl.multiple_of(i * TILE, TILE), TILE)
-            r = pl.ds(pl.multiple_of(t * TILE, TILE), TILE)
-            x = b_ref[r, :]
-            x_ref[0, here, :] = x
-            y = run(x)
-            y_ref[0, here, :] = y
-            shared = y * lane_of(pc_ref[r, :], SHARED)
-            for c in range(D // LANES):
-                cols = slice(c * LANES, (c + 1) * LANES)
-                mix_ref[r, cols] = acc8[pl.ds(t * TILE * 8 + c, TILE, stride=8), :] + shared[:, cols]
-            return carry
-
-        lax.fori_loop(0, tiles, step, 0)
-
-
-def expert_blocks(capacity, w):
-    return pl.BlockSpec((1, capacity, w), lambda e, *_: (e, 0, 0))
-
-
-def expert_weights(weights):
-    return pl.BlockSpec((1,) + weights.shape[1:], lambda e, *_: (jnp.minimum(e, ROUTED_EXPERTS), 0, 0))
-
-
-def expert_scratch(tokens):
-    return [
-        pltpu.VMEM(((tokens + 1) * 8, LANES), F32),
-        pltpu.VMEM(((tokens + 1) * 8, LANES), F32),
-        pltpu.VMEM((TILE * 8, LANES), F32),
-    ]
-
-
-def expert_forward(counts, source, b, pc, weights):
+        x_ref[...] = jnp.zeros_like(x_ref)
+
+    @pl.when(s >= routed)
+    def _():
+        r = block(s - routed, TILE)
+        x = b_ref[r, :]
+        x_ref[...] = x
+        sum_rows(done8, sum8, slots, (s - routed) * TILE, tokens)
+        y = run(x)
+        y_ref[...] = y
+        shared = y * lane_of(pc_ref[r, :], SHARED)
+        for c, part in enumerate(gathered_columns(sum8, D // LANES)):
+            cols = slice(c * LANES, (c + 1) * LANES)
+            mix_ref[r, cols] = part + shared[:, cols]
+
+
+def expert_specs(tokens, weights):
+    tiles = 5 * tokens // TILE
+    full = lambda shape: pl.BlockSpec(shape, lambda s, *_: (0,) * len(shape), pipeline_mode=pl.Buffered(1))
+    tile = lambda w: pl.BlockSpec((TILE, w), lambda s, *_: (s, 0))
+    weight = pl.BlockSpec((1,) + weights.shape[1:], lambda s, *_: (expert_of(s, tokens), 0, 0))
+    most = 2 * tokens // TILE + ROUTED_EXPERTS - 1
+    scratch = [
+        pltpu.VMEM(((tokens + 1) * 8, LANES), F32), pltpu.VMEM((most * TILE * 8, LANES), F32),
+        pltpu.VMEM((TILE * 8, LANES), F32), pltpu.VMEM((TILE * 8, LANES), F32)]
+    return tiles, full, tile, weight, scratch
+
+
+def expert_forward(plan, b, pc, weights):
     tokens = b.shape[0]
-    capacity = tokens // 2
-    blocks = ROUTED_EXPERTS + 2
-    full = lambda shape: pl.BlockSpec(shape, lambda e, *_: (0,) * len(shape), pipeline_mode=pl.Buffered(1))
+    tiles, full, tile, weight, scratch = expert_specs(tokens, weights)
     return pl.pallas_call(
         expert_forward_kernel,
         grid_spec=pltpu.PrefetchScalarGridSpec(
-            num_scalar_prefetch=2,
-            grid=(blocks,),
-            in_specs=[full(b.shape), full(pc.shape), expert_weights(weights)],
-            out_specs=[expert_blocks(capacity, D), expert_blocks(capacity, D), full((tokens, D))],
-            scratch_shapes=expert_scratch(tokens),
+            num_scalar_prefetch=4,
+            grid=(tiles,),
+            in_specs=[full(b.shape), full(pc.shape), weight],
+            out_specs=[tile(D), tile(D), full((tokens, D))],
+            scratch_shapes=scratch,
         ),
         out_shape=[
-            jax.ShapeDtypeStruct((blocks, capacity, D), BF16),
-            jax.ShapeDtypeStruct((blocks, capacity, D), F32),
+            jax.ShapeDtypeStruct((tiles * TILE, D), BF16),
+            jax.ShapeDtypeStruct((tiles * TILE, D), F32),
             jax.ShapeDtypeStruct((tokens, D), F32),
         ],
         compiler_params=params(),
         name="expert_forward",
-    )(counts, source, b, pc, weights)
+    )(*plan, b, pc, weights)
 
 
 def expert_backward_kernel(
-    counts, source, pc_ref, dx_ref, w_ref, x_ref, y_ref, dy_ref, dg_ref, h_ref, acc_ref, rows8, acc8, tile8
+    order, after, source, slots, pc_ref, dx_ref, w_ref, x_ref, y_ref, dy_ref, dg_ref, h_ref, acc_ref,
+    rows8, done8, tile8, sum8,
 ):
-    e = pl.program_id(0)
+    s = pl.program_id(0)
+    tokens = dx_ref.shape[0]
     hidden = w_ref.shape[2] // 3
-    capacity = y_ref.shape[1]
-    tiles = capacity // TILE
-
-    @pl.when(e == 0)
+    routed = ROUTED_EXPERTS * (tokens // 2 // TILE)
+    e = expert_of(s, tokens)
+    lanes = lax.broadcasted_iota(jnp.int32, (TILE, LANES), 1)
+
+    @pl.when(s == 0)
     def _():
-        lay_rows(dx_ref, pc_ref, rows8, acc8)
-
-    def run(r, dy):
-        x = x_ref[0, r, :]
-        dy_ref[0, r, :] = dy
+        lay_rows(dx_ref, pc_ref, rows8)
+        pick_rows(rows8, tile8, source, after[pl.num_programs(0)])
+
+    def run(dy):
+        dy_ref[...] = dy
         u = w_ref[0, :, : 2 * hidden]
-        g = dot(x, u)
+        g = dot(x_ref[...], u)
         gate, up = g[:, :hidden], g[:, hidden:]
-        s = sigmoid(gate)
-        silu = gate * s
-        h_ref[0, r, :] = (silu * up).astype(BF16)
+        sig = sigmoid(gate)
+        silu = gate * sig
+        h_ref[...] = (silu * up).astype(BF16)
         dh = dot(dy, w_ref[0, :, 2 * hidden:])
         d_up = (dh * silu).astype(BF16)
-        d_gate = (dh * up * (s * (1.0 + gate * (1.0 - s)))).astype(BF16)
-        dg_ref[0, r, :hidden] = d_gate
-        dg_ref[0, r, hidden:] = d_up
+        d_gate = (dh * up * (sig * (1.0 + gate * (1.0 - sig)))).astype(BF16)
+        dg_ref[:, :hidden] = d_gate
+        dg_ref[:, hidden:] = d_up
         return dot(d_gate, u[:, :hidden], 1, 1) + dot(d_up, u[:, hidden:], 1, 1)
 
-    lanes = lax.broadcasted_iota(jnp.int32, (TILE, LANES), 1)
-
-    @pl.when(e < ROUTED_EXPERTS)
+    @pl.when(order[s] >= 0)
     def _():
-        used = (counts[e] + TILE - 1) // TILE
-
-        def step(i, carry):
-            base = e * capacity + i * TILE
-            r = pl.ds(pl.multiple_of(i * TILE, TILE), TILE)
-            pick_rows(rows8, tile8, source, base)
-            c0, c1, c2, pc = gathered_columns(tile8, 4)
-            dx = jnp.concatenate([c0, c1, c2], axis=1)
-            d_gate = jnp.sum(y_ref[0, r, :] * dx, axis=1, keepdims=True)
-            back = run(r, (dx * lane_of(pc, ROUTER + e)).astype(BF16))
-            spread_rows(tile8, back, 0, TILE)
-            tile8[pl.ds(3, TILE, stride=8), :] = jnp.where(lanes == ROUTER + e, d_gate, 0.0)
-            add_rows(acc8, tile8, source, base)
-            return carry
-
-        def blank(i, carry):
-            r = pl.ds(pl.multiple_of(i * TILE, TILE), TILE)
-            dy_ref[0, r, :] = jnp.zeros((TILE, D), BF16)
-            dg_ref[0, r, :] = jnp.zeros((TILE, 2 * hidden), BF16)
-            h_ref[0, r, :] = jnp.zeros((TILE, hidden), BF16)
-            return carry
-
-        lax.fori_loop(0, used, step, 0)
-        lax.fori_loop(used, tiles, blank, 0)
-
-    @pl.when(e >= ROUTED_EXPERTS)
+        c0, c1, c2, pc = gathered_columns(tile8, 4)
+        dx = jnp.concatenate([c0, c1, c2], axis=1)
+        d_value = jnp.sum(y_ref[...] * dx, axis=1, keepdims=True)
+        dy = (dx * lane_of(pc, ROUTER + e)).astype(BF16)
+        pick_rows(rows8, tile8, source, after[s])
+        back = run(dy)
+        spread_rows(done8, back, order[s] * TILE, TILE)
+        done8[pl.ds(order[s] * TILE * 8 + 3, TILE, stride=8), :] = jnp.where(lanes == ROUTER + e, d_value, 0.0)
+
+    @pl.when((order[s] < 0) & (s < routed))
     def _():
-        def step(i, carry):
-            t = (e - ROUTED_EXPERTS) * tiles + i
-            here = pl.ds(pl.multiple_of(i * TILE, TILE), TILE)
-            r = pl.ds(pl.multiple_of(t * TILE, TILE), TILE)
-            dx = dx_ref[r, :]
-            d_gate = jnp.sum(y_ref[0, here, :] * dx, axis=1, keepdims=True)
-            back = run(here, (dx * lane_of(pc_ref[r, :], SHARED)).astype(BF16))
-            for c in range(D // LANES):
-                cols = slice(c * LANES, (c + 1) * LANES)
-                acc_ref[r, cols] = acc8[pl.ds(t * TILE * 8 + c, TILE, stride=8), :] + back[:, cols]
-            acc_ref[r, D:] = jnp.where(
-                lanes == SHARED, d_gate, acc8[pl.ds(t * TILE * 8 + 3, TILE, stride=8), :])
-            return carry
-
-        lax.fori_loop(0, tiles, step, 0)
-
-
-def expert_backward(counts, source, pc, dx, weights, x, y):
+        dy_ref[...] = jnp.zeros_like(dy_ref)
+        dg_ref[...] = jnp.zeros_like(dg_ref)
+        h_ref[...] = jnp.zeros_like(h_ref)
+
+    @pl.when(s >= routed)
+    def _():
+        r = block(s - routed, TILE)
+        dx = dx_ref[r, :]
+        d_value = jnp.sum(y_ref[...] * dx, axis=1, keepdims=True)
+        sum_rows(done8, sum8, slots, (s - routed) * TILE, tokens)
+        back = run((dx * lane_of(pc_ref[r, :], SHARED)).astype(BF16))
+        sums = gathered_columns(sum8, D // LANES + 1)
+        for c in range(D // LANES):
+            cols = slice(c * LANES, (c + 1) * LANES)
+            acc_ref[r, cols] = sums[c] + back[:, cols]
+        acc_ref[r, D:] = jnp.where(lanes == SHARED, d_value, sums[-1])
+
+
+def expert_backward(plan, pc, dx, weights, x, y):
     tokens = dx.shape[0]
-    capacity = tokens // 2
-    blocks = ROUTED_EXPERTS + 2
     hidden = weights.shape[2] // 3
-    full = lambda shape: pl.BlockSpec(shape, lambda e, *_: (0,) * len(shape), pipeline_mode=pl.Buffered(1))
+    tiles, full, tile, weight, scratch = expert_specs(tokens, weights)
     return pl.pallas_call(
         expert_backward_kernel,
         grid_spec=pltpu.PrefetchScalarGridSpec(
-            num_scalar_prefetch=2,
-            grid=(blocks,),
-            in_specs=[
-                full(pc.shape), full(dx.shape), expert_weights(weights),
-                expert_blocks(capacity, D), expert_blocks(capacity, D)],
-            out_specs=[
-                expert_blocks(capacity, D), expert_blocks(capacity, 2 * hidden), expert_blocks(capacity, hidden),
-                full((tokens, D + LANES))],
-            scratch_shapes=expert_scratch(tokens),
+            num_scalar_prefetch=4,
+            grid=(tiles,),
+            in_specs=[full(pc.shape), full(dx.shape), weight, tile(D), tile(D)],
+            out_specs=[tile(D), tile(2 * hidden), tile(hidden), full((tokens, D + LANES))],
+            scratch_shapes=scratch,
         ),
         out_shape=[
-            jax.ShapeDtypeStruct((blocks, capacity, D), BF16),
-            jax.ShapeDtypeStruct((blocks, capacity, 2 * hidden), BF16),
-            jax.ShapeDtypeStruct((blocks, capacity, hidden), BF16),
+            jax.ShapeDtypeStruct((tiles * TILE, D), BF16),
+            jax.ShapeDtypeStruct((tiles * TILE, 2 * hidden), BF16),
+            jax.ShapeDtypeStruct((tiles * TILE, hidden), BF16),
             jax.ShapeDtypeStruct((tokens, D + LANES), F32),
         ],
         compiler_params=params(),
         name="expert_backward",
-    )(counts, source, pc, dx, weights, x, y)
+    )(*plan, pc, dx, weights, x, y)
 
 
 def exchange(part, other, send_sem, recv_sem):
@@ -1418,9 +1376,22 @@
     found = jnp.einsum("teh,tel->ehl", left, low, preferred_element_type=F32)
     half = capacity // LANES
     source = (found[:, :half] * 16.0 + found[:, half:]).reshape(ROUTED_EXPERTS, capacity).astype(jnp.int32)
-    slots = jnp.arange(capacity, dtype=jnp.int32)
-    source = jnp.where(slots[None, :] < total[:, None], source, tokens)
-    return total, source.reshape(-1)
+    source = jnp.where(jnp.arange(capacity, dtype=jnp.int32)[None, :] < total[:, None], source, tokens)
+    source = jnp.concatenate([source.reshape(-1), jnp.full((TILE,), tokens, jnp.int32)]) * 8
+    per = capacity // TILE
+    routed = ROUTED_EXPERTS * per
+    tile = jnp.arange(routed + tokens // TILE, dtype=jnp.int32)
+    need = (total + TILE - 1) // TILE
+    begin = jnp.sum(jnp.where(experts[None, :] < experts[:, None], need[None, :], 0), axis=1)
+    mine = jnp.minimum(tile // per, ROUTED_EXPERTS - 1)[:, None] == experts[None, :]
+    used = (tile < routed) & (tile % per < jnp.sum(jnp.where(mine, need[None, :], 0), axis=1))
+    order = jnp.where(used, jnp.sum(jnp.where(mine, begin[None, :], 0), axis=1) + tile % per, -1)
+    next_tile = jnp.concatenate([tile, jnp.full((1,), -1, jnp.int32)])
+    later = used[None, :] & (tile[None, :] > next_tile[:, None])
+    after = jnp.min(jnp.where(later, tile[None, :], routed), axis=1) * TILE
+    slot = (begin[None, :] * TILE + count - 1) * 8
+    slots = jnp.sum(jnp.where(route_rows[:, :, None] == experts[None, None, :], slot[:, None, :], 0), axis=2)
+    return total, (order, after, source, slots.T.reshape(-1))
 
 
 def adam_update(master, moment, square, gradient, factor, bias_one, bias_two, step_rate):
@@ -1459,7 +1430,7 @@
         [upward_proj.astype(BF16).reshape(experts, shard, 2 * hidden), downward_proj.transpose(0, 2, 1).astype(BF16)],
         axis=2)
     marks = observed.astype(F32)
-    expert_here, source = dispatch(routes.reshape(tokens, 2), capacity)
+    expert_here, plan = dispatch(routes.reshape(tokens, 2), capacity)
     point = jnp.arange(length, dtype=F32)
     head_here = jnp.stack(
         [jnp.sum(jnp.sum(marks, axis=0) * jnp.minimum(point, float(horizon))) for horizon in horizons])
@@ -1475,17 +1446,18 @@
     expert_count, head_count = tally[:ROUTED_EXPERTS], tally[ROUTED_EXPERTS:ROUTED_EXPERTS + 4]
     total_tokens = tokens * dp_count
 
-    xs, ys, mixed = expert_forward(expert_here, source, b, pc, big)
+    xs, ys, mixed = expert_forward(plan, b, pc, big)
     head_weight = jnp.concatenate(
         [jnp.zeros((horizon,), F32) + 0.25 / head_count[3 - index] for index, horizon in enumerate(horizons[::-1])])
     head_weight = jnp.pad(head_weight, (0, LANES - head_weight.shape[0]))[None]
     dx2, d_table, d_gain3, fit = loss_stage(
         mixed, x1, vec, table, table_t, hankel_rows(series), hankel_rows(marks), head_weight, 1)
-    dys, dgs, hs, back = expert_backward(expert_here, source, pc, dx2, big, xs, ys)
+    dys, dgs, hs, back = expert_backward(plan, pc, dx2, big, xs, ys)
     balance = aux_factor * ROUTED_EXPERTS * expert_count / total_tokens / total_tokens
     balance = jnp.pad(balance, (ROUTER, LANES - SHARED))[None]
     local_loss = jnp.sum(fit) + jnp.sum(pr_total * balance)
     dx1, do, rest = mid_backward(back, dx2, x1, b, pc, vec, table_t, balance, wo, o, d_table, d_gain3, 2)
+    xs, dys, dgs, hs = [v.reshape(-1, capacity, v.shape[1]) for v in (xs, dys, dgs, hs)]
     big_red, small_red = backward_near(xs, dys, dgs, hs, qkv, do, lse, a, dx1, rest, x, wt, vec, cos, sin, 3)
 
     attn_red, table_red = small_red[:, :4 * width], small_red[:, 4 * width:]

time: 575 us -> 585 us (1.017)
  Pallas kernels: 513 us -> 520 us
    pallas_call x1, Pallas kernels: 67.7 us -> 74 us  [expert_backward(): pl.pallas_call(expert_backward_kernel, grid_spec=pltpu.PrefetchScalarGrid...]
where the time goes in v4:
time: 585 us; the launch traced here: 583 us
  Pallas kernels  520 us (89%)
  other arithmetic  31.1 us (5%)
  local copies, waits for them, and re-layouts  18.7 us (3%)
  between operations  9.75 us (2%)
    pallas_call x1, Pallas kernels, backward_near(): pl.pallas_call(backward_kernel, in_specs=[ANY] * 10 + [VMEM] * 5, out_spe...  199 us
    pallas_call x1, Pallas kernels, forward_near(): pl.pallas_call(forward_kernel, in_specs=[VMEM, ANY, VMEM, VMEM, VMEM, VME...  160 us
    pallas_call x1, Pallas kernels, expert_backward(): pl.pallas_call(expert_backward_kernel, grid_spec=pltpu.PrefetchScalarGrid...  74 us
    pallas_call x1, Pallas kernels, expert_forward(): pl.pallas_call(expert_forward_kernel, grid_spec=pltpu.PrefetchScalarGridS...  50.2 us
    pallas_call x1, Pallas kernels, mid_backward(): pl.pallas_call(mid_backward_kernel, in_specs=[VMEM] * 12, out_specs=[VMEM...  15.3 us
    pallas_call x1, Pallas kernels, loss_stage(): pl.pallas_call(loss_kernel, in_specs=[VMEM] * 8, out_specs=[VMEM] * 4, ou...  12.9 us

profile of v4, /device:TPU:0, one launch (start us, length us, event | category | flops | bytes accessed | tf_op | source)
XLA Modules:
  0.0 582.9 jit_solution(12502884651005460261)
XLA Ops:
  0.7 0.7 fusion.9
  1.4 2.3 reduce-window.6
  3.7 0.3 slice_reduce_fusion
  4.0 0.2 reduce-window.9
  4.2 0.1 add_bitcast_fusion
  4.3 0.2 slice_reduce_fusion.3
  4.5 0.1 select_reduce_fusion.3
  4.6 0.1 select_reduce_fusion.4
  4.7 0.5 add_select_fusion.5.order
  5.2 0.7 select_reduce_fusion.1
  6.0 0.5 broadcast_multiply_fusion.2.after
  6.6 0.2 select_convert_fusion.1
  6.8 3.7 fusion
  10.6 0.6 pad_multiply_fusion.source
  11.3 0.6 copy.99
  12.1 0.1 rev.30
  12.2 0.1 rev.31
  12.4 0.1 rev.32
  12.6 0.1 copy.88
  12.7 0.7 concatenate.30.small_own
  13.5 0.5 convert_element_type.89
  13.9 0.4 reshape.213
  14.4 1.0 pad_maximum_fusion.big_own
  15.4 0.1 pad_slice_fusion.3
  15.5 0.6 multiply_reduce_fusion.3
  16.1 2.7 concatenate.32
  18.8 0.6 broadcast_in_dim.145.tally
  19.4 0.6 reshape.214.x_ref
  20.0 1.0 fusion.11
  21.0 159.7 %forward_near.1 = (bf16[9,384,2304]{2,1,0:T(8,128)(2,1)}, bf16[896,384]{1,0:T(8,128)(2,1)}, f32[8,384]{1,0:T(8,128)}, bf16[384,128]{1,0:T(8,128)(2,1)}, bf16[204...) custom-call(bf16[24,896]{1,0:T(8,128)(2,1)} %concatenate.30.small_ow, ...), custom_call_target="tpu_custom_call" | custom-call | tf_op jit(solution)/shard_map/forward_near/pallas_call | solution.py:440
  180.7 50.2 %expert_forward.1 = (bf16[10240,384]{1,0:T(8,128)(2,1)}, f32[10240,384]{1,0:T(8,128)}, f32[2048,384]{1,0:T(8,128)}) custom-call(s32[40]{0:T(128)} %add_select_fusion.5.order, s32[41]{0:T(128)} %broadcast_multiply_fusion.2.after, s32[8448]{0:T(1024)} %pad_multiply_fusion.source, s32[4096]{0:T(1024)} %bitcast.104, ...), custom_call_target="tpu_custom_call" | custom-call | tf_op jit(solution)/shard_map/expert_forward/pallas_call | solution.py:581
  230.8 1.5 slice.157.table_t
  232.8 0.6 pad_maximum_fusion.1
  233.5 1.0 slice_reduce_fusion.2
  234.4 0.6 fusion.48
  237.8 0.6 fusion.36.weight
  238.4 12.9 %loss_stage.1 = (f32[2048,384]{1,0:T(8,128)}, f32[128,384]{1,0:T(8,128)}, f32[1,384]{1,0:T(1,128)}, f32[1,128]{1,0:T(1,128)}) custom-call(f32[2048,384]{1,0:T(8,128)} %get-tuple-element.53.part, f32[2048,384]{1,0:T(8,128)} %get-tuple-element.54.x1, f32[8,384]{1,0:T(8,128)} %get-tuple-element.55.vec, bf16[384,128]{1,0:T(8,128)(2,1)} %get-tuple-element.56.table, ...), custom_call_target="tpu_custom_call" | custom-call | tf_op jit(solution)/shard_map/loss_stage/pallas_call | solution.py:765
  251.3 1.3 reduce_sum.169
  252.6 0.7 multiply_reduce_fusion.7
  254.5 74.0 %expert_backward.1 = (bf16[10240,384]{1,0:T(8,128)(2,1)}, bf16[10240,1536]{1,0:T(8,128)(2,1)}, bf16[10240,768]{1,0:T(8,128)(2,1)}, f32[2048,512]{1,0:T(8,128)}) custom-call(s32[40]{0:T(128)} %add_select_fusion.5.order, s32[41]{0:T(128)} %broadcast_multiply_fusion.2.after, s32[8448]{0:T(1024)} %pad_multiply_fusion.source, s32[4096]{0:T(1024)} %bitcast.105, ...), custom_call_target="tpu_custom_call" | custom-call | tf_op jit(solution)/shard_map/expert_backward/pallas_call | solution.py:666
  328.5 0.6 pad_bitcast_fusion.balance
  329.1 1.6 slice.168.wo
  330.7 15.3 %mid_backward.1 = (f32[2048,384]{1,0:T(8,128)}, bf16[2,192,1024]{2,1,0:T(8,128)(2,1)}, f32[320,384]{1,0:T(8,128)}) custom-call(f32[2048,512]{1,0:T(8,128)} %get-tuple-element.65.part, f32[2048,384]{1,0:T(8,128)} %get-tuple-element.59.dx_ref.dx2, f32[2048,384]{1,0:T(8,128)} %get-tuple-element.54.x1, bf16[2048,384]{1,0:T(8,128)(2,1)} %get-tuple-element.49.b_ref.b, ...), custom_call_target="tpu_custom_call" | custom-call | tf_op jit(solution)/shard_map/mid_backward/pallas_call | solution.py:820
  346.0 198.7 %backward_near.1 = (f32[9,24,2304]{2,1,0:T(8,128)}, f32[24,896]{1,0:T(8,128)}) custom-call(bf16[10,1024,384]{2,1,0:T(8,128)(2,1)} %bitcast.100, bf16[10,1024,384]{2,1,0:T(8,128)(2,1)} %bitcast.102, bf16[10,1024,1536]{2,1,0:T(8,128)(2,1)} %bitcast.99, bf16[10,1024,768]{2,1,0:T(8,128)(2,1)} %bitcast.101, bf16[2,576,1024]{2,1,0:T(8,128)(2,1)} %get-tuple-element.64.qkvs, ...), custom_call_target="tpu_custom_call" | custom-call | tf_op jit(solution)/shard_map/backward_near/pallas_call | solution.py:1270
  544.7 2.8 multiply_reduce_fusion
  547.5 0.6 multiply_reduce_fusion.1
  549.5 0.6 multiply_reduce_fusion.2
  550.8 0.6 broadcast_in_dim.148.value
  551.4 8.9 %all_blocks.1 = f32[32,8,128]{2,1,0:T(8,128)} custom-call(f32[8,128]{1,0:T(8,128)} %broadcast_in_dim.148.value), custom_call_target="tpu_custom_call" | custom-call | tf_op jit(solution)/shard_map/all_blocks/pallas_call | solution.py:1320
  560.3 1.0 slice_reduce_fusion.1
  561.3 0.6 fusion.47
  563.4 0.7 multiply_subtract_fusion.2
  564.1 0.7 multiply_subtract_fusion.3
  564.8 1.2 slice_multiply_fusion
  566.1 3.1 mul.357
  569.2 7.3 %multiply_subtract_fusion = (f32[9,24,2,768]{3,2,1,0:T(2,128)}, f32[9,24,2,768]{3,2,1,0:T(2,128)}, f32[9,24,2,768]{3,2,1,0:T(2,128)}) fusion(f32[9,24,2,768]{3,2,1,0:T(2,128)S(1)} %copy-done.2, f32[]{:T(128)} %bitcast.33, f32[]{:T(128)} %bitcast.32, f32[9,24,2,768]{3,2,1,0:T(2,128)} %mul.357, f32[9,24,2,768]{3,2,1,0:T(2,128)} %param.34, ...), kind=kLoop, calls=%fused_computation.6 | loop fusion | flops 4976640 | bytes 9289736 | tf_op jit(solution)/shard_map/sub | solution.py:1401
  576.5 1.6 multiply_subtract_fusion.1
  578.7 0.6 multiply_subtract_fusion.5
  579.4 0.1 copy.93
  579.6 0.1 copy.89
  579.6 0.1 multiply_subtract_fusion.4
  579.7 0.7 copy.94
  580.4 0.7 copy.95
  581.1 0.7 copy.96
  (103 shorter events, 2.1 us)
Async XLA Ops:
  6.8 4.5 copy-start.13
  6.8 5.2 copy-start.8
  6.8 5.2 copy-start.10
  6.8 5.2 copy-start.14
  6.8 5.8 copy-start.18
  6.8 6.6 %copy-start.3 = (f32[9,768,24]{1,2,0:T(8,128)S(1)}, f32[9,768,24]{1,2,0:T(8,128)}, u32[]{:S(2)}) copy-start(f32[9,768,24]{1,2,0:T(8,128)} %param.35) | copy-start | bytes 1990660
  10.5 2.9 copy-start.1
  14.4 1.0 copy-start.15
  14.4 1.0 copy-start.21
  238.4 14.2 %copy-start.24 = (f32[1,128]{1,0:T(1,128)S(1)}, f32[1,128]{1,0:T(1,128)}, u32[]{:S(2)}) copy-start(f32[1,128]{1,0:T(1,128)} %get-tuple-element.77) | copy-start | bytes 1540
  544.6 2.9 copy-start.5
  544.7 18.7 %copy-start.9 = (f32[3,24,192]{2,1,0:T(8,128)S(1)}, f32[3,24,192]{2,1,0:T(8,128)}, u32[]{:S(2)}) copy-start(f32[3,24,192]{2,1,0:T(8,128)} %param.26) | copy-start | bytes 165892
  544.7 18.7 %copy-start.11 = (f32[3,24,192]{2,1,0:T(8,128)S(1)}, f32[3,24,192]{2,1,0:T(8,128)}, u32[]{:S(2)}) copy-start(f32[3,24,192]{2,1,0:T(8,128)} %param.28) | copy-start | bytes 165892
  544.7 18.7 %copy-start.12 = (f32[3,24,192]{2,1,0:T(8,128)S(1)}, f32[3,24,192]{2,1,0:T(8,128)}, u32[]{:S(2)}) copy-start(f32[3,24,192]{2,1,0:T(8,128)} %param.27) | copy-start | bytes 165892
  544.7 19.4 %copy-start.16 = (f32[192,24]{0,1:T(8,128)S(1)}, f32[192,24]{0,1:T(8,128)}, u32[]{:S(2)}) copy-start(f32[192,24]{0,1:T(8,128)} %param.31) | copy-start | bytes 55300
  544.7 19.4 %copy-start.17 = (f32[192,24]{0,1:T(8,128)S(1)}, f32[192,24]{0,1:T(8,128)}, u32[]{:S(2)}) copy-start(f32[192,24]{0,1:T(8,128)} %param.30) | copy-start | bytes 55300
  544.7 20.1 %copy-start = (f32[9,24,2304]{2,1,0:T(8,128)S(1)}, f32[9,24,2304]{2,1,0:T(8,128)}, u32[]{:S(2)}) copy-start(f32[9,24,2304]{2,1,0:T(8,128)} %get-tuple-element.74) | copy-start | bytes 5971972
  566.1 3.1 copy-start.2
  569.2 7.3 %copy-start.4 = (f32[9,768,24]{1,2,0:T(8,128)S(1)}, f32[9,768,24]{1,2,0:T(8,128)}, u32[]{:S(2)}) copy-start(f32[9,768,24]{1,2,0:T(8,128)} %param.35) | copy-start | bytes 1990660
  569.2 7.3 %copy-start.6 = (f32[9,768,24]{1,2,0:T(8,128)S(1)}, f32[9,768,24]{1,2,0:T(8,128)}, u32[]{:S(2)}) copy-start(f32[9,768,24]{1,2,0:T(8,128)} %param.37) | copy-start | bytes 1990660
  569.2 7.3 %copy-start.7 = (f32[9,768,24]{1,2,0:T(8,128)S(1)}, f32[9,768,24]{1,2,0:T(8,128)}, u32[]{:S(2)}) copy-start(f32[9,768,24]{1,2,0:T(8,128)} %param.36) | copy-start | bytes 1990660
  576.5 2.3 copy-start.19
  576.5 2.3 copy-start.20
  576.5 3.0 copy-start.22
  576.5 3.0 copy-start.23

commit v5 on v4

--- a/solution.py
+++ b/solution.py
@@ -510,23 +510,42 @@
     rows8[pl.ds(tokens * 8, 8), :] = jnp.zeros((8, LANES), F32)
 
 
-def expert_of(s, tokens):
-    return jnp.minimum(s // (tokens // 2 // TILE), ROUTED_EXPERTS)
+def expert_tiles(e, used, capacity, tile, blank, shared):
+    tiles = capacity // TILE
+
+    @pl.when(e < ROUTED_EXPERTS)
+    def _():
+        def one(i, carry):
+            tile(e * tiles + i, block(i, TILE))
+            return carry
+
+        def none(i, carry):
+            blank(block(i, TILE))
+            return carry
+
+        lax.fori_loop(0, used[e], one, 0)
+        lax.fori_loop(used[e], tiles, none, 0)
+
+    @pl.when(e >= ROUTED_EXPERTS)
+    def _():
+        def one(i, carry):
+            shared((e - ROUTED_EXPERTS) * tiles + i, block(i, TILE))
+            return carry
+
+        lax.fori_loop(0, tiles, one, 0)
 
 
 def expert_forward_kernel(
-    order, after, source, slots, b_ref, pc_ref, w_ref, x_ref, y_ref, mix_ref, rows8, done8, tile8, sum8
+    used, order, after, source, slots, b_ref, pc_ref, w_ref, x_ref, y_ref, mix_ref, rows8, done8, tile8, sum8
 ):
-    s = pl.program_id(0)
+    e = pl.program_id(0)
     tokens = b_ref.shape[0]
     hidden = w_ref.shape[2] // 3
-    routed = ROUTED_EXPERTS * (tokens // 2 // TILE)
-    e = expert_of(s, tokens)
-
-    @pl.when(s == 0)
+
+    @pl.when(e == 0)
     def _():
         lay_rows(b_ref, pc_ref, rows8)
-        pick_rows(rows8, tile8, source, after[pl.num_programs(0)])
+        pick_rows(rows8, tile8, source, after[after.shape[0] - 1])
 
     def run(x):
         g = dot(x, w_ref[0, :, : 2 * hidden])
@@ -534,62 +553,59 @@
         h = (gate * sigmoid(gate) * up).astype(BF16)
         return dot(h, w_ref[0, :, 2 * hidden:], 1, 1)
 
-    @pl.when(order[s] >= 0)
-    def _():
+    def tile(s, here):
         c0, c1, c2, pc = gathered_columns(tile8, 4)
         x = jnp.concatenate([c0, c1, c2], axis=1).astype(BF16)
-        x_ref[...] = x
+        x_ref[0, here, :] = x
         gate_column = lane_of(pc, ROUTER + e)
         pick_rows(rows8, tile8, source, after[s])
         y = run(x)
-        y_ref[...] = y
-        spread_rows(done8, y * gate_column, order[s] * TILE, TILE)
-
-    @pl.when((order[s] < 0) & (s < routed))
-    def _():
-        x_ref[...] = jnp.zeros_like(x_ref)
-
-    @pl.when(s >= routed)
-    def _():
-        r = block(s - routed, TILE)
+        y_ref[0, here, :] = y
+        spread_rows(done8, y * gate_column, order[s], TILE)
+
+    def blank(here):
+        x_ref[0, here, :] = jnp.zeros((TILE, D), BF16)
+
+    def shared(j, here):
+        r = block(j, TILE)
         x = b_ref[r, :]
-        x_ref[...] = x
-        sum_rows(done8, sum8, slots, (s - routed) * TILE, tokens)
+        x_ref[0, here, :] = x
+        sum_rows(done8, sum8, slots, j * TILE, tokens)
         y = run(x)
-        y_ref[...] = y
-        shared = y * lane_of(pc_ref[r, :], SHARED)
+        y_ref[0, here, :] = y
+        scaled = y * lane_of(pc_ref[r, :], SHARED)
         for c, part in enumerate(gathered_columns(sum8, D // LANES)):
             cols = slice(c * LANES, (c + 1) * LANES)
-            mix_ref[r, cols] = part + shared[:, cols]
+            mix_ref[r, cols] = part + scaled[:, cols]
+
+    expert_tiles(e, used, y_ref.shape[1], tile, blank, shared)
 
 
 def expert_specs(tokens, weights):
-    tiles = 5 * tokens // TILE
-    full = lambda shape: pl.BlockSpec(shape, lambda s, *_: (0,) * len(shape), pipeline_mode=pl.Buffered(1))
-    tile = lambda w: pl.BlockSpec((TILE, w), lambda s, *_: (s, 0))
-    weight = pl.BlockSpec((1,) + weights.shape[1:], lambda s, *_: (expert_of(s, tokens), 0, 0))
-    most = 2 * tokens // TILE + ROUTED_EXPERTS - 1
+    full = lambda shape: pl.BlockSpec(shape, lambda e, *_: (0,) * len(shape), pipeline_mode=pl.Buffered(1))
+    tile = lambda w: pl.BlockSpec((1, tokens // 2, w), lambda e, *_: (e, 0, 0))
+    weight = pl.BlockSpec((1,) + weights.shape[1:], lambda e, *_: (jnp.minimum(e, ROUTED_EXPERTS), 0, 0))
     scratch = [
-        pltpu.VMEM(((tokens + 1) * 8, LANES), F32), pltpu.VMEM((most * TILE * 8, LANES), F32),
+        pltpu.VMEM(((tokens + 1) * 8, LANES), F32), pltpu.VMEM(((2 * tokens + TILE) * 8, LANES), F32),
         pltpu.VMEM((TILE * 8, LANES), F32), pltpu.VMEM((TILE * 8, LANES), F32)]
-    return tiles, full, tile, weight, scratch
+    return full, tile, weight, scratch
 
 
 def expert_forward(plan, b, pc, weights):
     tokens = b.shape[0]
-    tiles, full, tile, weight, scratch = expert_specs(tokens, weights)
+    full, tile, weight, scratch = expert_specs(tokens, weights)
     return pl.pallas_call(
         expert_forward_kernel,
         grid_spec=pltpu.PrefetchScalarGridSpec(
-            num_scalar_prefetch=4,
-            grid=(tiles,),
+            num_scalar_prefetch=5,
+            grid=(ROUTED_EXPERTS + 2,),
             in_specs=[full(b.shape), full(pc.shape), weight],
             out_specs=[tile(D), tile(D), full((tokens, D))],
             scratch_shapes=scratch,
         ),
         out_shape=[
-            jax.ShapeDtypeStruct((tiles * TILE, D), BF16),
-            jax.ShapeDtypeStruct((tiles * TILE, D), F32),
+            jax.ShapeDtypeStruct((ROUTED_EXPERTS + 2, tokens // 2, D), BF16),
+            jax.ShapeDtypeStruct((ROUTED_EXPERTS + 2, tokens // 2, D), F32),
             jax.ShapeDtypeStruct((tokens, D), F32),
         ],
         compiler_params=params(),
@@ -598,84 +614,81 @@
 
 
 def expert_backward_kernel(
-    order, after, source, slots, pc_ref, dx_ref, w_ref, x_ref, y_ref, dy_ref, dg_ref, h_ref, acc_ref,
+    used, order, after, source, slots, pc_ref, dx_ref, w_ref, x_ref, y_ref, dy_ref, dg_ref, h_ref, acc_ref,
     rows8, done8, tile8, sum8,
 ):
-    s = pl.program_id(0)
+    e = pl.program_id(0)
     tokens = dx_ref.shape[0]
     hidden = w_ref.shape[2] // 3
-    routed = ROUTED_EXPERTS * (tokens // 2 // TILE)
-    e = expert_of(s, tokens)
     lanes = lax.broadcasted_iota(jnp.int32, (TILE, LANES), 1)
 
-    @pl.when(s == 0)
+    @pl.when(e == 0)
     def _():
         lay_rows(dx_ref, pc_ref, rows8)
-        pick_rows(rows8, tile8, source, after[pl.num_programs(0)])
-
-    def run(dy):
-        dy_ref[...] = dy
+        pick_rows(rows8, tile8, source, after[after.shape[0] - 1])
+
+    def run(here, dy):
+        dy_ref[0, here, :] = dy
         u = w_ref[0, :, : 2 * hidden]
-        g = dot(x_ref[...], u)
+        g = dot(x_ref[0, here, :], u)
         gate, up = g[:, :hidden], g[:, hidden:]
         sig = sigmoid(gate)
         silu = gate * sig
-        h_ref[...] = (silu * up).astype(BF16)
+        h_ref[0, here, :] = (silu * up).astype(BF16)
         dh = dot(dy, w_ref[0, :, 2 * hidden:])
         d_up = (dh * silu).astype(BF16)
         d_gate = (dh * up * (sig * (1.0 + gate * (1.0 - sig)))).astype(BF16)
-        dg_ref[:, :hidden] = d_gate
-        dg_ref[:, hidden:] = d_up
+        dg_ref[0, here, :hidden] = d_gate
+        dg_ref[0, here, hidden:] = d_up
         return dot(d_gate, u[:, :hidden], 1, 1) + dot(d_up, u[:, hidden:], 1, 1)
 
-    @pl.when(order[s] >= 0)
-    def _():
+    def tile(s, here):
         c0, c1, c2, pc = gathered_columns(tile8, 4)
         dx = jnp.concatenate([c0, c1, c2], axis=1)
-        d_value = jnp.sum(y_ref[...] * dx, axis=1, keepdims=True)
+        d_value = jnp.sum(y_ref[0, here, :] * dx, axis=1, keepdims=True)
         dy = (dx * lane_of(pc, ROUTER + e)).astype(BF16)
         pick_rows(rows8, tile8, source, after[s])
-        back = run(dy)
-        spread_rows(done8, back, order[s] * TILE, TILE)
-        done8[pl.ds(order[s] * TILE * 8 + 3, TILE, stride=8), :] = jnp.where(lanes == ROUTER + e, d_value, 0.0)
-
-    @pl.when((order[s] < 0) & (s < routed))
-    def _():
-        dy_ref[...] = jnp.zeros_like(dy_ref)
-        dg_ref[...] = jnp.zeros_like(dg_ref)
-        h_ref[...] = jnp.zeros_like(h_ref)
-
-    @pl.when(s >= routed)
-    def _():
-        r = block(s - routed, TILE)
+        back = run(here, dy)
+        spread_rows(done8, back, order[s], TILE)
+        done8[pl.ds(order[s] * 8 + 3, TILE, stride=8), :] = jnp.where(lanes == ROUTER + e, d_value, 0.0)
+
+    def blank(here):
+        dy_ref[0, here, :] = jnp.zeros((TILE, D), BF16)
+        dg_ref[0, here, :] = jnp.zeros((TILE, 2 * hidden), BF16)
+        h_ref[0, here, :] = jnp.zeros((TILE, hidden), BF16)
+
+    def shared(j, here):
+        r = block(j, TILE)
         dx = dx_ref[r, :]
-        d_value = jnp.sum(y_ref[...] * dx, axis=1, keepdims=True)
-        sum_rows(done8, sum8, slots, (s - routed) * TILE, tokens)
-        back = run((dx * lane_of(pc_ref[r, :], SHARED)).astype(BF16))
+        d_value = jnp.sum(y_ref[0, here, :] * dx, axis=1, keepdims=True)
+        sum_rows(done8, sum8, slots, j * TILE, tokens)
+        back = run(here, (dx * lane_of(pc_ref[r, :], SHARED)).astype(BF16))
         sums = gathered_columns(sum8, D // LANES + 1)
         for c in range(D // LANES):
             cols = slice(c * LANES, (c + 1) * LANES)
             acc_ref[r, cols] = sums[c] + back[:, cols]
         acc_ref[r, D:] = jnp.where(lanes == SHARED, d_value, sums[-1])
 
+    expert_tiles(e, used, y_ref.shape[1], tile, blank, shared)
+
 
 def expert_backward(plan, pc, dx, weights, x, y):
     tokens = dx.shape[0]
     hidden = weights.shape[2] // 3
-    tiles, full, tile, weight, scratch = expert_specs(tokens, weights)
+    full, tile, weight, scratch = expert_specs(tokens, weights)
     return pl.pallas_call(
         expert_backward_kernel,
         grid_spec=pltpu.PrefetchScalarGridSpec(
-            num_scalar_prefetch=4,
-            grid=(tiles,),
+            num_scalar_prefetch=5,
+            grid=(ROUTED_EXPERTS + 2,),
             in_specs=[full(pc.shape), full(dx.shape), weight, tile(D), tile(D)],
             out_specs=[tile(D), tile(2 * hidden), tile(hidden), full((tokens, D + LANES))],
             scratch_shapes=scratch,
         ),
         out_shape=[
-            jax.ShapeDtypeStruct((tiles * TILE, D), BF16),
-            jax.ShapeDtypeStruct((tiles * TILE, 2 * hidden), BF16),
-            jax.ShapeDtypeStruct((tiles * TILE, hidden), BF16),
+            jax.ShapeDtypeStruct((ROUTED_EXPERTS + 2, tokens // 2, D), BF16),
+            jax.ShapeDtypeStruct((ROUTED_EXPERTS + 2, tokens // 2, 2 * hidden), BF16),
+            jax.ShapeDtypeStruct((ROUTED_EXPERTS + 2, tokens // 2, hidden), BF16),
             jax.ShapeDtypeStruct((tokens, D + LANES), F32),
         ],
         compiler_params=params(),
@@ -1382,16 +1395,16 @@
     routed = ROUTED_EXPERTS * per
     tile = jnp.arange(routed + tokens // TILE, dtype=jnp.int32)
     need = (total + TILE - 1) // TILE
-    begin = jnp.sum(jnp.where(experts[None, :] < experts[:, None], need[None, :], 0), axis=1)
+    begin = jnp.sum(jnp.where(experts[None, :] < experts[:, None], total[None, :], 0), axis=1)
     mine = jnp.minimum(tile // per, ROUTED_EXPERTS - 1)[:, None] == experts[None, :]
     used = (tile < routed) & (tile % per < jnp.sum(jnp.where(mine, need[None, :], 0), axis=1))
-    order = jnp.where(used, jnp.sum(jnp.where(mine, begin[None, :], 0), axis=1) + tile % per, -1)
+    order = jnp.where(used, jnp.sum(jnp.where(mine, begin[None, :], 0), axis=1) + tile % per * TILE, -1)
     next_tile = jnp.concatenate([tile, jnp.full((1,), -1, jnp.int32)])
     later = used[None, :] & (tile[None, :] > next_tile[:, None])
     after = jnp.min(jnp.where(later, tile[None, :], routed), axis=1) * TILE
-    slot = (begin[None, :] * TILE + count - 1) * 8
+    slot = (begin[None, :] + count - 1) * 8
     slots = jnp.sum(jnp.where(route_rows[:, :, None] == experts[None, None, :], slot[:, None, :], 0), axis=2)
-    return total, (order, after, source, slots.T.reshape(-1))
+    return total, (need, order, after, source, slots.T.reshape(-1))
 
 
 def adam_update(master, moment, square, gradient, factor, bias_one, bias_two, step_rate):
@@ -1457,7 +1470,6 @@
     balance = jnp.pad(balance, (ROUTER, LANES - SHARED))[None]
     local_loss = jnp.sum(fit) + jnp.sum(pr_total * balance)
     dx1, do, rest = mid_backward(back, dx2, x1, b, pc, vec, table_t, balance, wo, o, d_table, d_gain3, 2)
-    xs, dys, dgs, hs = [v.reshape(-1, capacity, v.shape[1]) for v in (xs, dys, dgs, hs)]
     big_red, small_red = backward_near(xs, dys, dgs, hs, qkv, do, lse, a, dx1, rest, x, wt, vec, cos, sin, 3)
 
     attn_red, table_red = small_red[:, :4 * width], small_red[:, 4 * width:]

time: 585 us -> 554 us (0.947)
  Pallas kernels: 520 us -> 490 us
    pallas_call x1, Pallas kernels: 74 us -> 59.5 us  [expert_backward(): pl.pallas_call(expert_backward_kernel, grid_spec=pltpu.PrefetchScalarGrid...]
    pallas_call x1, Pallas kernels: 50.2 us -> 36.3 us  [expert_forward(): pl.pallas_call(expert_forward_kernel, grid_spec=pltpu.PrefetchScalarGridS...]
where the time goes in v5:
time: 554 us
  Pallas kernels  490 us (88%)
  other arithmetic  31.7 us (6%)
  local copies, waits for them, and re-layouts  18.7 us (3%)
  between operations  9.75 us (2%)
    pallas_call x1, Pallas kernels, backward_near(): pl.pallas_call(backward_kernel, in_specs=[ANY] * 10 + [VMEM] * 5, out_spe...  196 us
    pallas_call x1, Pallas kernels, forward_near(): pl.pallas_call(forward_kernel, in_specs=[VMEM, ANY, VMEM, VMEM, VMEM, VME...  160 us
    pallas_call x1, Pallas kernels, expert_backward(): pl.pallas_call(expert_backward_kernel, grid_spec=pltpu.PrefetchScalarGrid...  59.5 us
    pallas_call x1, Pallas kernels, expert_forward(): pl.pallas_call(expert_forward_kernel, grid_spec=pltpu.PrefetchScalarGridS...  36.3 us
    pallas_call x1, Pallas kernels, mid_backward(): pl.pallas_call(mid_backward_kernel, in_specs=[VMEM] * 12, out_specs=[VMEM...  15.3 us
    pallas_call x1, Pallas kernels, loss_stage(): pl.pallas_call(loss_kernel, in_specs=[VMEM] * 8, out_specs=[VMEM] * 4, ou...  12.9 us

profile of v5, /device:TPU:0, one launch (start us, length us, event | category | flops | bytes accessed | tf_op | source)
XLA Modules:
  0.0 553.9 jit_solution(18221661887669406057)
XLA Ops:
  0.7 0.7 fusion.9
  1.4 2.3 reduce-window.6
  3.7 0.3 slice_reduce_fusion
  4.0 0.2 reduce-window.9
  4.2 0.1 add_bitcast_fusion
  4.3 0.2 fusion.32
  4.5 0.5 fusion.49
  5.0 0.1 select_reduce_fusion.3
  5.1 0.1 select_reduce_fusion.4
  5.2 0.5 add_select_fusion.5.order
  5.8 0.7 select_reduce_fusion.1
  6.5 0.5 broadcast_multiply_fusion.1.after
  7.1 0.2 select_convert_fusion.1
  7.4 3.7 fusion
  11.2 0.6 pad_multiply_fusion.source
  11.8 0.6 copy.99
  12.6 0.1 rev.30
  12.8 0.1 rev.31
  12.9 0.1 rev.32
  13.1 0.1 copy.88
  13.2 0.7 concatenate.30.small_own
  14.0 0.5 convert_element_type.89
  14.5 0.4 reshape.197
  14.9 1.0 pad_maximum_fusion.big_own
  15.9 0.1 pad_slice_fusion.3
  16.0 0.6 multiply_reduce_fusion.3
  16.6 2.7 concatenate.32
  19.3 0.6 broadcast_in_dim.144.tally
  19.9 0.6 reshape.198.x_ref
  20.5 1.0 fusion.11
  21.5 159.7 %forward_near.1 = (bf16[9,384,2304]{2,1,0:T(8,128)(2,1)}, bf16[896,384]{1,0:T(8,128)(2,1)}, f32[8,384]{1,0:T(8,128)}, bf16[384,128]{1,0:T(8,128)(2,1)}, bf16[204...) custom-call(bf16[24,896]{1,0:T(8,128)(2,1)} %concatenate.30.small_ow, ...), custom_call_target="tpu_custom_call" | custom-call | tf_op jit(solution)/shard_map/forward_near/pallas_call | solution.py:440
  181.2 36.3 %expert_forward.1 = (bf16[10,1024,384]{2,1,0:T(8,128)(2,1)}, f32[10,1024,384]{2,1,0:T(8,128)}, f32[2048,384]{1,0:T(8,128)}) custom-call(s32[8]{0:T(128)} %get-tuple-element.230.used, s32[40]{0:T(128)} %add_select_fusion.5.order, s32[41]{0:T(128)} %broadcast_multiply_fusion.1.after, s32[8448]{0:T(1024)} %pad_multiply_fusion.source, s32[4096]{0:T(1024)} %bitcast.96, ...), custom_call_target="tpu_custom_call" | custom-call | tf_op jit(solution)/shard_map/expert_forward/pallas_call | solution.py:597
  217.5 1.5 slice.157.table_t
  219.5 0.6 pad_maximum_fusion.1
  220.1 1.0 slice_reduce_fusion.2
  221.1 0.6 fusion.48
  224.4 0.6 fusion.36.weight
  225.0 12.9 %loss_stage.1 = (f32[2048,384]{1,0:T(8,128)}, f32[128,384]{1,0:T(8,128)}, f32[1,384]{1,0:T(1,128)}, f32[1,128]{1,0:T(1,128)}) custom-call(f32[2048,384]{1,0:T(8,128)} %get-tuple-element.53.part, f32[2048,384]{1,0:T(8,128)} %get-tuple-element.54.x1, f32[8,384]{1,0:T(8,128)} %get-tuple-element.55.vec, bf16[384,128]{1,0:T(8,128)(2,1)} %get-tuple-element.56.table, ...), custom_call_target="tpu_custom_call" | custom-call | tf_op jit(solution)/shard_map/loss_stage/pallas_call | solution.py:778
  237.9 1.3 reduce_sum.169
  239.2 0.7 multiply_reduce_fusion.7
  241.2 59.5 %expert_backward.1 = (bf16[10,1024,384]{2,1,0:T(8,128)(2,1)}, bf16[10,1024,1536]{2,1,0:T(8,128)(2,1)}, bf16[10,1024,768]{2,1,0:T(8,128)(2,1)}, f32[2048,512]{1,0:T(8,128)}) custom-call(s32[8]{0:T(128)} %get-tuple-element.230.used, s32[40]{0:T(128)} %add_select_fusion.5.order, s32[41]{0:T(128)} %broadcast_multiply_fusion.1.after, ...), custom_call_target="tpu_custom_call" | custom-call | tf_op jit(solution)/shard_map/expert_backward/pallas_call | solution.py:679
  300.6 0.6 pad_bitcast_fusion.balance
  301.2 1.6 slice.168.wo
  302.8 15.3 %mid_backward.1 = (f32[2048,384]{1,0:T(8,128)}, bf16[2,192,1024]{2,1,0:T(8,128)(2,1)}, f32[320,384]{1,0:T(8,128)}) custom-call(f32[2048,512]{1,0:T(8,128)} %get-tuple-element.65.part, f32[2048,384]{1,0:T(8,128)} %get-tuple-element.59.dx_ref.dx2, f32[2048,384]{1,0:T(8,128)} %get-tuple-element.54.x1, bf16[2048,384]{1,0:T(8,128)(2,1)} %get-tuple-element.49.b_ref.b, ...), custom_call_target="tpu_custom_call" | custom-call | tf_op jit(solution)/shard_map/mid_backward/pallas_call | solution.py:833
  318.1 196.0 %backward_near.1 = (f32[9,24,2304]{2,1,0:T(8,128)}, f32[24,896]{1,0:T(8,128)}) custom-call(bf16[10,1024,384]{2,1,0:T(8,128)(2,1)} %get-tuple-element.52.x_ref.xs, bf16[10,1024,384]{2,1,0:T(8,128)(2,1)} %get-tuple-element.61.dys, bf16[10,1024,1536]{2,1,0:T(8,128)(2,1)} %get-tuple-element.62.dgs, bf16[10,1024,768]{2,1,0:T(8,128)(2,1)} %get-tuple-element.63.hs, ...), custom_call_target="tpu_custom_call" | custom-call | tf_op jit(solution)/shard_map/backward_near/pallas_call | solution.py:1283
  514.1 2.8 multiply_reduce_fusion
  516.9 0.6 multiply_reduce_fusion.1
  518.9 0.6 multiply_reduce_fusion.2
  520.2 0.6 broadcast_in_dim.147.value
  520.8 10.6 %all_blocks.1 = f32[32,8,128]{2,1,0:T(8,128)} custom-call(f32[8,128]{1,0:T(8,128)} %broadcast_in_dim.147.value), custom_call_target="tpu_custom_call" | custom-call | tf_op jit(solution)/shard_map/all_blocks/pallas_call | solution.py:1333
  531.4 1.0 slice_reduce_fusion.1
  532.3 0.6 fusion.47
  534.5 0.7 multiply_subtract_fusion.2
  535.2 0.7 multiply_subtract_fusion.3
  535.9 1.2 slice_multiply_fusion
  537.1 3.1 mul.356
  540.3 7.3 %multiply_subtract_fusion = (f32[9,24,2,768]{3,2,1,0:T(2,128)}, f32[9,24,2,768]{3,2,1,0:T(2,128)}, f32[9,24,2,768]{3,2,1,0:T(2,128)}) fusion(f32[9,24,2,768]{3,2,1,0:T(2,128)S(1)} %copy-done.2, f32[]{:T(128)} %bitcast.29, f32[]{:T(128)} %bitcast.28, f32[9,24,2,768]{3,2,1,0:T(2,128)} %mul.356, f32[9,24,2,768]{3,2,1,0:T(2,128)} %param.34, ...), kind=kLoop, calls=%fused_computation.6 | loop fusion | flops 4976640 | bytes 9289736 | tf_op jit(solution)/shard_map/sub | solution.py:1414
  547.6 1.6 multiply_subtract_fusion.1
  549.8 0.6 multiply_subtract_fusion.5
  550.5 0.1 copy.93
  550.7 0.1 multiply_subtract_fusion.4
  550.8 0.7 copy.94
  551.5 0.7 copy.95
  552.2 0.7 copy.96
  (102 shorter events, 2.2 us)
Async XLA Ops:
  7.3 4.5 copy-start.13
  7.3 5.2 copy-start.8
  7.3 5.2 copy-start.10
  7.3 5.2 copy-start.14
  7.3 5.8 %copy-start.18 = (f32[5,24]{1,0:T(8,128)S(1)}, f32[5,24]{1,0:T(8,128)}, u32[]{:S(2)}) copy-start(f32[5,24]{1,0:T(8,128)} %param.41) | copy-start | bytes 1444
  7.3 6.6 %copy-start.3 = (f32[9,768,24]{1,2,0:T(8,128)S(1)}, f32[9,768,24]{1,2,0:T(8,128)}, u32[]{:S(2)}) copy-start(f32[9,768,24]{1,2,0:T(8,128)} %param.35) | copy-start | bytes 1990660
  11.1 2.9 copy-start.1
  14.9 1.0 copy-start.15
  14.9 1.0 copy-start.21
  225.0 14.2 %copy-start.24 = (f32[1,128]{1,0:T(1,128)S(1)}, f32[1,128]{1,0:T(1,128)}, u32[]{:S(2)}) copy-start(f32[1,128]{1,0:T(1,128)} %get-tuple-element.77) | copy-start | bytes 1540
  514.0 2.9 copy-start.5
  514.0 20.4 %copy-start.9 = (f32[3,24,192]{2,1,0:T(8,128)S(1)}, f32[3,24,192]{2,1,0:T(8,128)}, u32[]{:S(2)}) copy-start(f32[3,24,192]{2,1,0:T(8,128)} %param.26) | copy-start | bytes 165892
  514.1 20.4 %copy-start.11 = (f32[3,24,192]{2,1,0:T(8,128)S(1)}, f32[3,24,192]{2,1,0:T(8,128)}, u32[]{:S(2)}) copy-start(f32[3,24,192]{2,1,0:T(8,128)} %param.28) | copy-start | bytes 165892
  514.1 20.4 %copy-start.12 = (f32[3,24,192]{2,1,0:T(8,128)S(1)}, f32[3,24,192]{2,1,0:T(8,128)}, u32[]{:S(2)}) copy-start(f32[3,24,192]{2,1,0:T(8,128)} %param.27) | copy-start | bytes 165892
  514.1 21.1 %copy-start.16 = (f32[192,24]{0,1:T(8,128)S(1)}, f32[192,24]{0,1:T(8,128)}, u32[]{:S(2)}) copy-start(f32[192,24]{0,1:T(8,128)} %param.31) | copy-start | bytes 55300
  514.1 21.1 %copy-start.17 = (f32[192,24]{0,1:T(8,128)S(1)}, f32[192,24]{0,1:T(8,128)}, u32[]{:S(2)}) copy-start(f32[192,24]{0,1:T(8,128)} %param.30) | copy-start | bytes 55300
  514.1 21.8 %copy-start = (f32[9,24,2304]{2,1,0:T(8,128)S(1)}, f32[9,24,2304]{2,1,0:T(8,128)}, u32[]{:S(2)}) copy-start(f32[9,24,2304]{2,1,0:T(8,128)} %get-tuple-element.74) | copy-start | bytes 5971972
  537.1 3.1 copy-start.2
  540.3 7.3 %copy-start.4 = (f32[9,768,24]{1,2,0:T(8,128)S(1)}, f32[9,768,24]{1,2,0:T(8,128)}, u32[]{:S(2)}) copy-start(f32[9,768,24]{1,2,0:T(8,128)} %param.35) | copy-start | bytes 1990660
  540.3 7.3 %copy-start.6 = (f32[9,768,24]{1,2,0:T(8,128)S(1)}, f32[9,768,24]{1,2,0:T(8,128)}, u32[]{:S(2)}) copy-start(f32[9,768,24]{1,2,0:T(8,128)} %param.37) | copy-start | bytes 1990660
  540.3 7.3 %copy-start.7 = (f32[9,768,24]{1,2,0:T(8,128)S(1)}, f32[9,768,24]{1,2,0:T(8,128)}, u32[]{:S(2)}) copy-start(f32[9,768,24]{1,2,0:T(8,128)} %param.36) | copy-start | bytes 1990660
  547.5 2.3 copy-start.19
  547.6 2.3 copy-start.20
  547.6 3.0 copy-start.22
  547.6 3.0 copy-start.23

commit v6 on v5

--- a/solution.py
+++ b/solution.py
@@ -869,19 +869,28 @@
         axis=1)
 
 
+def squared(v):
+    v = jnp.sum(v * v, axis=0, keepdims=True)
+    total = v[:, :LANES]
+    for c in range(1, v.shape[1] // LANES):
+        total = total + v[:, c * LANES:(c + 1) * LANES]
+    return total
+
+
 def backward_kernel(
-    xs, dys, dgs, hs, qkvs, dos, lses, a_all, dx1_all, rest, x_ref, wt, vec, cos_ref, sin_ref,
-    out, out_small,
+    xs, dys, dgs, hs, qkvs, dos, lses, a_all, dx1_all, rest, x_ref, wt, vec, cos_ref, sin_ref, losses,
+    out_up, out_down, out_small, sums,
     x_in, dy_in, dg_in, h_in, xt, dyt, temp, dw, acc, send1, recv1, send2, recv2, zs_up, zs_dn, up, dn,
     qkv, do_t, lse, a, dx1, dqkv, dk, dv, stack, part, other,
     sm, small_a1, small_b1, small_a2, small_b2, small_up, small_dn,
     load_sem, sem_s1, sem_r1, sem_s2, sem_r2, sem_su, sem_sd, sem_ru, sem_rd,
     attn_sem, dx1_sem, rest_sem, pair_send, pair_recv,
     small_send, small_sa, small_sb, small_r, small_su, small_sd, small_ru, small_rd,
+    mine, everyone, sum_send, sum_recv,
 ):
     dp, mp, x, y, z = place()
     xp, yp = dp + 1 - 2 * x, dp + 2 - 4 * y
-    count = out.shape[0]
+    count = out_up.shape[0]
     blocks = xs.shape[0]
     hidden = hs.shape[2]
     series, _, length = x_ref.shape
@@ -905,26 +914,8 @@
     for copy in loads(0) + attn_loads(0) + [dx1_load(0), rest_load]:
         copy.start()
 
-    barrier = pltpu.get_barrier_semaphore()
-    for peer, core in ((xp, mp), (yp, mp), (dp, 1 - mp)):
-        pl.semaphore_signal(barrier, inc=1, device_id=(peer, core), device_id_type=MESH)
-
-    @pl.when(z > 0)
-    def _():
-        pl.semaphore_signal(barrier, inc=1, device_id=(dp - 4, mp), device_id_type=MESH)
-
-    @pl.when(z < 3)
-    def _():
-        pl.semaphore_signal(barrier, inc=1, device_id=(dp + 4, mp), device_id_type=MESH)
-
-    @pl.when((z > 0) & (z < 3))
-    def _():
-        pl.semaphore_wait(barrier, 5)
-
-    @pl.when((z == 0) | (z == 3))
-    def _():
-        pl.semaphore_wait(barrier, 4)
-
+    meet_everyone(dp, mp)
+    mine[...] = losses[...]
     stack[0:3 * width, :] = jnp.zeros((3 * width, D), F32)
 
     def shard(slot, i):
@@ -1033,7 +1024,6 @@
             return carry
 
         lax.fori_loop(0, 4, add, 0)
-        out[c] = acc[there, z]
 
         @pl.when(z == 0)
         def _():
@@ -1066,15 +1056,23 @@
             drop(c, 0, True)
 
     def finish(c):
+        there = lax.rem(c, ACCS)
+
         @pl.when(z > 0)
         def _():
             done(up.at[c, z - 1], sem_ru.at[c, z - 1])
-            out[c] = out[c] + decode(up.at[c, z - 1])
+            acc[there, z] = acc[there, z] + decode(up.at[c, z - 1])
 
         @pl.when(z < 3)
         def _():
             done(dn.at[c, z], sem_rd.at[c, z])
-            out[c] = out[c] + decode(dn.at[c, z])
+            acc[there, z] = acc[there, z] + decode(dn.at[c, z])
+        v = acc[there, z]
+        mine[0:1, :] = mine[0:1, :] + squared(v)
+        for r in range(SHARD):
+            for part in range(2):
+                out_up[c, r, part:part + 1, :] = v[r:r + 1, part * hidden:(part + 1) * hidden]
+        out_down[c] = v[:, 2 * hidden:]
 
 
     def pair(n):
@@ -1203,6 +1201,7 @@
         def _():
             done(small_dn.at[z], small_rd.at[z])
             out_small[...] = out_small[...] + small_dn[z]
+        mine[0:1, :] = mine[0:1, :] + squared(out_small[:, :4 * width]) + 0.5 * squared(out_small[:, 4 * width:])
 
 
     def at(i, first, number, run):
@@ -1210,26 +1209,27 @@
         def _():
             run(i - first)
 
-    small_first = count
+    small_first = count + 1
 
     def step(i, carry):
         at(i, 0, count, begin)
 
-        @pl.when(i < series * heads // 2)
-        def _():
-            def two(q, carry):
-                head(2 * i + q)
-                return carry
-            lax.fori_loop(0, 2, two, 0)
-
-        for n in range(series):
-            @pl.when((i >= 3 + n * 3) & (i < 3 + n * 3 + per // 2))
-            def _():
-                def two(q, carry):
-                    embed(n * per + 2 * (i - 3 - n * 3) + q)
-                    return carry
-                lax.fori_loop(0, 2, two, 0)
+        def run(p, carry):
+            head(p)
+            return carry
+
+        @pl.when(i <= count)
+        def _():
+            lax.fori_loop(i, jnp.where(i == count, series * heads, i + 1), run, 0)
+
+        def piece(m, carry):
+            embed(m)
+            return carry
+
+        at(i, heads + 1, 1, lambda _: lax.fori_loop(0, per, piece, 0))
+        at(i, count + 1, 1, lambda _: lax.fori_loop(per, series * per, piece, 0))
         at(i, small_first, 1, lambda _: small_begin())
+        at(i, 7, count, finish)
         at(i, 2, count, fold)
         at(i, small_first + 1, 1, lambda _: small_fold())
         at(i, 4, count, line_a)
@@ -1238,11 +1238,20 @@
         at(i, small_first + 3, 1, lambda _: small_b())
         at(i, 6, count, line_c)
         at(i, small_first + 4, 1, lambda _: small_c())
-        at(i, 7, count, finish)
         at(i, small_first + 5, 1, lambda _: small_finish())
         return carry
 
     lax.fori_loop(0, count + 7, step, 0)
+
+    me = dp * 2 + mp
+
+    def tell(k, carry):
+        peer = lax.rem(me + k, 32)
+        remote(mine, everyone.at[me], sum_send, sum_recv, peer // 2, lax.rem(peer, 2)).start()
+        return carry
+
+    lax.fori_loop(1, 32, tell, 0)
+    everyone[me] = mine[...]
 
     for slot in range(SLOTS):
         done(send1.at[slot], sem_s1.at[slot])
@@ -1268,9 +1277,12 @@
         @pl.when(z > t)
         def _():
             done(small_dn.at[t], small_sd.at[t])
-
-
-def backward_near(xs, dys, dgs, hs, qkv, do, lse, a, dx1, rest, x, wt, vec, cos, sin, ident):
+    done(everyone.at[pl.ds(0, 31)], sum_recv)
+    done(everyone.at[pl.ds(0, 31)], sum_send)
+    sums[...] = jnp.sum(everyone[...], axis=0)
+
+
+def backward_near(xs, dys, dgs, hs, qkv, do, lse, a, dx1, rest, x, wt, vec, cos, sin, losses, ident):
     capacity, hidden = hs.shape[1], hs.shape[2]
     series, rows, length = qkv.shape
     heads_width = rows // 3
@@ -1282,10 +1294,12 @@
     v = pltpu.VMEM
     return pl.pallas_call(
         backward_kernel,
-        in_specs=[ANY] * 10 + [VMEM] * 5,
-        out_specs=[VMEM] * 2,
+        in_specs=[ANY] * 10 + [VMEM] * 6,
+        out_specs=[VMEM] * 4,
         out_shape=[
-            jax.ShapeDtypeStruct((count, SHARD, width), F32), jax.ShapeDtypeStruct((SHARD, small), F32)],
+            jax.ShapeDtypeStruct((count, SHARD, 2, hidden), F32),
+            jax.ShapeDtypeStruct((count, SHARD, hidden), F32), jax.ShapeDtypeStruct((SHARD, small), F32),
+            jax.ShapeDtypeStruct((8, LANES), F32)],
         scratch_shapes=[
             v((capacity, D), BF16), v((capacity, D), BF16), v((capacity, 2 * hidden), BF16), v((capacity, hidden), BF16),
             v((D, capacity), BF16), v((D, capacity), BF16),
@@ -1305,40 +1319,12 @@
             DMA((HOPS, 3)), DMA((HOPS, 3)), DMA((count, 3)), DMA((count, 3)),
             DMA((4,)), DMA, DMA, DMA((series,)), DMA((series,)),
             DMA((2,)), DMA, DMA, DMA((4,)), DMA((3,)), DMA((3,)), DMA((3,)), DMA((3,)),
+            v((8, LANES), F32), v((32, 8, LANES), F32), DMA, DMA,
         ],
         compiler_params=pltpu.CompilerParams(
             vmem_limit_bytes=67_000_000, collective_id=ident, has_side_effects=True),
         name="backward_near",
-    )(xs, dys, dgs, hs, qkv, do, lse, a, dx1, rest, x, wt, vec, cos, sin)
-
-
-def all_kernel(value, out, send_sem, recv_sem):
-    dp, mp = lax.axis_index("dp"), lax.axis_index("mp")
-    me = dp * 2 + mp
-    meet_everyone(dp, mp)
-
-    def tell(k, carry):
-        peer = lax.rem(me + k, 32)
-        remote(value, out.at[me], send_sem, recv_sem, peer // 2, lax.rem(peer, 2)).start()
-        return carry
-
-    lax.fori_loop(1, 32, tell, 0)
-    out[me] = value[...]
-    view = out.at[pl.ds(0, 31)]
-    done(view, recv_sem)
-    done(view, send_sem)
-
-
-def all_blocks(value, ident):
-    return pl.pallas_call(
-        all_kernel,
-        in_specs=[VMEM],
-        out_specs=VMEM,
-        out_shape=jax.ShapeDtypeStruct((32,) + value.shape, value.dtype),
-        scratch_shapes=[DMA, DMA],
-        compiler_params=pltpu.CompilerParams(collective_id=ident, has_side_effects=True),
-        name="all_blocks",
-    )(value)
+    )(xs, dys, dgs, hs, qkv, do, lse, a, dx1, rest, x, wt, vec, cos, sin, losses)
 
 
 def rope_rows(length):
@@ -1468,17 +1454,13 @@
     dys, dgs, hs, back = expert_backward(plan, pc, dx2, big, xs, ys)
     balance = aux_factor * ROUTED_EXPERTS * expert_count / total_tokens / total_tokens
     balance = jnp.pad(balance, (ROUTER, LANES - SHARED))[None]
-    local_loss = jnp.sum(fit) + jnp.sum(pr_total * balance)
     dx1, do, rest = mid_backward(back, dx2, x1, b, pc, vec, table_t, balance, wo, o, d_table, d_gain3, 2)
-    big_red, small_red = backward_near(xs, dys, dgs, hs, qkv, do, lse, a, dx1, rest, x, wt, vec, cos, sin, 3)
+    losses = jnp.pad((fit + pr_total * balance) / mp_count, ((1, 6), (0, 0)))
+    upward_red, down_red, small_red, sums = backward_near(
+        xs, dys, dgs, hs, qkv, do, lse, a, dx1, rest, x, wt, vec, cos, sin, losses, 3)
 
     attn_red, table_red = small_red[:, :4 * width], small_red[:, 4 * width:]
-    squares = (
-        jnp.sum(big_red * big_red) + jnp.sum(attn_red * attn_red) + jnp.sum(table_red * table_red) / mp_count
-    )
-    pair = jnp.pad(jnp.stack([squares, local_loss / mp_count]), (0, LANES - 2))
-    pair = jnp.sum(all_blocks(jnp.broadcast_to(pair[None], (8, LANES)), 4)[:, 0], axis=0)
-    grad_norm, loss_total = jnp.sqrt(pair[0]), pair[1]
+    grad_norm, loss_total = jnp.sqrt(jnp.sum(sums[0])), jnp.sum(sums[1])
 
     factor = clip_limit / (grad_norm + 1e-06)
     steps_taken = step_count[0].astype(F32)
@@ -1490,8 +1472,7 @@
 
     joint_red = jnp.stack([attn_red[:, k * width:(k + 1) * width] for k in range(3)], axis=0)
     mixer_red = attn_red[:, 3 * width:].T
-    upward_red = big_red[:, :, :2 * hidden].reshape(upward_proj.shape)
-    downward_red = big_red[:, :, 2 * hidden:].transpose(0, 2, 1)
+    downward_red = down_red.transpose(0, 2, 1)
     return (
         loss_total,
         grad_norm,

time: 554 us -> 545 us (0.984)
  Pallas kernels: 490 us -> 484 us
    pallas_call x2 -> x1, Pallas kernels: 207 us -> 196 us  [backward_near(): pl.pallas_call(backward_kernel, in_specs=[ANY] * 10 + [VMEM] * 6, out_spe...]
    reduce_sum x6 -> x1, other arithmetic: 6.96 us -> 1.37 us  [on_device(): grad_norm, loss_total = (jnp.sqrt(jnp.sum(sums[0])), jnp.sum(sums[1]))]
where the time goes in v6:
time: 545 us; the launch traced here: 544 us
  Pallas kernels  484 us (89%)
  other arithmetic  30.2 us (6%)
  local copies, waits for them, and re-layouts  20.1 us (4%)
  between operations  6.37 us (1%)
    pallas_call x1, Pallas kernels, backward_near(): pl.pallas_call(backward_kernel, in_specs=[ANY] * 10 + [VMEM] * 6, out_spe...  196 us
    pallas_call x1, Pallas kernels, forward_near(): pl.pallas_call(forward_kernel, in_specs=[VMEM, ANY, VMEM, VMEM, VMEM, VME...  160 us
    pallas_call x1, Pallas kernels, expert_backward(): pl.pallas_call(expert_backward_kernel, grid_spec=pltpu.PrefetchScalarGrid...  61.8 us
    pallas_call x1, Pallas kernels, expert_forward(): pl.pallas_call(expert_forward_kernel, grid_spec=pltpu.PrefetchScalarGridS...  37.8 us
    pallas_call x1, Pallas kernels, mid_backward(): pl.pallas_call(mid_backward_kernel, in_specs=[VMEM] * 12, out_specs=[VMEM...  15.3 us
    sub x6, other arithmetic, adam_update(): master - step_rate * (new_moment / bias_one / (jnp.sqrt(new_square / bias...  13.1 us
    pallas_call x1, Pallas kernels, loss_stage(): pl.pallas_call(loss_kernel, in_specs=[VMEM] * 8, out_specs=[VMEM] * 4, ou...  12.9 us

profile of v6, /device:TPU:0, one launch (start us, length us, event | category | flops | bytes accessed | tf_op | source)
XLA Modules:
  0.0 544.1 jit_solution(158755568512626146)
XLA Ops:
  0.7 0.8 fusion.9
  1.5 2.3 reduce-window.6
  3.8 0.3 slice_reduce_fusion
  4.1 0.2 reduce-window.9
  4.3 0.1 add_bitcast_fusion
  4.4 0.2 fusion.32
  4.6 0.5 fusion.47
  5.1 0.9 pad_slice_fusion.3
  6.0 0.6 multiply_reduce_fusion
  6.7 2.7 concatenate.32
  9.3 0.6 broadcast_in_dim.138.tally
  9.9 0.7 convert_element_type.86
  10.7 0.1 rev.30
  10.9 0.1 rev.31
  11.2 0.9 convert.10
  12.1 0.7 convert_bitcast_fusion.2
  12.9 0.7 convert_element_type.87
  13.6 0.1 copy.88
  13.7 0.7 concatenate.30.small_own
  14.4 0.6 reshape.193.x_ref
  15.0 1.0 fusion.11
  16.0 0.5 convert_element_type.89
  16.4 0.4 reshape.192
  16.9 0.2 copy-done.2
  17.1 1.0 pad_maximum_fusion.big_own
  18.1 159.7 %forward_near.1 = (bf16[9,384,2304]{2,1,0:T(8,128)(2,1)}, bf16[896,384]{1,0:T(8,128)(2,1)}, f32[8,384]{1,0:T(8,128)}, bf16[384,128]{1,0:T(8,128)(2,1)}, bf16[204...) custom-call(bf16[24,896]{1,0:T(8,128)(2,1)} %concatenate.30.small_ow, ...), custom_call_target="tpu_custom_call" | custom-call | tf_op jit(solution)/shard_map/forward_near/pallas_call | solution.py:440
  177.8 1.0 slice_reduce_fusion.1
  178.8 0.6 fusion.46
  182.1 0.6 fusion.35.weight
  182.7 0.1 select_reduce_fusion.3
  183.0 0.2 select_convert_fusion.1
  183.1 3.7 fusion
  186.9 0.6 pad_multiply_fusion.source
  187.7 0.5 add_select_fusion.5.order
  188.2 0.6 copy.99
  188.9 0.1 select_reduce_fusion.1
  188.9 0.5 broadcast_multiply_fusion.1.after
  189.5 37.8 %expert_forward.1 = (bf16[10,1024,384]{2,1,0:T(8,128)(2,1)}, f32[10,1024,384]{2,1,0:T(8,128)}, f32[2048,384]{1,0:T(8,128)}) custom-call(s32[8]{0:T(128)} %get-tuple-element.234.used, s32[40]{0:T(128)} %add_select_fusion.5.order, s32[41]{0:T(128)} %broadcast_multiply_fusion.1.after, s32[8448]{0:T(1024)} %pad_multiply_fusion.source, s32[4096]{0:T(1024)} %bitcast.92, ...), custom_call_target="tpu_custom_call" | custom-call | tf_op jit(solution)/shard_map/expert_forward/pallas_call | solution.py:597
  227.2 1.5 slice.144.table_t
  229.2 0.6 pad_maximum_fusion.1
  229.9 12.9 %loss_stage.1 = (f32[2048,384]{1,0:T(8,128)}, f32[128,384]{1,0:T(8,128)}, f32[1,384]{1,0:T(1,128)}, f32[1,128]{1,0:T(1,128)}) custom-call(f32[2048,384]{1,0:T(8,128)} %get-tuple-element.55.part, f32[2048,384]{1,0:T(8,128)} %get-tuple-element.56.x1, f32[8,384]{1,0:T(8,128)} %get-tuple-element.57.vec, bf16[384,128]{1,0:T(8,128)(2,1)} %get-tuple-element.58.table, ...), custom_call_target="tpu_custom_call" | custom-call | tf_op jit(solution)/shard_map/loss_stage/pallas_call | solution.py:778
  242.7 61.8 %expert_backward.1 = (bf16[10,1024,384]{2,1,0:T(8,128)(2,1)}, bf16[10,1024,1536]{2,1,0:T(8,128)(2,1)}, bf16[10,1024,768]{2,1,0:T(8,128)(2,1)}, f32[2048,512]{1,0:T(8,128)}) custom-call(s32[8]{0:T(128)} %get-tuple-element.234.used, s32[40]{0:T(128)} %add_select_fusion.5.order, s32[41]{0:T(128)} %broadcast_multiply_fusion.1.after, ...), custom_call_target="tpu_custom_call" | custom-call | tf_op jit(solution)/shard_map/expert_backward/pallas_call | solution.py:679
  304.5 1.6 slice.155.wo
  306.1 0.6 pad_bitcast_fusion.balance
  306.7 15.3 %mid_backward.1 = (f32[2048,384]{1,0:T(8,128)}, bf16[2,192,1024]{2,1,0:T(8,128)(2,1)}, f32[320,384]{1,0:T(8,128)}) custom-call(f32[2048,512]{1,0:T(8,128)} %get-tuple-element.67.part, f32[2048,384]{1,0:T(8,128)} %get-tuple-element.61.dx_ref.dx2, f32[2048,384]{1,0:T(8,128)} %get-tuple-element.56.x1, bf16[2048,384]{1,0:T(8,128)(2,1)} %get-tuple-element.51.b_ref.b, ...), custom_call_target="tpu_custom_call" | custom-call | tf_op jit(solution)/shard_map/mid_backward/pallas_call | solution.py:833
  322.0 0.6 pad.29.losses
  322.7 196.4 %backward_near.1 = (f32[9,24,2,768]{3,2,1,0:T(2,128)}, f32[9,24,768]{2,1,0:T(8,128)}, f32[24,896]{1,0:T(8,128)}, f32[8,128]{1,0:T(8,128)}) custom-call(bf16[10,1024,384]{2,1,0:T(8,128)(2,1)} %get-tuple-element.54.x_ref.xs, bf16[10,1024,384]{2,1,0:T(8,128)(2,1)} %get-tuple-element.63.dys, bf16[10,1024,1536]{2,1,0:T(8,128)(2,1)} %get-tuple-element.64.dgs, ...), custom_call_target="tpu_custom_call" | custom-call | tf_op jit(solution)/shard_map/backward_near/pallas_call | solution.py:1295
  519.1 1.4 slice_reduce_fusion.3
  521.9 0.8 copy.89
  522.7 0.8 copy.91
  523.5 0.8 multiply_subtract_fusion.4
  524.3 0.7 copy.94
  525.0 0.7 copy.95
  525.7 0.7 copy.96
  526.3 0.8 slice.164
  527.2 0.8 slice.165
  528.0 0.7 slice.166
  528.8 0.8 slice.162
  529.6 0.8 slice.163
  530.5 0.6 multiply_subtract_fusion.5
  531.1 3.4 multiply_subtract_fusion.1
  534.6 6.8 %multiply_subtract_fusion = (f32[9,24,2,768]{3,2,1,0:T(2,128)}, f32[9,24,2,768]{3,2,1,0:T(2,128)}, f32[9,24,2,768]{3,2,1,0:T(2,128)}) fusion(f32[9,24,2,768]{3,2,1,0:T(2,128)S(1)} %copy-done.1, f32[]{:T(128)} %bitcast.25, f32[]{:T(128)} %bitcast.24, f32[9,24,2,768]{3,2,1,0:T(2,128)} %get-tuple-element.80, f32[]{:T(128)S(6)} %div.213, ...), kind=kLoop, calls=%fused_computation.5 | loop fusion | flops 5308416 | bytes 9289740 | tf_op jit(solution)/shard_map/sub | solution.py:1400
  541.4 0.7 multiply_subtract_fusion.3
  542.2 0.7 multiply_subtract_fusion.2
  (85 shorter events, 1.9 us)
Async XLA Ops:
  0.7 15.3 %copy-start = (f32[9,24,2,768]{3,2,1,0:T(2,128)S(1)}, f32[9,24,2,768]{3,2,1,0:T(2,128)}, u32[]{:S(2)}) copy-start(f32[9,24,2,768]{3,2,1,0:T(2,128)} %param.32) | copy-start | bytes 3981316
  16.0 1.1 copy-start.2
  183.1 5.1 copy-start.10
  183.1 5.7 %copy-start.20 = (s32[41]{0:T(128)S(1)}, s32[41]{0:T(128)}, u32[]{:S(2)}) copy-start(s32[41]{0:T(128)} %constant.196.clone.1) | copy-start | bytes 496
  189.5 39.5 %copy-start.12 = (s32[2,1024]{1,0:T(2,128)S(1)}, s32[2,1024]{1,0:T(2,128)}, u32[]{:S(2)}) copy-start(s32[2,1024]{1,0:T(2,128)} %param.23) | copy-start | bytes 24580
  306.7 15.3 %copy-start.18 = (f32[1,128]{1,0:T(1,128)S(1)}, f32[1,128]{1,0:T(1,128)}, u32[]{:S(2)}) copy-start(f32[1,128]{1,0:T(1,128)} %get-tuple-element.77) | copy-start | bytes 1540
  306.7 15.3 %copy-start.19 = (f32[1,128]{1,0:T(1,128)S(1)}, f32[1,128]{1,0:T(1,128)}, u32[]{:S(2)}) copy-start(f32[1,128]{1,0:T(1,128)} %get-tuple-element.76) | copy-start | bytes 1540
  322.6 200.8 %copy-start.15 = (f32[5,24]{1,0:T(8,128)S(1)}, f32[5,24]{1,0:T(8,128)}, u32[]{:S(2)}) copy-start(f32[5,24]{1,0:T(8,128)} %param.41) | copy-start | bytes 1444
  322.6 207.8 %copy-start.11 = (f32[24,114]{1,0:T(8,128)S(1)}, f32[24,114]{1,0:T(8,128)}, u32[]{:S(2)}) copy-start(f32[24,114]{1,0:T(8,128)} %param.38) | copy-start | bytes 32836
  322.6 207.8 %copy-start.16 = (f32[24,114]{1,0:T(8,128)S(1)}, f32[24,114]{1,0:T(8,128)}, u32[]{:S(2)}) copy-start(f32[24,114]{1,0:T(8,128)} %param.40) | copy-start | bytes 32836
  322.6 207.8 %copy-start.17 = (f32[24,114]{1,0:T(8,128)S(1)}, f32[24,114]{1,0:T(8,128)}, u32[]{:S(2)}) copy-start(f32[24,114]{1,0:T(8,128)} %param.39) | copy-start | bytes 32836
  531.1 3.4 copy-start.1
  531.1 3.4 copy-start.3
  531.1 3.4 copy-start.4
  534.6 6.9 %copy-start.5 = (f32[24,896]{1,0:T(8,128)S(1)}, f32[24,896]{1,0:T(8,128)}, u32[]{:S(2)}) copy-start(f32[24,896]{1,0:T(8,128)} %get-tuple-element.79) | copy-start | bytes 258052
  534.6 6.9 %copy-start.7 = (f32[192,24]{0,1:T(8,128)S(1)}, f32[192,24]{0,1:T(8,128)}, u32[]{:S(2)}) copy-start(f32[192,24]{0,1:T(8,128)} %param.29) | copy-start | bytes 55300
  534.6 6.8 %copy-start.13 = (f32[192,24]{0,1:T(8,128)S(1)}, f32[192,24]{0,1:T(8,128)}, u32[]{:S(2)}) copy-start(f32[192,24]{0,1:T(8,128)} %param.31) | copy-start | bytes 55300
  534.6 6.8 %copy-start.14 = (f32[192,24]{0,1:T(8,128)S(1)}, f32[192,24]{0,1:T(8,128)}, u32[]{:S(2)}) copy-start(f32[192,24]{0,1:T(8,128)} %param.30) | copy-start | bytes 55300
  534.6 7.6 %copy-start.6 = (f32[3,24,192]{2,1,0:T(8,128)S(1)}, f32[3,24,192]{2,1,0:T(8,128)}, u32[]{:S(2)}) copy-start(f32[3,24,192]{2,1,0:T(8,128)} %param.26) | copy-start | bytes 165892
  534.6 7.6 %copy-start.8 = (f32[3,24,192]{2,1,0:T(8,128)S(1)}, f32[3,24,192]{2,1,0:T(8,128)}, u32[]{:S(2)}) copy-start(f32[3,24,192]{2,1,0:T(8,128)} %param.28) | copy-start | bytes 165892
  534.6 7.6 %copy-start.9 = (f32[3,24,192]{2,1,0:T(8,128)S(1)}, f32[3,24,192]{2,1,0:T(8,128)}, u32[]{:S(2)}) copy-start(f32[3,24,192]{2,1,0:T(8,128)} %param.27) | copy-start | bytes 165892

commit v7 on v6

--- a/solution.py
+++ b/solution.py
@@ -210,7 +210,7 @@
 
 def forward_kernel(
     small_own, big_own, tally, x_ref, cos_ref, sin_ref,
-    big, wt, vec, table, a, qkv, lse, o, x1, b, pc, total, tallies,
+    big, wt, wo, table_t, vec, table, a, qkv, lse, o, x1, b, pc, total, tallies,
     stage, small, x0, part, other,
     in_sem, own_sem, send_xy, send_up, send_dn, z_sem, p2_sem, p3_sem,
     small_send, small_z, small_y, small_x, tally_send, tally_recv, pair_send, pair_recv,
@@ -266,12 +266,15 @@
     def drop(c, zs, src):
         put(src, c, home(zs), send_dn, z_sem.at[c, zs], dp - 4)
 
-    def ends(c):
-        k = lax.rem(c, 2)
+    def turn_of(c, zs):
+        return jnp.where(c == count - 1, jnp.where(zs == 0, 0, 1), lax.rem(c, 2))
+
+    def ends(c, zs):
+        k = turn_of(c, zs)
         return jnp.where(k == 0, yp, xp), jnp.where(k == 0, xp, yp)
 
     def spread(c, zs, src):
-        first, second = ends(c)
+        first, second = ends(c, zs)
         put(src, c, home(zs), send_xy, p2_sem.at[c, zs], first)
         put(src, c, home(zs), send_xy, p3_sem, second)
 
@@ -287,6 +290,13 @@
         return carry
 
     lax.fori_loop(0, count, own_z, 0)
+
+    def own_xy(c, carry):
+        spread(c, z, stage.at[c])
+        return carry
+
+    early = 4
+    lax.fori_loop(0, early, own_xy, 0)
 
     for dist in (1, 2, 3):
         for sign in (-1, 1):
@@ -304,26 +314,24 @@
         small_put(small.at[slot], slot, small_x, xp)
     done(small.at[pl.ds(0, 8)], small_x)
 
-    def own_xy(c, carry):
-        spread(c, z, stage.at[c])
-        return carry
-
-    lax.fori_loop(0, count, own_xy, 0)
+    lax.fori_loop(early, count, own_xy, 0)
 
     whole = small[...].astype(F32).reshape(D, -1)
     table[...] = whole[:, 4 * width:].astype(BF16)
     turned = jnp.transpose(whole)
-    wt[...] = turned.astype(BF16)
+    wt[...] = turned[:3 * width].astype(BF16)
+    wo[...] = turned[3 * width:4 * width].astype(BF16)
+    table_t[...] = turned[4 * width:].astype(BF16)
     vec[...] = jnp.concatenate(
         [turned[4 * width + VECTOR:4 * width + VECTOR + 5], jnp.zeros((3, D), F32)], axis=0)
     total[...] = jnp.zeros_like(total)
 
     def relay(c, dist):
         def second(zs):
-            k = lax.rem(c, 2)
+            k = turn_of(c, zs)
             slot = zs * 4 + jnp.where(k == 0, 2 * (1 - y) + x, 2 * y + 1 - x)
             done(rows(c, slot), p2_sem.at[c, zs])
-            put(rows(c, slot), c, slot, send_xy, p3_sem, ends(c)[1])
+            put(rows(c, slot), c, slot, send_xy, p3_sem, ends(c, zs)[1])
 
         @pl.when(z >= dist)
         def _():
@@ -382,7 +390,7 @@
 
         @pl.when(j == pieces - 1)
         def _():
-            part[r, :] = dot(o[n], wt[3 * width:4 * width, :], 0, 0)
+            part[r, :] = dot(o[n], wo[...], 0, 0)
             pair(n).start()
 
     def middle(m):
@@ -440,10 +448,11 @@
     return pl.pallas_call(
         forward_kernel,
         in_specs=[VMEM, ANY, VMEM, VMEM, VMEM, VMEM],
-        out_specs=[ANY] + [VMEM] * 12,
+        out_specs=[ANY] + [VMEM] * 14,
         out_shape=[
             shape((count, D, columns), BF16),
-            shape((small_own.shape[1], D), BF16), shape((8, D), F32), shape((D, LANES), BF16),
+            shape((3 * width, D), BF16), shape((width, D), BF16), shape((LANES, D), BF16),
+            shape((8, D), F32), shape((D, LANES), BF16),
             shape((tokens, D), BF16), shape((series, 3 * width, length), BF16), shape((series, 8, length), F32),
             shape((series, width, length), BF16),
             shape((tokens, D), F32), shape((tokens, D), BF16), shape((tokens, LANES), F32), shape((1, LANES), F32),
@@ -949,7 +958,7 @@
                 copy.start()
 
     def begin(c):
-        k, slot = lax.rem(c, 2), lax.rem(c, SLOTS)
+        slot = lax.rem(c, SLOTS)
         weights(c, False)
 
         @pl.when(c == count - 1)
@@ -962,6 +971,7 @@
 
         def pack(i, carry):
             m, n = i // 2, lax.rem(i, 2)
+            k = m // 2
             gone = m * 4 + jnp.where(k == 0, n * 2 + 1 - x, (1 - y) * 2 + n)
             kept = m * 4 + jnp.where(k == 0, n * 2 + x, y * 2 + n)
             encode(send1.at[slot, i], temp[block(gone, SHARD), :])
@@ -969,11 +979,12 @@
             return carry
 
         lax.fori_loop(0, 8, pack, 0)
-        remote(send1.at[slot], recv1.at[c], sem_s1.at[slot], sem_r1.at[c], jnp.where(k == 0, xp, yp), mp).start()
+        for k, peer in enumerate((xp, yp)):
+            part = pl.ds(4 * k, 4)
+            remote(send1.at[slot, part], recv1.at[c, part], sem_s1.at[slot], sem_r1.at[c], peer, mp).start()
 
     def fold(c):
-        k, slot, hop = lax.rem(c, 2), lax.rem(c, SLOTS), lax.rem(c, HOPS)
-        o = jnp.where(k == 0, y, x)
+        slot, hop = lax.rem(c, SLOTS), lax.rem(c, HOPS)
         done(recv1.at[c], sem_r1.at[c])
 
         @pl.when(c >= HOPS)
@@ -981,13 +992,16 @@
             done(send2.at[hop], sem_s2.at[hop])
 
         def add(m, carry):
+            o = jnp.where(m // 2 == 0, y, x)
             gone, kept = m * 2 + 1 - o, m * 2 + o
             encode(send2.at[hop, m], dw[slot, gone] + decode(recv1.at[c, gone]))
             acc[lax.rem(c, ACCS), m] = dw[slot, kept] + decode(recv1.at[c, kept])
             return carry
 
         lax.fori_loop(0, 4, add, 0)
-        remote(send2.at[hop], recv2.at[c], sem_s2.at[hop], sem_r2.at[c], jnp.where(k == 0, yp, xp), mp).start()
+        for k, peer in enumerate((yp, xp)):
+            part = pl.ds(2 * k, 2)
+            remote(send2.at[hop, part], recv2.at[c, part], sem_s2.at[hop], sem_r2.at[c], peer, mp).start()
 
     def climb(c, t, relay):
         slot = lax.rem(c, HOPS)
@@ -1431,16 +1445,15 @@
     marks = observed.astype(F32)
     expert_here, plan = dispatch(routes.reshape(tokens, 2), capacity)
     point = jnp.arange(length, dtype=F32)
-    head_here = jnp.stack(
-        [jnp.sum(jnp.sum(marks, axis=0) * jnp.minimum(point, float(horizon))) for horizon in horizons])
+    reach = jnp.minimum(point[None], jnp.array(horizons, F32)[:, None])
+    head_here = jnp.sum(jnp.sum(marks, axis=0)[None] * reach, axis=1)
     tally = jnp.pad(jnp.concatenate([expert_here.astype(F32), head_here]), (0, LANES - 12))
     tally = jnp.broadcast_to(tally[None], (8, LANES))
     cos, sin = rope_rows(length)
     x = (series * marks).reshape(series_count, 1, length)
 
-    big, wt, vec, table, a, qkv, lse, o, x1, b, pc, pr_total, tallies = forward_near(
+    big, wt, wo, table_t, vec, table, a, qkv, lse, o, x1, b, pc, pr_total, tallies = forward_near(
         small_own, big_own, tally, x, cos, sin, width, 0)
-    wo, table_t = wt[3 * width:4 * width], wt[4 * width:]
     tally = jnp.sum(tallies[:, 0], axis=0) / mp_count
     expert_count, head_count = tally[:ROUTED_EXPERTS], tally[ROUTED_EXPERTS:ROUTED_EXPERTS + 4]
     total_tokens = tokens * dp_count

time: 545 us -> 525 us (0.963)
  Pallas kernels: 484 us -> 469 us
  local copies, waits for them, and re-layouts: 20.1 us -> 14.3 us
    pallas_call x1, Pallas kernels: 196 us -> 190 us  [backward_near(): pl.pallas_call(backward_kernel, in_specs=[ANY] * 10 + [VMEM] * 6, out_spe...]
where the time goes in v7:
time: 525 us; the launch traced here: 524 us
  Pallas kernels  469 us (89%)
  other arithmetic  30.5 us (6%)
  local copies, waits for them, and re-layouts  14.3 us (3%)
  between operations  6.38 us (1%)
    pallas_call x1, Pallas kernels, backward_near(): pl.pallas_call(backward_kernel, in_specs=[ANY] * 10 + [VMEM] * 6, out_spe...  190 us
    pallas_call x1, Pallas kernels, forward_near(): pl.pallas_call(forward_kernel, in_specs=[VMEM, ANY, VMEM, VMEM, VMEM, VME...  155 us
    pallas_call x1, Pallas kernels, expert_backward(): pl.pallas_call(expert_backward_kernel, grid_spec=pltpu.PrefetchScalarGrid...  60.4 us
    pallas_call x1, Pallas kernels, expert_forward(): pl.pallas_call(expert_forward_kernel, grid_spec=pltpu.PrefetchScalarGridS...  36.4 us
    pallas_call x1, Pallas kernels, mid_backward(): pl.pallas_call(mid_backward_kernel, in_specs=[VMEM] * 12, out_specs=[VMEM...  15.3 us
    sub x6, other arithmetic, adam_update(): master - step_rate * (new_moment / bias_one / (jnp.sqrt(new_square / bias...  13.1 us
    pallas_call x1, Pallas kernels, loss_stage(): pl.pallas_call(loss_kernel, in_specs=[VMEM] * 8, out_specs=[VMEM] * 4, ou...  12.9 us

profile of v7, /device:TPU:0, one launch (start us, length us, event | category | flops | bytes accessed | tf_op | source)
XLA Modules:
  0.0 524.3 jit_solution(16511453320431467374)
XLA Ops:
  0.7 0.8 convert_element_type.86
  1.6 0.1 rev.30
  1.7 0.1 rev.31
  1.9 0.1 rev.32
  2.0 0.9 convert.10
  3.0 0.7 convert_bitcast_fusion.2
  3.7 0.7 convert_element_type.87
  4.4 0.1 copy.89
  4.5 0.7 concatenate.30.small_own
  5.2 0.7 fusion.9
  6.0 2.3 reduce-window.6
  8.3 0.3 slice_reduce_fusion
  8.6 0.2 reduce-window.9
  8.8 0.1 add_bitcast_fusion
  8.9 0.2 fusion.32
  9.1 0.5 fusion.48
  9.6 0.9 pad_slice_fusion.3
  10.5 0.8 multiply_reduce_fusion
  11.4 0.6 broadcast_in_dim.141.tally
  12.0 0.6 reshape.195.x_ref
  12.6 1.0 fusion.11
  13.6 0.5 convert_element_type.89
  14.1 0.4 reshape.194
  14.5 0.2 copy-done.2
  14.8 1.0 pad_maximum_fusion.big_own
  15.8 154.6 %forward_near.1 = (bf16[9,384,2304]{2,1,0:T(8,128)(2,1)}, bf16[576,384]{1,0:T(8,128)(2,1)}, bf16[192,384]{1,0:T(8,128)(2,1)}, bf16[128,384]{1,0:T(8,128)(2,1)}, ...) custom-call(bf16[24,896]{1,0:T(8,128)(2,1)} %concatenate.30.small_ow, ...), custom_call_target="tpu_custom_call" | custom-call | tf_op jit(solution)/shard_map/forward_near/pallas_call | solution.py:448
  170.4 1.0 slice_reduce_fusion.1
  171.4 0.6 fusion.47
  174.7 0.6 fusion.36.weight
  175.3 0.1 select_reduce_fusion.3
  175.5 0.2 select_convert_fusion.1
  175.7 3.7 fusion
  179.5 0.6 pad_multiply_fusion.source
  180.2 0.1 select_reduce_fusion.4
  180.3 0.5 add_select_fusion.5.order
  180.8 0.6 copy.100
  181.5 0.1 select_reduce_fusion.1
  181.5 0.5 broadcast_multiply_fusion.1.after
  182.1 36.4 %expert_forward.1 = (bf16[10,1024,384]{2,1,0:T(8,128)(2,1)}, f32[10,1024,384]{2,1,0:T(8,128)}, f32[2048,384]{1,0:T(8,128)}) custom-call(s32[8]{0:T(128)} %get-tuple-element.234.used, s32[40]{0:T(128)} %add_select_fusion.5.order, s32[41]{0:T(128)} %broadcast_multiply_fusion.1.after, s32[8448]{0:T(1024)} %pad_multiply_fusion.source, s32[4096]{0:T(1024)} %bitcast.88, ...), custom_call_target="tpu_custom_call" | custom-call | tf_op jit(solution)/shard_map/expert_forward/pallas_call | solution.py:606
  218.9 0.6 pad_maximum_fusion.1
  219.6 12.9 %loss_stage.1 = (f32[2048,384]{1,0:T(8,128)}, f32[128,384]{1,0:T(8,128)}, f32[1,384]{1,0:T(1,128)}, f32[1,128]{1,0:T(1,128)}) custom-call(f32[2048,384]{1,0:T(8,128)} %get-tuple-element.57.part, f32[2048,384]{1,0:T(8,128)} %get-tuple-element.58.x1, f32[8,384]{1,0:T(8,128)} %get-tuple-element.59.vec, bf16[384,128]{1,0:T(8,128)(2,1)} %get-tuple-element.60.table, ...), custom_call_target="tpu_custom_call" | custom-call | tf_op jit(solution)/shard_map/loss_stage/pallas_call | solution.py:787
  232.4 60.4 %expert_backward.1 = (bf16[10,1024,384]{2,1,0:T(8,128)(2,1)}, bf16[10,1024,1536]{2,1,0:T(8,128)(2,1)}, bf16[10,1024,768]{2,1,0:T(8,128)(2,1)}, f32[2048,512]{1,0:T(8,128)}) custom-call(s32[8]{0:T(128)} %get-tuple-element.234.used, s32[40]{0:T(128)} %add_select_fusion.5.order, s32[41]{0:T(128)} %broadcast_multiply_fusion.1.after, ...), custom_call_target="tpu_custom_call" | custom-call | tf_op jit(solution)/shard_map/expert_backward/pallas_call | solution.py:688
  292.8 0.6 pad_bitcast_fusion.balance
  293.4 15.3 %mid_backward.1 = (f32[2048,384]{1,0:T(8,128)}, bf16[2,192,1024]{2,1,0:T(8,128)(2,1)}, f32[320,384]{1,0:T(8,128)}) custom-call(f32[2048,512]{1,0:T(8,128)} %get-tuple-element.69.part, f32[2048,384]{1,0:T(8,128)} %get-tuple-element.63.dx_ref.dx2, f32[2048,384]{1,0:T(8,128)} %get-tuple-element.58.x1, bf16[2048,384]{1,0:T(8,128)(2,1)} %get-tuple-element.53.b_ref.b, ...), custom_call_target="tpu_custom_call" | custom-call | tf_op jit(solution)/shard_map/mid_backward/pallas_call | solution.py:842
  308.8 0.6 pad.29.losses
  309.4 189.9 %backward_near.1 = (f32[9,24,2,768]{3,2,1,0:T(2,128)}, f32[9,24,768]{2,1,0:T(8,128)}, f32[24,896]{1,0:T(8,128)}, f32[8,128]{1,0:T(8,128)}) custom-call(bf16[10,1024,384]{2,1,0:T(8,128)(2,1)} %get-tuple-element.56.x_ref.xs, bf16[10,1024,384]{2,1,0:T(8,128)(2,1)} %get-tuple-element.65.dys, bf16[10,1024,1536]{2,1,0:T(8,128)(2,1)} %get-tuple-element.66.dgs, ...), custom_call_target="tpu_custom_call" | custom-call | tf_op jit(solution)/shard_map/backward_near/pallas_call | solution.py:1309
  499.3 1.4 slice_reduce_fusion.3
  502.1 0.8 copy.90
  502.9 0.8 copy.92
  503.7 0.1 copy.94
  503.7 0.8 multiply_subtract_fusion.4
  504.6 0.7 copy.95
  505.2 0.7 copy.96
  505.9 0.7 copy.97
  506.6 0.8 slice.156
  507.4 0.8 slice.157
  508.3 0.7 slice.158
  509.1 0.8 slice.154
  509.8 0.8 slice.155
  510.7 0.6 multiply_subtract_fusion.5
  511.4 3.4 multiply_subtract_fusion.1
  514.9 6.8 %multiply_subtract_fusion = (f32[9,24,2,768]{3,2,1,0:T(2,128)}, f32[9,24,2,768]{3,2,1,0:T(2,128)}, f32[9,24,2,768]{3,2,1,0:T(2,128)}) fusion(f32[9,24,2,768]{3,2,1,0:T(2,128)S(1)} %copy-done.1, f32[]{:T(128)} %bitcast.21, f32[]{:T(128)} %bitcast.20, f32[9,24,2,768]{3,2,1,0:T(2,128)} %get-tuple-element.84, f32[]{:T(128)S(6)} %div.213, ...), kind=kLoop, calls=%fused_computation.5 | loop fusion | flops 5308416 | bytes 9289740 | tf_op jit(solution)/shard_map/sub | solution.py:1414
  521.7 0.7 multiply_subtract_fusion.3
  522.5 0.7 multiply_subtract_fusion.2
  (82 shorter events, 1.7 us)
Async XLA Ops:
  0.7 13.0 %copy-start = (f32[9,24,2,768]{3,2,1,0:T(2,128)S(1)}, f32[9,24,2,768]{3,2,1,0:T(2,128)}, u32[]{:S(2)}) copy-start(f32[9,24,2,768]{3,2,1,0:T(2,128)} %param.33) | copy-start | bytes 3981316
  13.6 1.1 copy-start.2
  175.7 5.1 copy-start.10
  175.7 5.7 %copy-start.20 = (s32[41]{0:T(128)S(1)}, s32[41]{0:T(128)}, u32[]{:S(2)}) copy-start(s32[41]{0:T(128)} %constant.194.clone.1) | copy-start | bytes 496
  182.1 36.6 %copy-start.12 = (s32[2,1024]{1,0:T(2,128)S(1)}, s32[2,1024]{1,0:T(2,128)}, u32[]{:S(2)}) copy-start(s32[2,1024]{1,0:T(2,128)} %param.24) | copy-start | bytes 24580
  293.4 15.3 %copy-start.18 = (f32[1,128]{1,0:T(1,128)S(1)}, f32[1,128]{1,0:T(1,128)}, u32[]{:S(2)}) copy-start(f32[1,128]{1,0:T(1,128)} %get-tuple-element.81) | copy-start | bytes 1540
  293.4 15.3 %copy-start.19 = (f32[1,128]{1,0:T(1,128)S(1)}, f32[1,128]{1,0:T(1,128)}, u32[]{:S(2)}) copy-start(f32[1,128]{1,0:T(1,128)} %get-tuple-element.80) | copy-start | bytes 1540
  309.4 194.3 %copy-start.15 = (f32[5,24]{1,0:T(8,128)S(1)}, f32[5,24]{1,0:T(8,128)}, u32[]{:S(2)}) copy-start(f32[5,24]{1,0:T(8,128)} %param.42) | copy-start | bytes 1444
  309.4 201.3 %copy-start.11 = (f32[24,114]{1,0:T(8,128)S(1)}, f32[24,114]{1,0:T(8,128)}, u32[]{:S(2)}) copy-start(f32[24,114]{1,0:T(8,128)} %param.39) | copy-start | bytes 32836
  309.4 201.3 %copy-start.16 = (f32[24,114]{1,0:T(8,128)S(1)}, f32[24,114]{1,0:T(8,128)}, u32[]{:S(2)}) copy-start(f32[24,114]{1,0:T(8,128)} %param.41) | copy-start | bytes 32836
  309.4 201.3 %copy-start.17 = (f32[24,114]{1,0:T(8,128)S(1)}, f32[24,114]{1,0:T(8,128)}, u32[]{:S(2)}) copy-start(f32[24,114]{1,0:T(8,128)} %param.40) | copy-start | bytes 32836
  511.4 3.4 copy-start.1
  511.4 3.4 copy-start.3
  511.4 3.4 copy-start.4
  514.8 6.9 %copy-start.5 = (f32[24,896]{1,0:T(8,128)S(1)}, f32[24,896]{1,0:T(8,128)}, u32[]{:S(2)}) copy-start(f32[24,896]{1,0:T(8,128)} %get-tuple-element.83) | copy-start | bytes 258052
  514.8 6.9 %copy-start.7 = (f32[192,24]{0,1:T(8,128)S(1)}, f32[192,24]{0,1:T(8,128)}, u32[]{:S(2)}) copy-start(f32[192,24]{0,1:T(8,128)} %param.30) | copy-start | bytes 55300
  514.8 6.8 %copy-start.13 = (f32[192,24]{0,1:T(8,128)S(1)}, f32[192,24]{0,1:T(8,128)}, u32[]{:S(2)}) copy-start(f32[192,24]{0,1:T(8,128)} %param.32) | copy-start | bytes 55300
  514.8 6.8 %copy-start.14 = (f32[192,24]{0,1:T(8,128)S(1)}, f32[192,24]{0,1:T(8,128)}, u32[]{:S(2)}) copy-start(f32[192,24]{0,1:T(8,128)} %param.31) | copy-start | bytes 55300
  514.8 7.6 %copy-start.6 = (f32[3,24,192]{2,1,0:T(8,128)S(1)}, f32[3,24,192]{2,1,0:T(8,128)}, u32[]{:S(2)}) copy-start(f32[3,24,192]{2,1,0:T(8,128)} %param.27) | copy-start | bytes 165892
  514.9 7.6 %copy-start.8 = (f32[3,24,192]{2,1,0:T(8,128)S(1)}, f32[3,24,192]{2,1,0:T(8,128)}, u32[]{:S(2)}) copy-start(f32[3,24,192]{2,1,0:T(8,128)} %param.29) | copy-start | bytes 165892
  514.9 7.6 %copy-start.9 = (f32[3,24,192]{2,1,0:T(8,128)S(1)}, f32[3,24,192]{2,1,0:T(8,128)}, u32[]{:S(2)}) copy-start(f32[3,24,192]{2,1,0:T(8,128)} %param.28) | copy-start | bytes 165892
